TPU v7x, 256 devices: a whole 4x4x8 slice. The times are simulated.
256 devices in a mesh: seq: 16 (over y, x), exp: 16 (over z, core), dp: 1.
Axes of the slice: x: 4, y: 4, z: 8, core: 2. Of those that a mesh axis runs over, the one named last changes fastest.
Arguments:
- tokens: bfloat16 [16, 64, 64, 1280], P(('dp', 'exp'), 'seq'), may hold values from -6 to 6
- expert_ids: int32 [16, 64, 64, 1], P(('dp', 'exp'), 'seq'), may hold values from 0 to 31; in each aligned block of 256 rows (0 to 255, 256 to 511, ..., all dimensions but the last counted through in order) at most 10 rows name the same one
- gate_values: float32 [16, 64, 64], P(('dp', 'exp'), 'seq'), may hold values from 0.25 to 1
- mixer_gain: float32 [1280], replicated, may hold values from 0.1 to 1.9
- expert_gain: float32 [1280], replicated, may hold values from 0.1 to 1.9
- conv_weight: float32 [3, 3, 1280], replicated, may hold values from -2 to 2
- conv_bias: float32 [1280], replicated, may hold values from -3 to 3
- w_in: bfloat16 [32, 1280, 5120], P('exp', None, 'seq'), may hold values from -0.15625 to 0.15625
- b_in: float32 [32, 5120], P('exp', 'seq'), may hold values from -3 to 3
- w_out: bfloat16 [32, 5120, 1280], P('exp', 'seq'), may hold values from -0.078125 to 0.078125
- b_out: float32 [32, 1280], P('exp'), may hold values from -3 to 3
Outputs:
- result: bfloat16 [16, 64, 64, 1280], P(('dp', 'exp'), 'seq')
Inputs may be any that keep to these rules, and one draw needn't show every extreme that they name: `expert_ids`: among the 256 patches of one image's block of 4 rows (rows k * 4 to k * 4 + 3), no expert is chosen more than 10 times, and in every draw some expert is chosen exactly 10 times in some block.
All inputs are finite; a program needn't handle non-finite values.
Results may differ from a plain program's by a relative error of at most 0.006.
Values may be sent and summed in bfloat16 or wider, within the bound.
No kernel may reach another device: no remote copies, remote signals or barrier semaphores. Data moves between devices by JAX's collectives and lax.ppermute only.
A program may use at most 128 MiB of HBM per device.

v0:
```python
import jax
import jax.numpy as jnp
from jax import lax
from jax.sharding import PartitionSpec as P


def with_halo(cells, sides, width):
    for axis, dim in sides:
        count = lax.axis_size(axis)
        ends = count - 1
        head = lax.slice_in_dim(cells, 0, width, axis=dim)
        tail = lax.slice_in_dim(cells, cells.shape[dim] - width, cells.shape[dim], axis=dim)
        cells = jnp.concatenate(
            [
                lax.ppermute(tail, axis, [(i, (i + 1) % count) for i in range(ends)]),
                cells,
                lax.ppermute(head, axis, [((i + 1) % count, i) for i in range(ends)]),
            ],
            axis=dim,
        )
    return cells


def normalize(values, scales):
    row_mean = jnp.mean(values, axis=-1, keepdims=True)
    centred = values - row_mean
    row_var = jnp.mean(centred * centred, axis=-1, keepdims=True)
    return centred * lax.rsqrt(row_var + 1e-06) * scales


def depthwise(padded, conv_weight, height, width):
    summed = padded[..., 0:height, 0:width, :] * conv_weight[0, 0]
    for row_off in range(3):
        for col_off in range(3):
            if row_off + col_off > 0:
                summed = (
                    summed
                    + padded[..., row_off : row_off + height, col_off : col_off + width, :]
                    * conv_weight[row_off, col_off]
                )
    return summed


def body(
    tokens,
    expert_ids,
    gate_values,
    mixer_gain,
    expert_gain,
    conv_weight,
    conv_bias,
    w_in,
    b_in,
    w_out,
    b_out,
):
    row_count = tokens.shape[1]
    col_count = tokens.shape[2]
    width_d = tokens.shape[3]
    values = tokens[0].astype(jnp.float32)
    normed = normalize(values, mixer_gain).astype(jnp.bfloat16)
    rim_source = tokens[0]
    extended = with_halo(rim_source, (("seq", 0),), 1)
    rim_rows = jnp.concatenate([extended[0:1], extended[row_count + 1 : row_count + 2]], axis=0)
    rim_rows = normalize(rim_rows.astype(jnp.float32), mixer_gain).astype(jnp.bfloat16)
    extended = jnp.concatenate([rim_rows[0:1], normed, rim_rows[1:2]], axis=0)
    padded = jnp.pad(extended.astype(jnp.float32), ((0, 0), (1, 1), (0, 0)))
    mixed = values + depthwise(padded, conv_weight, row_count, col_count) + conv_bias
    tok_rows = row_count * col_count
    expert_in = normalize(mixed, expert_gain).astype(jnp.bfloat16).reshape(tok_rows, width_d)
    per_device = w_in.shape[0]
    holders = lax.axis_size("exp")
    experts = per_device * holders
    slot_count = 5 * tok_rows // (4 * experts)
    route_ids = expert_ids.reshape(tok_rows)
    one_hot = (route_ids[:, None] == jnp.arange(experts, dtype=jnp.int32)[None, :]).astype(
        jnp.float32
    )
    positions = jnp.arange(tok_rows, dtype=jnp.int32)
    below_mask = (positions[:, None] > positions[None, :]).astype(jnp.float32)
    earlier = jnp.dot(below_mask, one_hot, precision=lax.Precision.HIGHEST)
    slot_rank = jnp.sum(earlier * one_hot, axis=1).astype(jnp.int32)
    column = (
        route_ids // per_device * slot_count + slot_rank
    ) * per_device + route_ids % per_device
    dispatch_mask = (
        column[:, None] == jnp.arange(experts * slot_count, dtype=jnp.int32)[None, :]
    ).astype(jnp.bfloat16)
    dispatched = jnp.einsum(
        "tk,td->kd", dispatch_mask, expert_in, preferred_element_type=jnp.float32
    ).astype(jnp.bfloat16)
    dispatched = dispatched.reshape(holders, slot_count, per_device, width_d)
    received = lax.all_to_all(dispatched, "exp", split_axis=0, concat_axis=0, tiled=True)
    gathered = lax.all_gather(received, "seq", axis=0, tiled=True)
    hidden = (
        jnp.einsum("kcjd,jdf->kcjf", gathered, w_in, preferred_element_type=jnp.float32)
        + b_in[None, None]
    )
    hidden = jax.nn.gelu(hidden, approximate=False).astype(jnp.bfloat16)
    summed = lax.psum_scatter(
        jnp.einsum("kcjf,jfd->kcjd", hidden, w_out, preferred_element_type=jnp.float32).astype(
            jnp.bfloat16
        ),
        "seq",
        scatter_dimension=0,
        tiled=True,
    ).astype(jnp.float32)
    back = (summed + b_out[None, None]).astype(jnp.bfloat16)
    returned = lax.all_to_all(back, "exp", split_axis=0, concat_axis=0, tiled=True).reshape(
        experts * slot_count, width_d
    )
    combined = jnp.dot(dispatch_mask, returned, preferred_element_type=jnp.float32)
    result = mixed.reshape(tok_rows, width_d) + gate_values.reshape(tok_rows)[:, None] * combined
    return result.astype(jnp.bfloat16).reshape(tokens.shape)


def solution(mesh):
    in_specs = (
        P(("dp", "exp"), "seq", None, None),
        P(("dp", "exp"), "seq", None, None),
        P(("dp", "exp"), "seq", None),
        P(),
        P(),
        P(),
        P(),
        P("exp", None, "seq"),
        P("exp", "seq"),
        P("exp", "seq", None),
        P("exp", None),
    )
    out_specs = P(("dp", "exp"), "seq", None, None)
    return jax.shard_map(body, mesh=mesh, in_specs=in_specs, out_specs=out_specs, check_vma=False)
```

profile of v0, /device:TPU:1, one launch (start us, length us, event | category | flops | bytes accessed | tf_op | source)
XLA Modules:
  0.0 334.6 jit_solution(12479019363799753572)
XLA Ops:
  6.5 0.0 copy-start
  6.5 0.0 copy-start.4
  6.5 0.0 all-gather.2.cloned.1.call-start
  6.5 1.1 slice_bitcast_fusion.1
  7.7 4.0 %collective-permute-start = (bf16[1,64,1280]{2,1,0:T(8,128)(2,1)S(1)}, bf16[1,64,1280]{2,1,0:T(8,128)(2,1)S(1)}, u32[]{:S(2)}, u32[]{:S(2)}) collective-permute-start(bf16[1,64,1280]{2,1,0:T(8,128)(2,1)S(1)} %get-tuple-element.16), channel_id=1, source_target_pairs={{0,16},{16,32},{32,48},{48,64},{64,80},{80,96},{96,112},{112,128},... | collective-permute-start | bytes 491528 | tf_op jit(solution)/shard_map/ppermute | solution.py:15
  11.7 1.3 collective-permute-start.1
  13.0 1.3 convert_reduce_fusion
  14.2 1.4 fusion.61
  15.6 0.5 broadcast.173
  16.2 1.3 reduce.22
  17.5 0.1 reshape.120
  17.6 0.0 copy-start.1
  17.6 0.2 fusion.79
  17.8 1.4 fusion.63
  19.2 1.0 slice_reduce_fusion.8
  20.2 0.0 collective-permute-done
  20.2 0.0 collective-permute-done.1
  20.2 0.1 convert_reduce_fusion.1
  20.4 0.2 fusion.82
  20.6 0.9 fusion.84
  21.5 0.0 copy-start.3
  21.6 0.2 maximum_convert_fusion
  21.8 0.0 copy-done.4
  21.8 0.0 copy-done.1
  21.8 1.7 fusion.119
  23.4 0.0 copy-start.6
  23.5 0.3 multiply_reduce_fusion
  23.8 0.0 copy-done.3
  23.8 0.2 multiply_convert_fusion
  24.0 1.4 convolution_convert_fusion
  25.4 2.9 reshape.122
  28.3 33.1 %all_to_all.10 = bf16[16,10,2,1280]{3,2,1,0:T(2,128)(2,1)S(1)} all-to-all(bf16[16,10,2,1280]{3,2,1,0:T(2,128)(2,1)} %reshape.122), channel_id=1, replica_groups=mesh['seq'=16,'exp'=16,'dp'=1] {'exp'}, dimensions={0} | all-to-all | bytes 1638400 | tf_op jit(solution)/shard_map/all_to_all | solution.py:93
  61.4 1.0 copy.19
  62.4 0.0 all-gather.2.cloned.1.call-update
  62.5 0.2 reduce-scatter.2.cloned.1.call-start
  62.7 95.3 %all-gather.2.cloned.1.call-done = bf16[256,10,2,1280]{3,0,1,2:T(8,128)(2,1)} async-done(((bf16[16,10,2,1280]{3,0,1,2:T(8,128)(2,1)}), bf16[256,10,2,1280]{3,0,1,2:T(8,128)(2,1)}) %all-gather.2.cloned.1.call-update) | async-done | bytes 13107216 | tf_op jit(solution)/shard_map/all_gather | solution.py:94
  158.0 0.0 copy-done
  158.0 0.0 copy-done.6
  158.0 29.0 %convert_bitcast_fusion = bf16[256,10,2,1280]{3,0,1,2:T(8,128)(2,1)} fusion(bf16[256,10,2,1280]{3,0,1,2:T(8,128)(2,1)} %all-gather.2.cloned.1.call-done, f32[2,320]{1,0:T(2,128)S(1)} %copy-done.6, bf16[2,320,1280]{2,1,0:T(8,128)(2,1)S(1)} %copy-done, bf16[2,1280,320]{1,2,0:T(8,128)(2,1)} %param.18), kind=kOutput, calls=%fused_computation | convolution fusion | flops 8503296000 | bytes 29493760 | tf_op jit(solution)/shard_map/kcjf,jfd->kcjd/dot_general | solution.py:101
  187.0 0.0 copy-start.2
  187.0 0.0 copy-start.5
  187.0 0.0 reduce-scatter.2.cloned.1.call-update
  187.0 100.8 %reduce-scatter.2.cloned.1.call-done = bf16[16,10,2,1280]{3,0,1,2:T(8,128)(2,1)} async-done(((bf16[256,10,2,1280]{3,0,1,2:T(8,128)(2,1)}), bf16[16,10,2,1280]{3,0,1,2:T(8,128)(2,1)}) %reduce-scatter.2.cloned.1.call-update) | async-done | bytes 819216 | tf_op jit(solution)/shard_map/reduce_scatter | solution.py:100
  287.8 0.0 copy-done.2
  287.8 1.3 add_convert_fusion
  289.1 1.7 copy.20
  290.9 7.9 %all-to-all-start.1 = ((bf16[16,10,2,1280]{3,2,1,0:T(2,128)(2,1)}), bf16[16,10,2,1280]{3,2,1,0:T(2,128)(2,1)}, u32[]{:S(2)}, u32[]{:S(2)}) async-start(bf16[16,10,2,1280]{3,2,1,0:T(2,128)(2,1)} %copy.20), calls=%async_computation.2 | async-start | bytes 1638400 | tf_op jit(solution)/shard_map/all_to_all | solution.py:109
  298.8 0.0 copy-done.5
  298.8 0.1 mul.236
  298.9 23.3 %all-to-all-done.1 = bf16[16,10,2,1280]{3,2,1,0:T(2,128)(2,1)} async-done(((bf16[16,10,2,1280]{3,2,1,0:T(2,128)(2,1)}), bf16[16,10,2,1280]{3,2,1,0:T(2,128)(2,1)}, u32[]{:S(2)}, u32[]{:S(2)}) %all-to-all-start.1) | async-done | bytes 819232 | tf_op jit(solution)/shard_map/all_to_all | solution.py:109
  322.2 3.0 reshape.123
  325.2 2.5 fusion.53
  (8 shorter events, 0.1 us)
Async XLA Ops:
  6.5 151.5 %copy-start = (bf16[2,320,1280]{2,1,0:T(8,128)(2,1)S(1)}, bf16[2,320,1280]{2,1,0:T(8,128)(2,1)}, u32[]{:S(2)}) copy-start(bf16[2,320,1280]{2,1,0:T(8,128)(2,1)} %param.20) | copy-start | bytes 4915204
  6.5 15.2 %copy-start.4 = (f32[1280]{0:T(1024)S(1)}, f32[1280]{0:T(1024)}, u32[]{:S(2)}) copy-start(f32[1280]{0:T(1024)} %param.17) | copy-start | bytes 15364
  6.5 151.5 %all-gather.2.cloned.1.call-start = ((), (), s32[]{:S(2)}) async-start(), calls=%async_computation.3 | async-start | bytes 13926400 | tf_op jit(solution)/shard_map/all_gather | solution.py:94
  7.7 12.5 %collective-permute-start = (bf16[1,64,1280]{2,1,0:T(8,128)(2,1)S(1)}, bf16[1,64,1280]{2,1,0:T(8,128)(2,1)S(1)}, u32[]{:S(2)}, u32[]{:S(2)}) collective-permute-start(bf16[1,64,1280]{2,1,0:T(8,128)(2,1)S(1)} %get-tuple-element.16), channel_id=1, source_target_pairs={{0,16},{16,32},{32,48},{48,64},{64,80},{80,96},{96,112},{112,128},... | collective-permute-start | bytes 491528 | tf_op jit(solution)/shard_map/ppermute | solution.py:15
  11.7 8.6 %collective-permute-start.1 = (bf16[1,64,1280]{2,1,0:T(8,128)(2,1)S(1)}, bf16[1,64,1280]{2,1,0:T(8,128)(2,1)S(1)}, u32[]{:S(2)}, u32[]{:S(2)}) collective-permute-start(bf16[1,64,1280]{2,1,0:T(8,128)(2,1)S(1)} %get-tuple-element.17), channel_id=1, source_target_pairs={{16,0},{32,16},{48,32},{64,48},{80,64},{96,80},{112,96},{128,112},... | collective-permute-start | bytes 491528 | tf_op jit(solution)/shard_map/ppermute | solution.py:17
  17.6 4.2 %copy-start.1 = (bf16[1,4,64,1280]{3,2,1,0:T(8,128)(2,1)S(1)}, bf16[1,4,64,1280]{3,2,1,0:T(8,128)(2,1)}, u32[]{:S(2)}) copy-start(bf16[1,4,64,1280]{3,2,1,0:T(8,128)(2,1)} %param.11) | copy-start | bytes 1966084
  21.5 2.2 copy-start.3
  23.4 134.6 %copy-start.6 = (f32[2,320]{1,0:T(2,128)S(1)}, f32[2,320]{1,0:T(2,128)}, u32[]{:S(2)}) copy-start(f32[2,320]{1,0:T(2,128)} %param.19) | copy-start | bytes 7684
  62.5 225.4 %reduce-scatter.2.cloned.1.call-start = ((), (), s32[]{:S(2)}) async-start(), calls=%async_computation.4 | async-start | bytes 13926400 | tf_op jit(solution)/shard_map/reduce_scatter | solution.py:100
  187.0 100.9 %copy-start.2 = (f32[2,1280]{1,0:T(2,128)S(1)}, f32[2,1280]{1,0:T(2,128)}, u32[]{:S(2)}) copy-start(f32[2,1280]{1,0:T(2,128)} %param.21) | copy-start | bytes 30724
  187.0 111.8 %copy-start.5 = (f32[1,4,64]{2,1,0:T(4,128)S(1)}, f32[1,4,64]{2,1,0:T(4,128)}, u32[]{:S(2)}) copy-start(f32[1,4,64]{2,1,0:T(4,128)} %param.13) | copy-start | bytes 3076
  290.9 31.3 %all-to-all-start.1 = ((bf16[16,10,2,1280]{3,2,1,0:T(2,128)(2,1)}), bf16[16,10,2,1280]{3,2,1,0:T(2,128)(2,1)}, u32[]{:S(2)}, u32[]{:S(2)}) async-start(bf16[16,10,2,1280]{3,2,1,0:T(2,128)(2,1)} %copy.20), calls=%async_computation.2 | async-start | bytes 1638400 | tf_op jit(solution)/shard_map/all_to_all | solution.py:109
Sparse Core Ops, SparseCore 0:
  62.6 95.3 all-gather.1
  187.1 100.6 reduce-scatter.1
where the time goes:
time: 335 us
  waiting for transfers between devices  220 us (66%)
  matrix products  33.1 us (10%)
  blocking collectives  33.1 us (10%)
  between operations  13.6 us (4%)
  starting transfers between devices  13.4 us (4%)
  local copies, waits for them, and re-layouts  11.6 us (3%)
  other arithmetic  10.4 us (3%)
    reduce_scatter x1, waiting for transfers between devices, body(): lax.psum_scatter(jnp.einsum('kcjf,jfd->kcjd', hidden, w_out, preferred_el...  101 us
    all_gather x1, waiting for transfers between devices, body(): gathered = lax.all_gather(received, 'seq', axis=0, tiled=True)  95.3 us
    all_to_all x1, blocking collectives, body(): lax.all_to_all(dispatched, 'exp', split_axis=0, concat_axis=0, tiled=True)  33.1 us
    dot_general x1, matrix products, body(): jnp.einsum('kcjf,jfd->kcjd', hidden, w_out, preferred_element_type=jnp.fl...  29 us
    all_to_all x1, waiting for transfers between devices, body(): lax.all_to_all(back, 'exp', split_axis=0, concat_axis=0, tiled=True)  23.3 us
    all_to_all x1, starting transfers between devices, body(): lax.all_to_all(back, 'exp', split_axis=0, concat_axis=0, tiled=True)  7.91 us
  transfers between devices with their start and end apart: 5, of which 3 were waited for; matrix products, arithmetic and copies ran while one was open for 2% of the time, Pallas kernels for 0%

commit v1 on v0

--- a/solution.py
+++ b/solution.py
@@ -1,7 +1,36 @@
+import functools
 import jax
 import jax.numpy as jnp
 from jax import lax
+from jax.experimental import pallas as pl
+from jax.experimental.pallas import tpu as pltpu
 from jax.sharding import PartitionSpec as P
+
+SIDE = 4
+AXES = ("seq", "exp")
+
+
+def ring(shift, weights, exp_size):
+    pairs = []
+    for y in range(SIDE):
+        for x in range(SIDE):
+            for e in range(exp_size):
+                along_x = (e % 2 == 0) == weights
+                to_y = y if along_x else (y + shift) % SIDE
+                to_x = (x + shift) % SIDE if along_x else x
+                pairs.append(((y * SIDE + x) * exp_size + e, (to_y * SIDE + to_x) * exp_size + e))
+    return pairs
+
+
+def weight_groups(exp_size):
+    groups = []
+    for e in range(exp_size):
+        for a in range(SIDE):
+            if e % 2 == 0:
+                groups.append([(a * SIDE + b) * exp_size + e for b in range(SIDE)])
+            else:
+                groups.append([(b * SIDE + a) * exp_size + e for b in range(SIDE)])
+    return groups
 
 
 def with_halo(cells, sides, width):
@@ -41,6 +70,78 @@
     return summed
 
 
+def gelu(v):
+    return 0.5 * v * (1.0 + lax.erf(v * 0.7071067811865476))
+
+
+def ffn_kernel(*refs):
+    xs, wis, wos, bias, ys = refs[0:4], refs[4:8], refs[8:12], refs[12], refs[13:17]
+    x_v, wi_v, wo_v, y_v, in_sem, out_sem = refs[17:]
+    experts = x_v.shape[0]
+    rows = xs[0].shape[1]
+    units = wis[0].shape[1]
+    copies = []
+    for j in range(experts):
+        for what, (sources, target, size) in enumerate(
+            ((xs, x_v, rows), (wis, wi_v, units), (wos, wo_v, units))
+        ):
+            for k in range(SIDE):
+                copy = pltpu.make_async_copy(
+                    sources[k].at[j], target.at[j, pl.ds(k * size, size)], in_sem.at[j, what, k]
+                )
+                copy.start()
+                copies.append(copy)
+    out = []
+    for j in range(experts):
+        base = j * 3 * SIDE
+        for copy in copies[base : base + 2 * SIDE]:
+            copy.wait()
+        for half in range(2):
+            at = pl.ds(half * 2 * rows, 2 * rows)
+            hidden = lax.dot_general(
+                x_v[j, at], wi_v[j], (((1,), (1,)), ((), ())), preferred_element_type=jnp.float32
+            )
+            hidden = gelu(hidden + bias[j : j + 1]).astype(jnp.bfloat16)
+            if half == 0:
+                for copy in copies[base + 2 * SIDE : base + 3 * SIDE]:
+                    copy.wait()
+            part = jnp.dot(hidden, wo_v[j], preferred_element_type=jnp.float32)
+            y_v[j, at] = part.astype(jnp.bfloat16)
+            for k in (2 * half, 2 * half + 1):
+                copy = pltpu.make_async_copy(
+                    y_v.at[j, pl.ds(k * rows, rows)], ys[k].at[j], out_sem.at[j, k]
+                )
+                copy.start()
+                out.append(copy)
+    for copy in out:
+        copy.wait()
+
+
+def ffn(xs, wis, wos, bias):
+    experts, rows, width = xs[0].shape
+    units = wis[0].shape[1]
+    any_spec = pl.BlockSpec(memory_space=pl.ANY)
+    flops = 4 * SIDE * SIDE * experts * rows * units * width
+    moved = 2 * SIDE * experts * width * (2 * rows + 2 * units)
+    return pl.pallas_call(
+        ffn_kernel,
+        out_shape=[jax.ShapeDtypeStruct((experts, rows, width), jnp.bfloat16)] * SIDE,
+        in_specs=[any_spec] * 12 + [pl.BlockSpec(memory_space=pltpu.VMEM)],
+        out_specs=[any_spec] * SIDE,
+        scratch_shapes=[
+            pltpu.VMEM((experts, SIDE * rows, width), jnp.bfloat16),
+            pltpu.VMEM((experts, SIDE * units, width), jnp.bfloat16),
+            pltpu.VMEM((experts, SIDE * units, width), jnp.bfloat16),
+            pltpu.VMEM((experts, SIDE * rows, width), jnp.bfloat16),
+            pltpu.SemaphoreType.DMA((experts, 3, SIDE)),
+            pltpu.SemaphoreType.DMA((experts, SIDE)),
+        ],
+        compiler_params=pltpu.CompilerParams(vmem_limit_bytes=44 * 1024 * 1024),
+        cost_estimate=pl.CostEstimate(flops=flops, transcendentals=0, bytes_accessed=moved),
+        name="ffn",
+    )(*xs, *wis, *wos, bias)
+
+
 def body(
     tokens,
     expert_ids,
@@ -54,6 +155,31 @@
     w_out,
     b_out,
 ):
+    exp_size = lax.axis_size("exp")
+    send_w = functools.partial(ring, weights=True, exp_size=exp_size)
+    send_t = functools.partial(ring, weights=False, exp_size=exp_size)
+
+    wi = jnp.swapaxes(w_in, 1, 2)
+    wi_prev = lax.ppermute(wi, AXES, send_w(1))
+    wi_next = lax.ppermute(wi, AXES, send_w(-1))
+    wo_prev = lax.ppermute(w_out, AXES, send_w(1))
+    wo_next = lax.ppermute(w_out, AXES, send_w(-1))
+    wi_far = lax.ppermute(wi_prev, AXES, send_w(1))
+    wo_far = lax.ppermute(wo_next, AXES, send_w(-1))
+    biases = lax.all_gather(b_in, AXES, axis_index_groups=weight_groups(exp_size))
+    seq = lax.axis_index("seq")
+    place = jnp.where(lax.axis_index("exp") % 2 == 0, seq % SIDE, seq // SIDE)
+    bias = jnp.concatenate(
+        [
+            sum(
+                jnp.where((place + shift) % SIDE == k, biases[k], 0.0)
+                for k in range(SIDE)
+            )
+            for shift in (0, SIDE - 1, 1, 2)
+        ],
+        axis=1,
+    )
+
     row_count = tokens.shape[1]
     col_count = tokens.shape[2]
     width_d = tokens.shape[3]
@@ -91,21 +217,27 @@
     ).astype(jnp.bfloat16)
     dispatched = dispatched.reshape(holders, slot_count, per_device, width_d)
     received = lax.all_to_all(dispatched, "exp", split_axis=0, concat_axis=0, tiled=True)
-    gathered = lax.all_gather(received, "seq", axis=0, tiled=True)
-    hidden = (
-        jnp.einsum("kcjd,jdf->kcjf", gathered, w_in, preferred_element_type=jnp.float32)
-        + b_in[None, None]
-    )
-    hidden = jax.nn.gelu(hidden, approximate=False).astype(jnp.bfloat16)
-    summed = lax.psum_scatter(
-        jnp.einsum("kcjf,jfd->kcjd", hidden, w_out, preferred_element_type=jnp.float32).astype(
-            jnp.bfloat16
-        ),
-        "seq",
-        scatter_dimension=0,
-        tiled=True,
-    ).astype(jnp.float32)
-    back = (summed + b_out[None, None]).astype(jnp.bfloat16)
+    rows = jnp.transpose(received, (2, 1, 0, 3)).reshape(per_device, slot_count * holders, width_d)
+    x_prev = lax.ppermute(rows, AXES, send_t(1))
+    x_next = lax.ppermute(rows, AXES, send_t(-1))
+    x_far = lax.ppermute(rows, AXES, send_t(2))
+    y_own, y_prev, y_next, y_far = ffn(
+        (rows, x_prev, x_next, x_far),
+        (wi, wi_prev, wi_next, wi_far),
+        (w_out, wo_prev, wo_next, wo_far),
+        bias,
+    )
+    parts = (
+        y_own,
+        lax.ppermute(y_prev, AXES, send_t(-1)),
+        lax.ppermute(y_next, AXES, send_t(1)),
+        lax.ppermute(y_far, AXES, send_t(2)),
+    )
+    summed = sum(part.astype(jnp.float32) for part in parts)
+    back = (summed + b_out[:, None]).astype(jnp.bfloat16)
+    back = jnp.transpose(
+        back.reshape(per_device, slot_count, holders, width_d), (2, 1, 0, 3)
+    )
     returned = lax.all_to_all(back, "exp", split_axis=0, concat_axis=0, tiled=True).reshape(
         experts * slot_count, width_d
     )

time: 335 us -> 163 us (0.49)
  waiting for transfers between devices: 220 us -> 63.9 us
  starting transfers between devices: 13.4 us -> 50.2 us
  matrix products: 33.1 us -> 2.1 us
  Pallas kernels: 0 us -> 15.2 us
  blocking collectives: 33.1 us -> 18 us
  between operations: 13.6 us -> 0.3 us
  local copies, waits for them, and re-layouts: 11.6 us -> 6.37 us
  other arithmetic: 10.4 us -> 6.03 us
    reduce_scatter x1 -> x0, waiting for transfers between devices: 101 us -> none  [body(): lax.psum_scatter(jnp.einsum('kcjf,jfd->kcjd', hidden, w_out, preferred_el...]
    all_gather x1 -> x0, waiting for transfers between devices: 95.3 us -> none  [body(): gathered = lax.all_gather(received, 'seq', axis=0, tiled=True)]
    all_to_all x1 -> x0, blocking collectives: 33.1 us -> none  [body(): lax.all_to_all(dispatched, 'exp', split_axis=0, concat_axis=0, tiled=True)]
    dot_general x1 -> x0, matrix products: 29 us -> none  [body(): jnp.einsum('kcjf,jfd->kcjd', hidden, w_out, preferred_element_type=jnp.fl...]
    all_to_all x0 -> x1, waiting for transfers between devices: none -> 20.4 us  [body(): lax.all_to_all(dispatched, 'exp', split_axis=0, concat_axis=0, tiled=True)]
    ppermute x0 -> x12, waiting for transfers between devices: none -> 20.3 us  [the longest x1 16.8 us: body(): lax.ppermute(y_prev, AXES, send_t(-1))]
    ppermute x0 -> x12, starting transfers between devices: none -> 19.2 us  [the longest x1 4.42 us: body(): wo_next = lax.ppermute(w_out, AXES, send_w(-1))]
    all_to_all x0 -> x1, starting transfers between devices: none -> 19 us  [body(): lax.all_to_all(dispatched, 'exp', split_axis=0, concat_axis=0, tiled=True)]
  transfers between devices with their start and end apart: 5 -> 16, of which waited for: 3 -> 5; matrix products, arithmetic and copies ran while one was open for 2% -> 6% of each run, Pallas kernels for 0% -> 0%
where the time goes in v1:
time: 163 us; the launch traced here: 162 us
  waiting for transfers between devices  63.9 us (39%)
  starting transfers between devices  50.2 us (31%)
  blocking collectives  18 us (11%)
  Pallas kernels  15.2 us (9%)
  local copies, waits for them, and re-layouts  6.37 us (4%)
  other arithmetic  6.03 us (4%)
  matrix products  2.1 us (1%)
    all_to_all x1, waiting for transfers between devices, body(): lax.all_to_all(back, 'exp', split_axis=0, concat_axis=0, tiled=True)  23.2 us
    all_to_all x1, waiting for transfers between devices, body(): lax.all_to_all(dispatched, 'exp', split_axis=0, concat_axis=0, tiled=True)  20.4 us
    all_to_all x1, starting transfers between devices, body(): lax.all_to_all(dispatched, 'exp', split_axis=0, concat_axis=0, tiled=True)  19 us
    all_gather x1, blocking collectives, body(): lax.all_gather(b_in, AXES, axis_index_groups=weight_groups(exp_size))  18 us
    ppermute x1, waiting for transfers between devices, body(): lax.ppermute(y_prev, AXES, send_t(-1))  16.8 us
    pallas_call x1, Pallas kernels, ffn(): pl.pallas_call(ffn_kernel, out_shape=[jax.ShapeDtypeStruct((experts, rows...  15.2 us
    all_to_all x1, starting transfers between devices, body(): lax.all_to_all(back, 'exp', split_axis=0, concat_axis=0, tiled=True)  7.39 us
    ppermute x1, starting transfers between devices, body(): wo_next = lax.ppermute(w_out, AXES, send_w(-1))  4.42 us
  transfers between devices with their start and end apart: 16, of which 5 were waited for; matrix products, arithmetic and copies ran while one was open for 6% of the time, Pallas kernels for 0%

profile of v1, /device:TPU:1, one launch (start us, length us, event | category | flops | bytes accessed | tf_op | source)
XLA Modules:
  0.0 162.1 jit_solution(9411442842756099388)
XLA Ops:
  0.0 2.2 %collective-permute-start.5 = (bf16[2,320,1280]{2,1,0:T(8,128)(2,1)}, bf16[2,320,1280]{2,1,0:T(8,128)(2,1)}, u32[]{:S(2)}, u32[]{:S(2)}) collective-permute-start(bf16[2,320,1280]{2,1,0:T(8,128)(2,1)} %bitcast.57), channel_id=1, source_target_pairs={{0,16},{1,65},{2,18},{3,67},{4,20},{5,69},{6,22},{7,71},{8,24},{9,... | collective-permute-start | bytes 4915208 | tf_op jit(solution)/shard_map/ppermute | solution.py:163
  2.2 1.5 collective-permute-start.6
  3.7 1.0 slice_bitcast_fusion.1
  4.8 3.1 %collective-permute-start = (bf16[1,64,1280]{2,1,0:T(8,128)(2,1)S(1)}, bf16[1,64,1280]{2,1,0:T(8,128)(2,1)S(1)}, u32[]{:S(2)}, u32[]{:S(2)}) collective-permute-start(bf16[1,64,1280]{2,1,0:T(8,128)(2,1)S(1)} %get-tuple-element.24), channel_id=1, source_target_pairs={{0,16},{16,32},{32,48},{48,64},{64,80},{80,96},{96,112},{112,128},... | collective-permute-start | bytes 491528 | tf_op jit(solution)/shard_map/ppermute | solution.py:44
  7.9 0.0 copy-start.4
  7.9 1.4 collective-permute-start.1
  9.3 4.4 %collective-permute-start.9 = (bf16[2,320,1280]{2,1,0:T(8,128)(2,1)}, bf16[2,320,1280]{2,1,0:T(8,128)(2,1)}, u32[]{:S(2)}, u32[]{:S(2)}) collective-permute-start(bf16[2,320,1280]{2,1,0:T(8,128)(2,1)} %refs_8_.1), channel_id=1, source_target_pairs={{0,48},{1,193},{2,50},{3,195},{4,52},{5,197},{6,54},{7,199},{8,56}... | collective-permute-start | bytes 4915208 | tf_op jit(solution)/shard_map/ppermute | solution.py:166
  13.8 1.3 convert_reduce_fusion
  15.0 0.3 fusion.6
  15.4 0.5 broadcast.337
  15.9 0.7 reduce.22
  16.6 0.1 reshape.185
  16.6 0.2 fusion.24
  16.9 0.3 fusion.8
  17.2 0.1 slice_reduce_fusion.8
  17.3 0.0 collective-permute-done
  17.3 0.1 collective-permute-start.8
  17.4 0.0 collective-permute-done.1
  17.4 0.1 convert_reduce_fusion.1
  17.6 0.2 fusion.27
  17.8 0.2 fusion.29
  18.1 0.0 copy-start.8
  18.1 0.2 maximum_convert_fusion
  18.3 0.5 copy-done.8
  18.8 1.7 %fusion.34 = (f32[4,64]{1,0:T(4,128)S(1)}, f32[4,64,1280]{2,1,0:T(8,128)S(1)}) fusion(f32[1280]{0:T(1024)S(1)} %copy-done.8, f32[1280]{0:T(1024)S(1)} %get-tuple-element.20, f32[1280]{0:T(1024)S(1)} %get-tuple-element.21, f32[6,64,1280]{2,1,0:T(8,128)S(1)} %maximum_convert_fusion, f32[1280]{0:T(1024)S(1)} %get-tuple-element.14, ...), kind=kLoop, calls=%fused_computation.85 | loop fusion | flops 6881024 | bytes 7947264 | tf_op jit(solution)/shard_map/reduce_sum | solution.py:54
  20.5 0.0 copy-start.7
  20.5 0.3 multiply_reduce_fusion
  20.8 0.4 copy-done.7
  21.2 0.2 multiply_convert_fusion
  21.4 0.1 copy-done.1
  21.5 0.5 convolution_convert_fusion
  22.0 1.2 reshape.187
  23.3 19.0 %all-to-all-start = ((bf16[16,10,2,1280]{3,2,1,0:T(2,128)(2,1)}), bf16[16,10,2,1280]{3,2,1,0:T(2,128)(2,1)S(1)}, u32[]{:S(2)}, u32[]{:S(2)}) async-start(bf16[16,10,2,1280]{3,2,1,0:T(2,128)(2,1)} %reshape.187), calls=%async_computation | async-start | bytes 1638400 | tf_op jit(solution)/shard_map/all_to_all | solution.py:219
  42.3 0.0 copy-start
  42.3 0.0 collective-permute-done.5.refs_5_
  42.3 1.4 collective-permute-start.7
  43.7 0.0 collective-permute-done.9.refs_10_
  43.7 1.5 collective-permute-start.10
  45.2 20.4 %all-to-all-done = bf16[16,10,2,1280]{3,2,1,0:T(2,128)(2,1)S(1)} async-done(((bf16[16,10,2,1280]{3,2,1,0:T(2,128)(2,1)}), bf16[16,10,2,1280]{3,2,1,0:T(2,128)(2,1)S(1)}, u32[]{:S(2)}, u32[]{:S(2)}) %all-to-all-start) | async-done | bytes 819232 | tf_op jit(solution)/shard_map/all_to_all | solution.py:219
  65.6 0.1 copy.18
  65.7 1.3 collective-permute-start.2
  67.0 0.0 collective-permute-done.6.refs_6_
  67.0 2.7 %collective-permute-start.3 = (bf16[2,160,1280]{2,1,0:T(8,128)(2,1)S(1)}, bf16[2,160,1280]{2,1,0:T(8,128)(2,1)}, u32[]{:S(2)}, u32[]{:S(2)}) collective-permute-start(bf16[2,160,1280]{2,1,0:T(8,128)(2,1)S(1)} %bitcast.54), channel_id=1, source_target_pairs={{0,192},{1,49},{2,194},{3,51},{4,196},{5,53},{6,198},{7,55},{8,200... | collective-permute-start | bytes 2457608 | tf_op jit(solution)/shard_map/ppermute | solution.py:222
  69.6 1.2 collective-permute-start.4
  70.8 18.0 %all-gather.1 = f32[4,2,320]{2,1,0:T(2,128)S(1)} all-gather(f32[1,2,320]{2,1,0:T(2,128)S(1)} %bitcast.64), channel_id=2, replica_groups={{0,16,32,48},{64,80,96,112},{128,144,160,176},{192,208,224,240},{1,65,1..., dimensions={0}, use_global_device_ids=true | all-gather | bytes 12800 | tf_op jit(solution)/shard_map/all_gather | solution.py:169
  88.8 0.1 concatenate.11.refs_12_
  89.0 0.0 collective-permute-done.2.refs_1_
  89.0 0.0 collective-permute-done.3.refs_2_
  89.0 0.4 collective-permute-done.4.refs_3_
  89.4 0.0 collective-permute-done.7.refs_7_
  89.4 0.0 collective-permute-done.10.refs_11_
  89.4 15.2 %ffn.1 = (bf16[2,160,1280]{2,1,0:T(8,128)(2,1)S(1)}, bf16[2,160,1280]{2,1,0:T(8,128)(2,1)S(1)}, bf16[2,160,1280]{2,1,0:T(8,128)(2,1)S(1)}, bf16[2,160,1280]{2,1,0:T(8,128)(2,1)S(1)}) custom-call(bf16[2,160,1280]{2,1,0:T(8,128)(2,1)S(1)} %bitcast.56, bf16[2,160,1280]{2,1,0:T(8,128)(2,1)S(1)} %collective-permute-done.2.refs_1_, ...), custom_call_target="tpu_custom_call" | custom-call | flops 8388608000 | bytes 19660800 | tf_op jit(solution)/shard_map/ffn/pallas_call | solution.py:126
  104.6 1.7 %collective-permute-start.11 = (bf16[2,160,1280]{2,1,0:T(8,128)(2,1)S(1)}, bf16[2,160,1280]{2,1,0:T(8,128)(2,1)S(1)}, u32[]{:S(2)}, u32[]{:S(2)}) collective-permute-start(bf16[2,160,1280]{2,1,0:T(8,128)(2,1)S(1)} %get-tuple-element.10), channel_id=1, source_target_pairs={{0,192},{1,49},{2,194},{3,51},{4,196},{5,53},{6,198},{7,55},{8,200... | collective-permute-start | bytes 2457608 | tf_op jit(solution)/shard_map/ppermute | solution.py:232
  106.3 1.3 collective-permute-start.13
  107.5 16.8 %collective-permute-done.11 = bf16[2,160,1280]{2,1,0:T(8,128)(2,1)S(1)} collective-permute-done((bf16[2,160,1280]{2,1,0:T(8,128)(2,1)S(1)}, bf16[2,160,1280]{2,1,0:T(8,128)(2,1)S(1)}, u32[]{:S(2)}, u32[]{:S(2)}) %collective-permute-start.11) | collective-permute-done | bytes 819232 | tf_op jit(solution)/shard_map/ppermute | solution.py:232
  124.3 3.1 %collective-permute-done.12 = bf16[2,160,1280]{2,1,0:T(8,128)(2,1)S(1)} collective-permute-done((bf16[2,160,1280]{2,1,0:T(8,128)(2,1)S(1)}, bf16[2,160,1280]{2,1,0:T(8,128)(2,1)S(1)}, u32[]{:S(2)}, u32[]{:S(2)}) %collective-permute-start.12) | collective-permute-done | bytes 819232 | tf_op jit(solution)/shard_map/ppermute | solution.py:233
  127.4 0.5 add_convert_fusion
  127.9 0.0 copy-start.10
  127.9 1.7 %copy.21 = bf16[2,10,16,1280]{3,0,1,2:T(2,128)(2,1)} copy(bf16[2,10,16,1280]{3,2,1,0:T(8,128)(2,1)S(1)} %bitcast.61) | data formatting | bytes 1638400 | tf_op jit(solution)/shard_map/reshape | solution.py:239
  129.7 7.4 %all-to-all-start.1 = ((bf16[16,10,2,1280]{3,2,1,0:T(2,128)(2,1)}), bf16[16,10,2,1280]{3,2,1,0:T(2,128)(2,1)S(1)}, u32[]{:S(2)}, u32[]{:S(2)}) async-start(bf16[16,10,2,1280]{3,2,1,0:T(2,128)(2,1)} %bitcast.52), calls=%async_computation.1 | async-start | bytes 1638400 | tf_op jit(solution)/shard_map/all_to_all | solution.py:241
  137.1 0.1 mul.215
  137.1 23.2 %all-to-all-done.1 = bf16[16,10,2,1280]{3,2,1,0:T(2,128)(2,1)S(1)} async-done(((bf16[16,10,2,1280]{3,2,1,0:T(2,128)(2,1)}), bf16[16,10,2,1280]{3,2,1,0:T(2,128)(2,1)S(1)}, u32[]{:S(2)}, u32[]{:S(2)}) %all-to-all-start.1) | async-done | bytes 819232 | tf_op jit(solution)/shard_map/all_to_all | solution.py:241
  160.4 0.3 reshape.190
  160.7 1.4 fusion.1
  (29 shorter events, 0.1 us)
Async XLA Ops:
  0.0 15.0 %copy-start.3 = (bf16[1,4,64,1280]{3,2,1,0:T(8,128)(2,1)S(1)}, bf16[1,4,64,1280]{3,2,1,0:T(8,128)(2,1)}, u32[]{:S(2)}) copy-start(bf16[1,4,64,1280]{3,2,1,0:T(8,128)(2,1)} %param.11) | copy-start | bytes 1966084
  0.0 15.9 %copy-start.11 = (s32[1,4,64,1]{2,3,1,0:T(1,128)S(1)}, s32[1,4,64,1]{2,3,1,0:T(1,128)}, u32[]{:S(2)}) copy-start(s32[1,4,64,1]{2,3,1,0:T(1,128)} %param.12) | copy-start | bytes 3076
  0.0 16.8 %copy-start.5 = (f32[1280]{0:T(1024)S(1)}, f32[1280]{0:T(1024)}, u32[]{:S(2)}) copy-start(f32[1280]{0:T(1024)} %param.14) | copy-start | bytes 15364
  0.0 42.3 %collective-permute-start.5 = (bf16[2,320,1280]{2,1,0:T(8,128)(2,1)}, bf16[2,320,1280]{2,1,0:T(8,128)(2,1)}, u32[]{:S(2)}, u32[]{:S(2)}) collective-permute-start(bf16[2,320,1280]{2,1,0:T(8,128)(2,1)} %bitcast.57), channel_id=1, source_target_pairs={{0,16},{1,65},{2,18},{3,67},{4,20},{5,69},{6,22},{7,71},{8,24},{9,... | collective-permute-start | bytes 4915208 | tf_op jit(solution)/shard_map/ppermute | solution.py:163
  2.2 64.7 %collective-permute-start.6 = (bf16[2,320,1280]{2,1,0:T(8,128)(2,1)}, bf16[2,320,1280]{2,1,0:T(8,128)(2,1)}, u32[]{:S(2)}, u32[]{:S(2)}) collective-permute-start(bf16[2,320,1280]{2,1,0:T(8,128)(2,1)} %bitcast.58), channel_id=1, source_target_pairs={{0,48},{1,193},{2,50},{3,195},{4,52},{5,197},{6,54},{7,199},{8,56}... | collective-permute-start | bytes 4915208 | tf_op jit(solution)/shard_map/ppermute | solution.py:164
  4.8 12.5 %collective-permute-start = (bf16[1,64,1280]{2,1,0:T(8,128)(2,1)S(1)}, bf16[1,64,1280]{2,1,0:T(8,128)(2,1)S(1)}, u32[]{:S(2)}, u32[]{:S(2)}) collective-permute-start(bf16[1,64,1280]{2,1,0:T(8,128)(2,1)S(1)} %get-tuple-element.24), channel_id=1, source_target_pairs={{0,16},{16,32},{32,48},{48,64},{64,80},{80,96},{96,112},{112,128},... | collective-permute-start | bytes 491528 | tf_op jit(solution)/shard_map/ppermute | solution.py:44
  7.9 9.3 %copy-start.4 = (f32[3,3,1280]{2,1,0:T(4,128)S(1)}, f32[3,3,1280]{2,1,0:T(4,128)}, u32[]{:S(2)}) copy-start(f32[3,3,1280]{2,1,0:T(4,128)} %param.16) | copy-start | bytes 138244
  7.9 9.5 %collective-permute-start.1 = (bf16[1,64,1280]{2,1,0:T(8,128)(2,1)S(1)}, bf16[1,64,1280]{2,1,0:T(8,128)(2,1)S(1)}, u32[]{:S(2)}, u32[]{:S(2)}) collective-permute-start(bf16[1,64,1280]{2,1,0:T(8,128)(2,1)S(1)} %get-tuple-element.25), channel_id=1, source_target_pairs={{16,0},{32,16},{48,32},{64,48},{80,64},{96,80},{112,96},{128,112},... | collective-permute-start | bytes 491528 | tf_op jit(solution)/shard_map/ppermute | solution.py:46
  9.3 34.3 %collective-permute-start.9 = (bf16[2,320,1280]{2,1,0:T(8,128)(2,1)}, bf16[2,320,1280]{2,1,0:T(8,128)(2,1)}, u32[]{:S(2)}, u32[]{:S(2)}) collective-permute-start(bf16[2,320,1280]{2,1,0:T(8,128)(2,1)} %refs_8_.1), channel_id=1, source_target_pairs={{0,48},{1,193},{2,50},{3,195},{4,52},{5,197},{6,54},{7,199},{8,56}... | collective-permute-start | bytes 4915208 | tf_op jit(solution)/shard_map/ppermute | solution.py:166
  17.3 52.3 %collective-permute-start.8 = (bf16[2,320,1280]{2,1,0:T(8,128)(2,1)}, bf16[2,320,1280]{2,1,0:T(8,128)(2,1)}, u32[]{:S(2)}, u32[]{:S(2)}) collective-permute-start(bf16[2,320,1280]{2,1,0:T(8,128)(2,1)} %refs_8_.1), channel_id=1, source_target_pairs={{0,16},{1,65},{2,18},{3,67},{4,20},{5,69},{6,22},{7,71},{8,24},{9,... | collective-permute-start | bytes 4915208 | tf_op jit(solution)/shard_map/ppermute | solution.py:165
  18.1 0.7 copy-start.8
  20.5 1.1 copy-start.1
  20.5 0.7 copy-start.7
  23.3 42.3 %all-to-all-start = ((bf16[16,10,2,1280]{3,2,1,0:T(2,128)(2,1)}), bf16[16,10,2,1280]{3,2,1,0:T(2,128)(2,1)S(1)}, u32[]{:S(2)}, u32[]{:S(2)}) async-start(bf16[16,10,2,1280]{3,2,1,0:T(2,128)(2,1)} %reshape.187), calls=%async_computation | async-start | bytes 1638400 | tf_op jit(solution)/shard_map/all_to_all | solution.py:219
  42.2 28.6 %copy-start.9 = (f32[2,320]{1,0:T(2,128)S(1)}, f32[2,320]{1,0:T(2,128)}, u32[]{:S(2)}) copy-start(f32[2,320]{1,0:T(2,128)} %param.19) | copy-start | bytes 7684
  42.3 47.1 %copy-start = (bf16[2,1280,320]{1,2,0:T(8,128)(2,1)S(1)}, bf16[2,1280,320]{1,2,0:T(8,128)(2,1)}, u32[]{:S(2)}) copy-start(bf16[2,1280,320]{1,2,0:T(8,128)(2,1)} %param.18) | copy-start | bytes 4915204
  42.3 47.1 %collective-permute-start.7 = (bf16[2,320,1280]{2,1,0:T(8,128)(2,1)}, bf16[2,320,1280]{2,1,0:T(8,128)(2,1)}, u32[]{:S(2)}, u32[]{:S(2)}) collective-permute-start(bf16[2,320,1280]{2,1,0:T(8,128)(2,1)} %collective-permute-done.5.refs_5_), channel_id=1, source_target_pairs={{0,16},{1,65},{2,18},{3,67},{4,20},{5,69},{6,22},{7,71},{8,24},{9,... | collective-permute-start | bytes 4915208 | tf_op jit(solution)/shard_map/ppermute | solution.py:167
  43.7 45.7 %collective-permute-start.10 = (bf16[2,320,1280]{2,1,0:T(8,128)(2,1)}, bf16[2,320,1280]{2,1,0:T(8,128)(2,1)}, u32[]{:S(2)}, u32[]{:S(2)}) collective-permute-start(bf16[2,320,1280]{2,1,0:T(8,128)(2,1)} %collective-permute-done.9.refs_10_), channel_id=1, source_target_pairs={{0,48},{1,193},{2,50},{3,195},{4,52},{5,197},{6,54},{7,199},{8,56}... | collective-permute-start | bytes 4915208 | tf_op jit(solution)/shard_map/ppermute | solution.py:168
  65.7 23.3 %collective-permute-start.2 = (bf16[2,160,1280]{2,1,0:T(8,128)(2,1)S(1)}, bf16[2,160,1280]{2,1,0:T(8,128)(2,1)S(1)}, u32[]{:S(2)}, u32[]{:S(2)}) collective-permute-start(bf16[2,160,1280]{2,1,0:T(8,128)(2,1)S(1)} %bitcast.53), channel_id=1, source_target_pairs={{0,64},{1,17},{2,66},{3,19},{4,68},{5,21},{6,70},{7,23},{8,72},{9,... | collective-permute-start | bytes 2457608 | tf_op jit(solution)/shard_map/ppermute | solution.py:221
  67.0 22.0 %collective-permute-start.3 = (bf16[2,160,1280]{2,1,0:T(8,128)(2,1)S(1)}, bf16[2,160,1280]{2,1,0:T(8,128)(2,1)}, u32[]{:S(2)}, u32[]{:S(2)}) collective-permute-start(bf16[2,160,1280]{2,1,0:T(8,128)(2,1)S(1)} %bitcast.54), channel_id=1, source_target_pairs={{0,192},{1,49},{2,194},{3,51},{4,196},{5,53},{6,198},{7,55},{8,200... | collective-permute-start | bytes 2457608 | tf_op jit(solution)/shard_map/ppermute | solution.py:222
  69.6 19.8 %collective-permute-start.4 = (bf16[2,160,1280]{2,1,0:T(8,128)(2,1)S(1)}, bf16[2,160,1280]{2,1,0:T(8,128)(2,1)}, u32[]{:S(2)}, u32[]{:S(2)}) collective-permute-start(bf16[2,160,1280]{2,1,0:T(8,128)(2,1)S(1)} %bitcast.55), channel_id=1, source_target_pairs={{0,128},{1,33},{2,130},{3,35},{4,132},{5,37},{6,134},{7,39},{8,136... | collective-permute-start | bytes 2457608 | tf_op jit(solution)/shard_map/ppermute | solution.py:223
  89.0 38.5 %copy-start.6 = (f32[2,1280]{1,0:T(2,128)S(1)}, f32[2,1280]{1,0:T(2,128)}, u32[]{:S(2)}) copy-start(f32[2,1280]{1,0:T(2,128)} %param.21) | copy-start | bytes 30724
  104.6 19.7 %collective-permute-start.11 = (bf16[2,160,1280]{2,1,0:T(8,128)(2,1)S(1)}, bf16[2,160,1280]{2,1,0:T(8,128)(2,1)S(1)}, u32[]{:S(2)}, u32[]{:S(2)}) collective-permute-start(bf16[2,160,1280]{2,1,0:T(8,128)(2,1)S(1)} %get-tuple-element.10), channel_id=1, source_target_pairs={{0,192},{1,49},{2,194},{3,51},{4,196},{5,53},{6,198},{7,55},{8,200... | collective-permute-start | bytes 2457608 | tf_op jit(solution)/shard_map/ppermute | solution.py:232
  106.3 21.2 %collective-permute-start.12 = (bf16[2,160,1280]{2,1,0:T(8,128)(2,1)S(1)}, bf16[2,160,1280]{2,1,0:T(8,128)(2,1)S(1)}, u32[]{:S(2)}, u32[]{:S(2)}) collective-permute-start(bf16[2,160,1280]{2,1,0:T(8,128)(2,1)S(1)} %get-tuple-element.11), channel_id=1, source_target_pairs={{0,64},{1,17},{2,66},{3,19},{4,68},{5,21},{6,70},{7,23},{8,72},{9,... | collective-permute-start | bytes 2457608 | tf_op jit(solution)/shard_map/ppermute | solution.py:233
  106.3 21.2 %collective-permute-start.13 = (bf16[2,160,1280]{2,1,0:T(8,128)(2,1)S(1)}, bf16[2,160,1280]{2,1,0:T(8,128)(2,1)S(1)}, u32[]{:S(2)}, u32[]{:S(2)}) collective-permute-start(bf16[2,160,1280]{2,1,0:T(8,128)(2,1)S(1)} %get-tuple-element.12), channel_id=1, source_target_pairs={{0,128},{1,33},{2,130},{3,35},{4,132},{5,37},{6,134},{7,39},{8,136... | collective-permute-start | bytes 2457608 | tf_op jit(solution)/shard_map/ppermute | solution.py:234
  127.9 9.1 %copy-start.10 = (f32[1,4,64]{2,1,0:T(4,128)S(1)}, f32[1,4,64]{2,1,0:T(4,128)}, u32[]{:S(2)}) copy-start(f32[1,4,64]{2,1,0:T(4,128)} %param.13) | copy-start | bytes 3076
  129.7 31.0 %copy-start.2 = (f32[4,64,1280]{2,1,0:T(8,128)S(1)}, f32[4,64,1280]{2,1,0:T(8,128)}, u32[]{:S(2)}) copy-start(f32[4,64,1280]{2,1,0:T(8,128)} %copy-done.1) | copy-start | bytes 3932164
  129.7 30.7 %all-to-all-start.1 = ((bf16[16,10,2,1280]{3,2,1,0:T(2,128)(2,1)}), bf16[16,10,2,1280]{3,2,1,0:T(2,128)(2,1)S(1)}, u32[]{:S(2)}, u32[]{:S(2)}) async-start(bf16[16,10,2,1280]{3,2,1,0:T(2,128)(2,1)} %bitcast.52), calls=%async_computation.1 | async-start | bytes 1638400 | tf_op jit(solution)/shard_map/all_to_all | solution.py:241

commit v2 on v0

v2 whole, which is shorter than its diff:
```python
import functools
import jax
import jax.numpy as jnp
import numpy as np
from jax import lax
from jax.experimental import pallas as pl
from jax.experimental.pallas import tpu as pltpu
from jax.sharding import PartitionSpec as P

SIDE = 4
AXES = ("seq", "exp")
VMEM = pl.BlockSpec(memory_space=pltpu.VMEM)
ANY = pl.BlockSpec(memory_space=pl.ANY)
HBM = pl.BlockSpec(memory_space=pltpu.HBM)
PIECES = 3
MIX_COST = 60000
ADD_COST = 16000
EXTRA = 16


def ring(shift, weights, exp_size):
    pairs = []
    for y in range(SIDE):
        for x in range(SIDE):
            for e in range(exp_size):
                along_x = (e % 2 == 0) == weights
                to_y = y if along_x else (y + shift) % SIDE
                to_x = (x + shift) % SIDE if along_x else x
                pairs.append(((y * SIDE + x) * exp_size + e, (to_y * SIDE + to_x) * exp_size + e))
    return pairs


def tables(holders, slots):
    pick = np.zeros((2, 2 * holders * slots, 4 * holders * slots), np.float32)
    for half in range(2):
        for j in range(2):
            for s in range(holders):
                for c in range(slots):
                    row = (j * holders + s) * slots + c
                    pick[half, row, s * 4 * slots + half * 2 * slots + j * slots + c] = 1.0
    return pick.astype(jnp.bfloat16), np.swapaxes(pick, 1, 2).astype(jnp.bfloat16)


def append_kernel(wi_ref, bias_ref, out_ref, rows_v, sems):
    experts, units, width = wi_ref.shape
    copies = []
    for j in range(experts):
        copy = pltpu.make_async_copy(wi_ref.at[j], out_ref.at[j, pl.ds(0, units)], sems.at[j])
        copy.start()
        copies.append(copy)
    rows_v[...] = jnp.zeros_like(rows_v)
    for j in range(experts):
        rows_v[j, 0:1, 0:units] = bias_ref[j : j + 1]
    for j in range(experts):
        left = rows_v[j, 0:1]
        for p in range(PIECES):
            piece = left.astype(jnp.bfloat16).astype(jnp.float32)
            left = left - piece
            for k in range(SIDE):
                row = PIECES * k + p
                rows_v[j, row : row + 1] = pltpu.roll(piece, k * units, 1) if k else piece
        out_ref[j, units : units + EXTRA] = rows_v[j].astype(jnp.bfloat16)
    for copy in copies:
        copy.wait()


def append_rows(wi, bias):
    experts, units, width = wi.shape
    return pl.pallas_call(
        append_kernel,
        out_shape=jax.ShapeDtypeStruct((experts, units + EXTRA, width), jnp.bfloat16),
        in_specs=[ANY, VMEM],
        out_specs=VMEM,
        scratch_shapes=[
            pltpu.VMEM((experts, EXTRA, width), jnp.float32),
            pltpu.SemaphoreType.DMA((experts,)),
        ],
        compiler_params=pltpu.CompilerParams(vmem_limit_bytes=8 * 1024 * 1024),
        name="append_rows",
    )(wi, bias)


def normalize(values, scales):
    row_mean = jnp.mean(values, axis=-1, keepdims=True)
    centred = values - row_mean
    row_var = jnp.mean(centred * centred, axis=-1, keepdims=True)
    return centred * lax.rsqrt(row_var + 1e-06) * scales


def gelu(v):
    return 0.5 * v * (1.0 + lax.erf(v * 0.7071067811865476))


def mix_kernel(
    holders,
    slots,
    tok_ref,
    up_ref,
    down_ref,
    ids_ref,
    mixer_gain,
    expert_gain,
    conv_weight,
    conv_bias,
    mixed_ref,
    msg_ref,
    column_ref,
    norm_v,
    in_v,
    mixed_v,
    msg_v,
    sems,
):
    rows, cols, width = tok_ref.shape
    tokens = rows * cols
    gain = mixer_gain[...].reshape(1, width)
    out_gain = expert_gain[...].reshape(1, width)
    shift = conv_bias[...].reshape(1, width)
    for r in range(rows):
        norm_v[r + 1] = normalize(tok_ref[r].astype(jnp.float32), gain).astype(jnp.bfloat16)
    norm_v[0] = normalize(up_ref[0].astype(jnp.float32), gain).astype(jnp.bfloat16)
    norm_v[rows + 1] = normalize(down_ref[0].astype(jnp.float32), gain).astype(jnp.bfloat16)
    place = lax.broadcasted_iota(jnp.int32, (cols, 1), 0)
    copies = []
    for r in range(rows):
        sums = []
        for b in range(3):
            total = None
            for a in range(3):
                term = norm_v[r + a].astype(jnp.float32) * conv_weight[a, b : b + 1]
                total = term if total is None else total + term
            sums.append(total)
        left = jnp.where(place == 0, 0.0, pltpu.roll(sums[0], 1, 0))
        right = jnp.where(place == cols - 1, 0.0, pltpu.roll(sums[2], cols - 1, 0))
        mixed = tok_ref[r].astype(jnp.float32) + shift + sums[1] + left + right
        at = pl.ds(r * cols, cols)
        mixed_v[at] = mixed
        in_v[at] = normalize(mixed, out_gain).astype(jnp.bfloat16)
    copies.append(pltpu.make_async_copy(mixed_v, mixed_ref, sems.at[0]))
    copies[0].start()
    ids = ids_ref[...]
    experts = 2 * holders
    kinds = lax.broadcasted_iota(jnp.int32, (experts, tokens), 0)
    hot = kinds == ids
    before = lax.broadcasted_iota(jnp.int32, (tokens, tokens), 0) < lax.broadcasted_iota(
        jnp.int32, (tokens, tokens), 1
    )
    earlier = jnp.dot(
        hot.astype(jnp.float32).astype(jnp.bfloat16),
        before.astype(jnp.float32).astype(jnp.bfloat16),
        preferred_element_type=jnp.float32,
    )
    rank = jnp.sum(jnp.where(hot, earlier, 0.0), axis=0, keepdims=True).astype(jnp.int32)
    holder = lax.shift_right_logical(ids, 1)
    which = ids & 1
    col = holder * (4 * slots) + which * slots + rank
    column_ref[...] = col
    at = lax.broadcasted_iota(jnp.int32, (4 * slots * holders, tokens), 0)
    pick_left = (at == col).astype(jnp.float32).astype(jnp.bfloat16)
    pick_right = (at == col + 2 * slots).astype(jnp.float32).astype(jnp.bfloat16)
    msg_v[...] = (
        jnp.dot(pick_left, in_v[:, : width // 2], preferred_element_type=jnp.float32)
        + jnp.dot(pick_right, in_v[:, width // 2 :], preferred_element_type=jnp.float32)
    ).astype(jnp.bfloat16)
    copies.append(pltpu.make_async_copy(msg_v, msg_ref, sems.at[1]))
    copies[1].start()
    for copy in copies:
        copy.wait()


def mix(holders, slots, tokens, up, down, ids, mixer_gain, expert_gain, conv_weight, conv_bias):
    rows, cols, width = tokens.shape
    size = rows * cols * width
    message = (4 * slots * holders, width // 2)
    return pl.pallas_call(
        functools.partial(mix_kernel, holders, slots),
        out_shape=[
            jax.ShapeDtypeStruct((rows * cols, width), jnp.float32),
            jax.ShapeDtypeStruct(message, jnp.bfloat16),
            jax.ShapeDtypeStruct((1, rows * cols), jnp.int32),
        ],
        in_specs=[VMEM] * 8,
        out_specs=[HBM, HBM, VMEM],
        scratch_shapes=[
            pltpu.VMEM((rows + 2, cols, width), jnp.bfloat16),
            pltpu.VMEM((rows * cols, width), jnp.bfloat16),
            pltpu.VMEM((rows * cols, width), jnp.float32),
            pltpu.VMEM(message, jnp.bfloat16),
            pltpu.SemaphoreType.DMA((2,)),
        ],
        compiler_params=pltpu.CompilerParams(vmem_limit_bytes=16 * 1024 * 1024),
        cost_estimate=pl.CostEstimate(flops=MIX_COST * size, transcendentals=0, bytes_accessed=6 * size),
        name="mix",
    )(tokens, up, down, ids, mixer_gain, expert_gain, conv_weight, conv_bias)


def ffn_kernel(count, *refs):
    wis, wos, refs = refs[0:4], refs[4:8], refs[8:]
    pick, place, refs = refs[0], refs[1], refs[2:]
    msgs, outs, refs = refs[:count], refs[count : 2 * count], refs[2 * count :]
    r_v, x_v, wi_v, wo_v, b_v, y_v, o_v, msg_sem, w_sem, b_sem, out_sem = refs
    experts, _, width = x_v.shape
    rows = pick.shape[1] // experts
    units = wos[0].shape[1]
    half = width // 2
    msg_copies = []
    for k in range(count):
        copy = pltpu.make_async_copy(msgs[k], r_v.at[k], msg_sem.at[k])
        copy.start()
        msg_copies.append(copy)
    w_copies = {}
    for j in range(experts):
        for what, (sources, target) in enumerate(((wis, wi_v), (wos, wo_v))):
            group = []
            for k in range(SIDE):
                copy = pltpu.make_async_copy(
                    sources[k].at[j, pl.ds(0, units)],
                    target.at[j, pl.ds(k * units, units)],
                    w_sem.at[j, what, k],
                )
                copy.start()
                group.append(copy)
                if what == 0:
                    copy = pltpu.make_async_copy(
                        wis[k].at[j, pl.ds(units, EXTRA)], b_v.at[j, k], b_sem.at[j, k]
                    )
                    copy.start()
                    group.append(copy)
            w_copies[j, what] = group
    for k in range(count):
        msg_copies[k].wait()
        for side in range(2):
            rows_of = jnp.dot(pick[side], r_v[k], preferred_element_type=jnp.float32).astype(
                jnp.bfloat16
            )
            for j in range(experts):
                x_v[j, k * rows : (k + 1) * rows, side * half : (side + 1) * half] = rows_of[
                    j * rows : (j + 1) * rows
                ]
    for j in range(experts):
        for copy in w_copies[j, 0]:
            copy.wait()
        hidden = lax.dot_general(
            x_v[j], wi_v[j], (((1,), (1,)), ((), ())), preferred_element_type=jnp.float32
        )
        bias = sum(
            jnp.sum(
                b_v[j, k].astype(jnp.float32)[PIECES * k : PIECES * (k + 1)], axis=0, keepdims=True
            )
            for k in range(SIDE)
        )
        hidden = gelu(hidden + bias).astype(jnp.bfloat16)
        for copy in w_copies[j, 1]:
            copy.wait()
        part = jnp.dot(hidden, wo_v[j], preferred_element_type=jnp.float32).astype(jnp.bfloat16)
        for k in range(count):
            y_v[k, j * rows : (j + 1) * rows] = part[k * rows : (k + 1) * rows]
    out_copies = []
    for k in range(count):
        o_v[k] = (
            jnp.dot(place[0], y_v[k, :, :half], preferred_element_type=jnp.float32)
            + jnp.dot(place[1], y_v[k, :, half:], preferred_element_type=jnp.float32)
        ).astype(jnp.bfloat16)
        copy = pltpu.make_async_copy(o_v.at[k], outs[k], out_sem.at[k])
        copy.start()
        out_copies.append(copy)
    for copy in out_copies:
        copy.wait()


def ffn(msgs, wis, wos, pick, place):
    experts, units, width = wos[0].shape
    count = len(msgs)
    rows = pick.shape[1] // experts
    total = count * rows
    flops = 4 * experts * total * SIDE * units * width
    moved = 2 * experts * width * (4 * total + 2 * SIDE * units)
    return pl.pallas_call(
        functools.partial(ffn_kernel, count),
        out_shape=[jax.ShapeDtypeStruct(msgs[0].shape, jnp.bfloat16)] * count,
        in_specs=[ANY] * 8 + [VMEM] * 2 + [ANY] * count,
        out_specs=[ANY] * count,
        scratch_shapes=[
            pltpu.VMEM((count,) + msgs[0].shape, jnp.bfloat16),
            pltpu.VMEM((experts, total, width), jnp.bfloat16),
            pltpu.VMEM((experts, SIDE * units, width), jnp.bfloat16),
            pltpu.VMEM((experts, SIDE * units, width), jnp.bfloat16),
            pltpu.VMEM((experts, SIDE, EXTRA, width), jnp.bfloat16),
            pltpu.VMEM((count, experts * rows, width), jnp.bfloat16),
            pltpu.VMEM((count,) + msgs[0].shape, jnp.bfloat16),
            pltpu.SemaphoreType.DMA((count,)),
            pltpu.SemaphoreType.DMA((experts, 2, SIDE)),
            pltpu.SemaphoreType.DMA((experts, SIDE)),
            pltpu.SemaphoreType.DMA((count,)),
        ],
        compiler_params=pltpu.CompilerParams(vmem_limit_bytes=32 * 1024 * 1024),
        cost_estimate=pl.CostEstimate(flops=2 * flops, transcendentals=0, bytes_accessed=moved),
        name="ffn",
    )(*wis, *wos, pick, place, *msgs)


def add_kernel(a_ref, b_ref, c_ref, out_ref):
    out_ref[...] = a_ref[...].astype(jnp.float32) + b_ref[...].astype(jnp.float32) + c_ref[...]


def add_parts(a, b, c):
    return pl.pallas_call(
        add_kernel,
        out_shape=jax.ShapeDtypeStruct(a.shape, jnp.float32),
        in_specs=[VMEM] * 3,
        out_specs=VMEM,
        cost_estimate=pl.CostEstimate(
            flops=ADD_COST * a.size, transcendentals=0, bytes_accessed=12 * a.size
        ),
        compiler_params=pltpu.CompilerParams(vmem_limit_bytes=16 * 1024 * 1024),
        name="add_parts",
    )(a, b, c)


def combine_kernel(mixed_ref, gate_ref, col_ref, msg_ref, out_ref):
    tokens, width = mixed_ref.shape
    gate = gate_ref[...]
    count = msg_ref.shape[0]
    step = count // 32
    at_col = lax.broadcasted_iota(jnp.int32, (tokens, count), 1)
    for side in range(2):
        at = slice(side * width // 2, (side + 1) * width // 2)
        pick = at_col == col_ref[...] + step * side
        picked = jnp.dot(
            pick.astype(jnp.float32).astype(jnp.bfloat16),
            msg_ref[...],
            preferred_element_type=jnp.float32,
        )
        out_ref[:, at] = (mixed_ref[:, at] + gate * picked).astype(jnp.bfloat16)


def combine(mixed, gate, columns, msg):
    return pl.pallas_call(
        combine_kernel,
        out_shape=jax.ShapeDtypeStruct(mixed.shape, jnp.bfloat16),
        in_specs=[VMEM] * 4,
        out_specs=VMEM,
        compiler_params=pltpu.CompilerParams(vmem_limit_bytes=16 * 1024 * 1024),
        name="combine",
    )(mixed, gate, columns, msg)


def body(
    tokens,
    expert_ids,
    gate_values,
    mixer_gain,
    expert_gain,
    conv_weight,
    conv_bias,
    w_in,
    b_in,
    w_out,
    b_out,
):
    exp_size = lax.axis_size("exp")
    seq_size = lax.axis_size("seq")
    send_w = functools.partial(ring, weights=True, exp_size=exp_size)
    send_t = functools.partial(ring, weights=False, exp_size=exp_size)
    _, row_count, col_count, width = tokens.shape
    tok_rows = row_count * col_count
    per_device = w_in.shape[0]
    slots = 5 * tok_rows // (4 * per_device * exp_size)

    together = lax.optimization_barrier
    head, tail = tokens[0, 0:1], tokens[0, row_count - 1 : row_count]
    wi = append_rows(jnp.swapaxes(w_in, 1, 2), b_in)
    head, tail, wo = together((head, tail, w_out))
    up = lax.ppermute(tail, "seq", [(i, i + 1) for i in range(seq_size - 1)])
    down = lax.ppermute(head, "seq", [(i + 1, i) for i in range(seq_size - 1)])
    wo_prev = lax.ppermute(wo, AXES, send_w(1))
    wo_next = lax.ppermute(wo, AXES, send_w(-1))
    wi_prev = lax.ppermute(wi, AXES, send_w(1))
    wi_next = lax.ppermute(wi, AXES, send_w(-1))
    wo_far = lax.ppermute(wo_prev, AXES, send_w(1))
    wi_far = lax.ppermute(wi_next, AXES, send_w(-1))
    mixed, msg, columns = mix(
        exp_size,
        slots,
        tokens[0],
        up,
        down,
        expert_ids.reshape(1, tok_rows),
        mixer_gain,
        expert_gain,
        conv_weight,
        conv_bias,
    )

    def exchange(msg):
        shape = msg.shape
        msg = msg.reshape(exp_size, shape[0] // exp_size, shape[1])
        return lax.all_to_all(msg, "exp", split_axis=0, concat_axis=0, tiled=True).reshape(shape)

    msg = exchange(msg)
    msg_far = lax.ppermute(msg, AXES, send_t(2))
    msg_prev = lax.ppermute(msg, AXES, send_t(1))
    msg_next = lax.ppermute(msg, AXES, send_t(-1))
    weights = ((wi, wi_prev, wi_next, wi_far), (wo, wo_prev, wo_next, wo_far))
    lists = tables(exp_size, slots)
    (own,) = ffn((msg,), *weights, *lists)
    msg_far, own = together((msg_far, own))
    (far,) = ffn((msg_far,), *weights, *lists)
    msg_prev, msg_next, far = together((msg_prev, msg_next, far))
    prev, nxt = ffn((msg_prev, msg_next), *weights, *lists)
    far = lax.ppermute(far, AXES, send_t(2))
    prev = lax.ppermute(prev, AXES, send_t(-1))
    nxt = lax.ppermute(nxt, AXES, send_t(1))
    shift = jnp.transpose(b_out.reshape(per_device, 2, width // 2), (1, 0, 2))
    shift = jnp.broadcast_to(shift[None, :, :, None], (exp_size, 2, per_device, slots, width // 2))
    early = add_parts(own, far, shift.reshape(own.shape))
    back = (early + prev.astype(jnp.float32) + nxt.astype(jnp.float32)).astype(jnp.bfloat16)
    back = exchange(back)
    result = combine(mixed, gate_values.reshape(tok_rows, 1), columns.reshape(tok_rows, 1), back)
    return result.reshape(tokens.shape)


def solution(mesh):
    in_specs = (
        P(("dp", "exp"), "seq", None, None),
        P(("dp", "exp"), "seq", None, None),
        P(("dp", "exp"), "seq", None),
        P(),
        P(),
        P(),
        P(),
        P("exp", None, "seq"),
        P("exp", "seq"),
        P("exp", "seq", None),
        P("exp", None),
    )
    out_specs = P(("dp", "exp"), "seq", None, None)
    return jax.shard_map(body, mesh=mesh, in_specs=in_specs, out_specs=out_specs, check_vma=False)
```

time: 335 us -> 172 us (0.51)
  waiting for transfers between devices: 220 us -> 71.1 us
  Pallas kernels: 0 us -> 36.6 us
  matrix products: 33.1 us -> 0 us
  blocking collectives: 33.1 us -> 0 us
  starting transfers between devices: 13.4 us -> 45.8 us
  between operations: 13.6 us -> 0.23 us
  other arithmetic: 10.4 us -> 3.03 us
    reduce_scatter x1 -> x0, waiting for transfers between devices: 101 us -> none  [body(): lax.psum_scatter(jnp.einsum('kcjf,jfd->kcjd', hidden, w_out, preferred_el...]
    all_gather x1 -> x0, waiting for transfers between devices: 95.3 us -> none  [body(): gathered = lax.all_gather(received, 'seq', axis=0, tiled=True)]
    pallas_call x0 -> x7, Pallas kernels: none -> 36.6 us  [the longest x3 28.6 us: ffn(): pl.pallas_call(functools.partial(ffn_kernel, count), out_shape=[jax.Shape...]
    dot_general x4 -> x0, matrix products: 33.1 us -> none  [the longest x1 29 us: body(): jnp.einsum('kcjf,jfd->kcjd', hidden, w_out, preferred_element_type=jnp.fl...]
    all_to_all x1 -> x0, blocking collectives: 33.1 us -> none  [body(): lax.all_to_all(dispatched, 'exp', split_axis=0, concat_axis=0, tiled=True)]
    ppermute x2 -> x14, waiting for transfers between devices: 0.01 us -> 31 us  [the longest x1 25.8 us: body(): wo_next = lax.ppermute(wo, AXES, send_w(-1))]
    ppermute x2 -> x14, starting transfers between devices: 5.25 us -> 24.2 us  [the longest x1 5.15 us: body(): wi_next = lax.ppermute(wi, AXES, send_w(-1))]
    all_to_all x1 -> x2, waiting for transfers between devices: 23.3 us -> 40.1 us  [exchange(): lax.all_to_all(msg, 'exp', split_axis=0, concat_axis=0, tiled=True)]
  transfers between devices with their start and end apart: 5 -> 16, of which waited for: 3 -> 5; matrix products, arithmetic and copies ran while one was open for 2% -> 3% of each run, Pallas kernels for 0% -> 20%
where the time goes in v2:
time: 172 us
  waiting for transfers between devices  71.1 us (41%)
  starting transfers between devices  45.8 us (27%)
  Pallas kernels  36.6 us (21%)
  local copies, waits for them, and re-layouts  14.8 us (9%)
  other arithmetic  3.03 us (2%)
    all_to_all x2, waiting for transfers between devices, exchange(): lax.all_to_all(msg, 'exp', split_axis=0, concat_axis=0, tiled=True)  40.1 us
    pallas_call x3, Pallas kernels, ffn(): pl.pallas_call(functools.partial(ffn_kernel, count), out_shape=[jax.Shape...  28.6 us
    ppermute x1, waiting for transfers between devices, body(): wo_next = lax.ppermute(wo, AXES, send_w(-1))  25.8 us
    all_to_all x2, starting transfers between devices, exchange(): lax.all_to_all(msg, 'exp', split_axis=0, concat_axis=0, tiled=True)  21.7 us
    unnamed x35, local copies, waits for them, and re-layouts  9.02 us
    ppermute x1, starting transfers between devices, body(): wi_next = lax.ppermute(wi, AXES, send_w(-1))  5.15 us
    ppermute x1, waiting for transfers between devices, body(): nxt = lax.ppermute(nxt, AXES, send_t(1))  5.08 us
    ppermute x1, starting transfers between devices, body(): up = lax.ppermute(tail, 'seq', [(i, i + 1) for i in range(seq_size - 1)])  4.6 us
  transfers between devices with their start and end apart: 16, of which 5 were waited for; matrix products, arithmetic and copies ran while one was open for 3% of the time, Pallas kernels for 20%

profile of v2, /device:TPU:1, one launch (start us, length us, event | category | flops | bytes accessed | tf_op | source)
XLA Modules:
  0.0 171.5 jit_solution(4461867594155769283)
XLA Ops:
  0.0 1.7 %slice_bitcast_fusion = (bf16[1,64,1280]{2,1,0:T(8,128)(2,1)}, bf16[1,64,1280]{2,1,0:T(8,128)(2,1)}) fusion(bf16[1,4,64,1280]{3,2,1,0:T(8,128)(2,1)} %param.13), kind=kLoop, calls=%fused_computation.1 | loop fusion | bytes 655360 | tf_op jit(solution)/shard_map/squeeze | solution.py:371
  1.7 4.6 %collective-permute-start = (bf16[1,64,1280]{2,1,0:T(8,128)(2,1)}, bf16[1,64,1280]{2,1,0:T(8,128)(2,1)}, u32[]{:S(2)}, u32[]{:S(2)}) collective-permute-start(bf16[1,64,1280]{2,1,0:T(8,128)(2,1)} %get-tuple-element.18), channel_id=1, source_target_pairs={{0,16},{16,32},{32,48},{48,64},{64,80},{80,96},{96,112},{112,128},... | collective-permute-start | bytes 491528 | tf_op jit(solution)/shard_map/ppermute | solution.py:374
  6.3 1.3 collective-permute-start.1
  7.6 0.0 copy-start.2
  7.6 1.4 copy-done.2
  9.1 0.7 copy-done.9
  9.7 0.0 copy-start.13
  9.8 0.4 append_rows.1.refs_0_
  10.1 5.1 %collective-permute-start.4 = (bf16[2,336,1280]{2,1,0:T(8,128)(2,1)S(1)}, bf16[2,336,1280]{2,1,0:T(8,128)(2,1)S(1)}, u32[]{:S(2)}, u32[]{:S(2)}) collective-permute-start(bf16[2,336,1280]{2,1,0:T(8,128)(2,1)S(1)} %append_rows.1.refs_0_), channel_id=1, source_target_pairs={{0,48},{1,193},{2,50},{3,195},{4,52},{5,197},{6,54},{7,199},{8,56}... | collective-permute-start | bytes 5160968 | tf_op jit(solution)/shard_map/ppermute | solution.py:379
  15.3 0.0 collective-permute-start.6
  15.3 0.5 broadcast.4
  15.8 0.0 copy-done.16
  15.8 0.7 reduce.3
  16.5 0.1 reshape.31.ids_ref
  16.6 0.0 collective-permute-done.up_ref
  16.6 0.0 collective-permute-done.1.down_ref
  16.6 0.0 copy-start.8
  16.6 1.1 copy-done.8
  17.7 4.5 %mix.1 = (f32[256,1280]{1,0:T(8,128)S(1)}, bf16[640,640]{1,0:T(8,128)(2,1)S(1)}, s32[1,256]{1,0:T(1,128)S(1)}) custom-call(bf16[4,64,1280]{2,1,0:T(8,128)(2,1)S(1)} %bitcast.17, bf16[1,64,1280]{2,1,0:T(8,128)(2,1)} %collective-permute-done.up_ref, bf16[1,64,1280]{2,1,0:T(8,128)(2,1)} %collective-permute-done.1.down_ref, s32[1,256]{1,0:T(1,128)S(1)} %reshape.31.ids_ref, ...), custom_call_target="tpu_custom_call" | custom-call | flops 19660800000 | bytes 1966080 | tf_op jit(solution)/shard_map/mix/pallas_call | solution.py:175
  22.2 0.0 copy-start.3
  22.2 1.1 copy-done.3
  23.3 0.9 copy-done.5
  24.2 8.6 %all-to-all-start = ((bf16[16,40,640]{2,1,0:T(8,128)(2,1)}), bf16[16,40,640]{2,1,0:T(8,128)(2,1)}, u32[]{:S(2)}, u32[]{:S(2)}) async-start(bf16[16,40,640]{2,1,0:T(8,128)(2,1)} %bitcast.16), calls=%async_computation | async-start | bytes 1638400 | tf_op jit(solution)/shard_map/all_to_all | solution.py:398
  32.9 1.7 collective-permute-start.3
  34.6 0.0 collective-permute-done.4.refs_2_
  34.6 3.2 %collective-permute-start.5 = (bf16[2,336,1280]{2,1,0:T(8,128)(2,1)S(1)}, bf16[2,336,1280]{2,1,0:T(8,128)(2,1)}, u32[]{:S(2)}, u32[]{:S(2)}) collective-permute-start(bf16[2,336,1280]{2,1,0:T(8,128)(2,1)S(1)} %collective-permute-done.4.refs_2_), channel_id=1, source_target_pairs={{0,48},{1,193},{2,50},{3,195},{4,52},{5,197},{6,54},{7,199},{8,56}... | collective-permute-start | bytes 5160968 | tf_op jit(solution)/shard_map/ppermute | solution.py:381
  37.7 0.0 collective-permute-start.7
  37.8 0.0 collective-permute-done.6.refs_5_
  37.8 1.4 collective-permute-start.8
  39.2 17.1 %all-to-all-done = bf16[16,40,640]{2,1,0:T(8,128)(2,1)} async-done(((bf16[16,40,640]{2,1,0:T(8,128)(2,1)}), bf16[16,40,640]{2,1,0:T(8,128)(2,1)}, u32[]{:S(2)}, u32[]{:S(2)}) %all-to-all-start) | async-done | bytes 819232 | tf_op jit(solution)/shard_map/all_to_all | solution.py:398
  56.3 1.0 collective-permute-start.2
  57.3 25.8 %collective-permute-done.7.refs_6_ = bf16[2,320,1280]{2,1,0:T(8,128)(2,1)} collective-permute-done((bf16[2,320,1280]{2,1,0:T(8,128)(2,1)}, bf16[2,320,1280]{2,1,0:T(8,128)(2,1)}, u32[]{:S(2)}, u32[]{:S(2)}) %collective-permute-start.7) | collective-permute-done | bytes 1638432 | tf_op jit(solution)/shard_map/ppermute | solution.py:377
  83.1 0.0 collective-permute-start.9
  83.1 0.0 collective-permute-done.3.refs_1_
  83.1 2.7 %collective-permute-start.10 = (bf16[640,640]{1,0:T(8,128)(2,1)}, bf16[640,640]{1,0:T(8,128)(2,1)S(1)}, u32[]{:S(2)}, u32[]{:S(2)}) collective-permute-start(bf16[640,640]{1,0:T(8,128)(2,1)} %bitcast.5.refs_10_), channel_id=1, source_target_pairs={{0,192},{1,49},{2,194},{3,51},{4,196},{5,53},{6,198},{7,55},{8,200... | collective-permute-start | bytes 2457608 | tf_op jit(solution)/shard_map/ppermute | solution.py:403
  85.8 0.0 collective-permute-done.8.refs_7_
  85.8 0.0 collective-permute-done.5.refs_3_
  85.8 1.2 copy-done
  87.0 1.1 copy-done.1
  88.2 8.1 %ffn.3.a_ref = bf16[640,640]{1,0:T(8,128)(2,1)S(1)} custom-call(bf16[2,336,1280]{2,1,0:T(8,128)(2,1)S(1)} %append_rows.1.refs_0_, bf16[2,336,1280]{2,1,0:T(8,128)(2,1)} %collective-permute-done.3.refs_1_, bf16[2,336,1280]{2,1,0:T(8,128)(2,1)S(1)} %collective-permute-done.4.refs_2_, bf16[2,336,1280]{2,1,0:T(8,128)(2,1)} %collective-permute-done.5.refs_3_, ...), custom_call_target="tpu_custom_call" | custom-call | flops 4194304000 | bytes 16384000 | tf_op jit(solution)/shard_map/ffn/pallas_call | solution.py:278
  96.3 0.0 copy-start.6
  96.3 0.9 copy-done.6
  97.2 0.0 collective-permute-done.2.refs_10_
  97.2 8.9 %ffn.4 = bf16[640,640]{1,0:T(8,128)(2,1)} custom-call(bf16[2,336,1280]{2,1,0:T(8,128)(2,1)S(1)} %append_rows.1.refs_0_, bf16[2,336,1280]{2,1,0:T(8,128)(2,1)} %collective-permute-done.3.refs_1_, bf16[2,336,1280]{2,1,0:T(8,128)(2,1)S(1)} %collective-permute-done.4.refs_2_, bf16[2,336,1280]{2,1,0:T(8,128)(2,1)} %collective-permute-done.5.refs_3_, ...), custom_call_target="tpu_custom_call" | custom-call | flops 4194304000 | bytes 16384000 | tf_op jit(solution)/shard_map/ffn/pallas_call | solution.py:278
  106.1 0.0 copy-start.14
  106.1 0.0 collective-permute-done.9.refs_10_
  106.1 0.0 collective-permute-done.10.refs_11_
  106.1 0.3 collective-permute-start.11
  106.4 11.6 %ffn.5 = (bf16[640,640]{1,0:T(8,128)(2,1)}, bf16[640,640]{1,0:T(8,128)(2,1)}) custom-call(bf16[2,336,1280]{2,1,0:T(8,128)(2,1)S(1)} %append_rows.1.refs_0_, bf16[2,336,1280]{2,1,0:T(8,128)(2,1)} %collective-permute-done.3.refs_1_, bf16[2,336,1280]{2,1,0:T(8,128)(2,1)S(1)} %collective-permute-done.4.refs_2_, ...), custom_call_target="tpu_custom_call" | custom-call | flops 8388608000 | bytes 19660800 | tf_op jit(solution)/shard_map/ffn/pallas_call | solution.py:278
  118.1 0.8 collective-permute-start.13
  118.9 1.9 %collective-permute-start.12 = (bf16[640,640]{1,0:T(8,128)(2,1)}, bf16[640,640]{1,0:T(8,128)(2,1)}, u32[]{:S(2)}, u32[]{:S(2)}) collective-permute-start(bf16[640,640]{1,0:T(8,128)(2,1)} %get-tuple-element.29), channel_id=1, source_target_pairs={{0,192},{1,49},{2,194},{3,51},{4,196},{5,53},{6,198},{7,55},{8,200... | collective-permute-start | bytes 2457608 | tf_op jit(solution)/shard_map/ppermute | solution.py:412
  120.9 1.8 %broadcast_in_dim.2 = f32[16,2,2,10,640]{4,3,2,1,0:T(8,128)} broadcast(f32[2,2,640]{2,1,0:T(2,128)S(1)} %copy.15), dimensions={1,2,4} | broadcast | bytes 1648640 | tf_op jit(solution)/shard_map/broadcast_in_dim | solution.py:415
  122.6 1.9 %reshape.37.c_ref = f32[640,640]{1,0:T(8,128)S(1)} reshape(f32[16,2,2,10,640]{4,3,2,1,0:T(8,128)} %broadcast_in_dim.2) | data formatting | bytes 3276800 | tf_op jit(solution)/shard_map/reshape | solution.py:416
  124.6 0.0 collective-permute-done.11.b_ref
  124.6 1.4 add_parts.1
  126.0 5.1 %collective-permute-done.13 = bf16[640,640]{1,0:T(8,128)(2,1)S(1)} collective-permute-done((bf16[640,640]{1,0:T(8,128)(2,1)}, bf16[640,640]{1,0:T(8,128)(2,1)S(1)}, u32[]{:S(2)}, u32[]{:S(2)}) %collective-permute-start.13) | collective-permute-done | bytes 819232 | tf_op jit(solution)/shard_map/ppermute | solution.py:413
  131.1 0.1 collective-permute-done.12
  131.1 2.4 %add_convert_fusion = bf16[640,640]{1,0:T(8,128)(2,1)} fusion(bf16[640,640]{1,0:T(8,128)(2,1)S(1)} %collective-permute-done.13, f32[640,640]{1,0:T(8,128)S(1)} %add_parts.1, bf16[640,640]{1,0:T(8,128)(2,1)} %collective-permute-done.12), kind=kLoop, calls=%fused_computation | loop fusion | flops 2048000 | bytes 4096000 | tf_op jit(solution)/shard_map/convert_element_type | solution.py:417
  133.5 13.0 %all-to-all-start.1 = ((bf16[16,40,640]{2,1,0:T(8,128)(2,1)}), bf16[16,40,640]{2,1,0:T(8,128)(2,1)S(1)}, u32[]{:S(2)}, u32[]{:S(2)}) async-start(bf16[16,40,640]{2,1,0:T(8,128)(2,1)} %bitcast.8), calls=%async_computation.1 | async-start | bytes 1638400 | tf_op jit(solution)/shard_map/all_to_all | solution.py:398
  146.5 0.1 reshape.41.gate_ref
  146.7 0.1 copy.17.col_ref
  146.8 23.0 %all-to-all-done.1 = bf16[16,40,640]{2,1,0:T(8,128)(2,1)S(1)} async-done(((bf16[16,40,640]{2,1,0:T(8,128)(2,1)}), bf16[16,40,640]{2,1,0:T(8,128)(2,1)S(1)}, u32[]{:S(2)}, u32[]{:S(2)}) %all-to-all-start.1) | async-done | bytes 819232 | tf_op jit(solution)/shard_map/all_to_all | solution.py:398
  169.8 0.0 copy-done.4
  169.9 1.7 combine.1
  (20 shorter events, 0.1 us)
Async XLA Ops:
  1.7 14.8 %collective-permute-start = (bf16[1,64,1280]{2,1,0:T(8,128)(2,1)}, bf16[1,64,1280]{2,1,0:T(8,128)(2,1)}, u32[]{:S(2)}, u32[]{:S(2)}) collective-permute-start(bf16[1,64,1280]{2,1,0:T(8,128)(2,1)} %get-tuple-element.18), channel_id=1, source_target_pairs={{0,16},{16,32},{32,48},{48,64},{64,80},{80,96},{96,112},{112,128},... | collective-permute-start | bytes 491528 | tf_op jit(solution)/shard_map/ppermute | solution.py:374
  6.3 10.2 %collective-permute-start.1 = (bf16[1,64,1280]{2,1,0:T(8,128)(2,1)}, bf16[1,64,1280]{2,1,0:T(8,128)(2,1)}, u32[]{:S(2)}, u32[]{:S(2)}) collective-permute-start(bf16[1,64,1280]{2,1,0:T(8,128)(2,1)} %get-tuple-element.19), channel_id=1, source_target_pairs={{16,0},{32,16},{48,32},{64,48},{80,64},{96,80},{112,96},{128,112},... | collective-permute-start | bytes 491528 | tf_op jit(solution)/shard_map/ppermute | solution.py:375
  7.6 1.4 copy-start.2
  9.1 0.7 copy-start.9
  9.7 6.1 %copy-start.16 = (s32[1,4,64,1]{2,3,1,0:T(1,128)S(1)}, s32[1,4,64,1]{2,3,1,0:T(1,128)}, u32[]{:S(2)}) copy-start(s32[1,4,64,1]{2,3,1,0:T(1,128)} %param.14) | copy-start | bytes 3076
  9.7 6.8 %copy-start.10 = (f32[3,3,1280]{2,1,0:T(4,128)S(1)}, f32[3,3,1280]{2,1,0:T(4,128)}, u32[]{:S(2)}) copy-start(f32[3,3,1280]{2,1,0:T(4,128)} %conv_weight.1) | copy-start | bytes 138244
  9.7 6.8 %copy-start.11 = (f32[1280]{0:T(1024)S(1)}, f32[1280]{0:T(1024)}, u32[]{:S(2)}) copy-start(f32[1280]{0:T(1024)} %mixer_gain.1) | copy-start | bytes 15364
  9.7 6.8 %copy-start.12 = (f32[1280]{0:T(1024)S(1)}, f32[1280]{0:T(1024)}, u32[]{:S(2)}) copy-start(f32[1280]{0:T(1024)} %expert_gain.1) | copy-start | bytes 15364
  9.7 6.9 %copy-start.13 = (f32[1280]{0:T(1024)S(1)}, f32[1280]{0:T(1024)}, u32[]{:S(2)}) copy-start(f32[1280]{0:T(1024)} %conv_bias.1) | copy-start | bytes 15364
  10.1 24.4 %collective-permute-start.4 = (bf16[2,336,1280]{2,1,0:T(8,128)(2,1)S(1)}, bf16[2,336,1280]{2,1,0:T(8,128)(2,1)S(1)}, u32[]{:S(2)}, u32[]{:S(2)}) collective-permute-start(bf16[2,336,1280]{2,1,0:T(8,128)(2,1)S(1)} %append_rows.1.refs_0_), channel_id=1, source_target_pairs={{0,48},{1,193},{2,50},{3,195},{4,52},{5,197},{6,54},{7,199},{8,56}... | collective-permute-start | bytes 5160968 | tf_op jit(solution)/shard_map/ppermute | solution.py:379
  15.3 22.5 %collective-permute-start.6 = (bf16[2,320,1280]{2,1,0:T(8,128)(2,1)}, bf16[2,320,1280]{2,1,0:T(8,128)(2,1)}, u32[]{:S(2)}, u32[]{:S(2)}) collective-permute-start(bf16[2,320,1280]{2,1,0:T(8,128)(2,1)} %refs_4_.2), channel_id=1, source_target_pairs={{0,16},{1,65},{2,18},{3,67},{4,20},{5,69},{6,22},{7,71},{8,24},{9,... | collective-permute-start | bytes 4915208 | tf_op jit(solution)/shard_map/ppermute | solution.py:376
  16.6 1.1 copy-start.8
  22.2 1.1 copy-start.3
  23.3 0.9 copy-start.5
  24.2 32.0 %all-to-all-start = ((bf16[16,40,640]{2,1,0:T(8,128)(2,1)}), bf16[16,40,640]{2,1,0:T(8,128)(2,1)}, u32[]{:S(2)}, u32[]{:S(2)}) async-start(bf16[16,40,640]{2,1,0:T(8,128)(2,1)} %bitcast.16), calls=%async_computation | async-start | bytes 1638400 | tf_op jit(solution)/shard_map/all_to_all | solution.py:398
  32.9 50.3 %collective-permute-start.3 = (bf16[2,336,1280]{2,1,0:T(8,128)(2,1)S(1)}, bf16[2,336,1280]{2,1,0:T(8,128)(2,1)}, u32[]{:S(2)}, u32[]{:S(2)}) collective-permute-start(bf16[2,336,1280]{2,1,0:T(8,128)(2,1)S(1)} %append_rows.1.refs_0_), channel_id=1, source_target_pairs={{0,16},{1,65},{2,18},{3,67},{4,20},{5,69},{6,22},{7,71},{8,24},{9,... | collective-permute-start | bytes 5160968 | tf_op jit(solution)/shard_map/ppermute | solution.py:378
  34.6 51.3 %collective-permute-start.5 = (bf16[2,336,1280]{2,1,0:T(8,128)(2,1)S(1)}, bf16[2,336,1280]{2,1,0:T(8,128)(2,1)}, u32[]{:S(2)}, u32[]{:S(2)}) collective-permute-start(bf16[2,336,1280]{2,1,0:T(8,128)(2,1)S(1)} %collective-permute-done.4.refs_2_), channel_id=1, source_target_pairs={{0,48},{1,193},{2,50},{3,195},{4,52},{5,197},{6,54},{7,199},{8,56}... | collective-permute-start | bytes 5160968 | tf_op jit(solution)/shard_map/ppermute | solution.py:381
  37.7 45.4 %collective-permute-start.7 = (bf16[2,320,1280]{2,1,0:T(8,128)(2,1)}, bf16[2,320,1280]{2,1,0:T(8,128)(2,1)}, u32[]{:S(2)}, u32[]{:S(2)}) collective-permute-start(bf16[2,320,1280]{2,1,0:T(8,128)(2,1)} %refs_4_.2), channel_id=1, source_target_pairs={{0,48},{1,193},{2,50},{3,195},{4,52},{5,197},{6,54},{7,199},{8,56}... | collective-permute-start | bytes 4915208 | tf_op jit(solution)/shard_map/ppermute | solution.py:377
  37.8 48.0 %collective-permute-start.8 = (bf16[2,320,1280]{2,1,0:T(8,128)(2,1)}, bf16[2,320,1280]{2,1,0:T(8,128)(2,1)}, u32[]{:S(2)}, u32[]{:S(2)}) collective-permute-start(bf16[2,320,1280]{2,1,0:T(8,128)(2,1)} %collective-permute-done.6.refs_5_), channel_id=1, source_target_pairs={{0,16},{1,65},{2,18},{3,67},{4,20},{5,69},{6,22},{7,71},{8,24},{9,... | collective-permute-start | bytes 4915208 | tf_op jit(solution)/shard_map/ppermute | solution.py:380
  56.3 40.9 %collective-permute-start.2 = (bf16[640,640]{1,0:T(8,128)(2,1)}, bf16[640,640]{1,0:T(8,128)(2,1)S(1)}, u32[]{:S(2)}, u32[]{:S(2)}) collective-permute-start(bf16[640,640]{1,0:T(8,128)(2,1)} %bitcast.5.refs_10_), channel_id=1, source_target_pairs={{0,128},{1,33},{2,130},{3,35},{4,132},{5,37},{6,134},{7,39},{8,136... | collective-permute-start | bytes 2457608 | tf_op jit(solution)/shard_map/ppermute | solution.py:401
  83.1 23.0 %collective-permute-start.9 = (bf16[640,640]{1,0:T(8,128)(2,1)}, bf16[640,640]{1,0:T(8,128)(2,1)S(1)}, u32[]{:S(2)}, u32[]{:S(2)}) collective-permute-start(bf16[640,640]{1,0:T(8,128)(2,1)} %bitcast.5.refs_10_), channel_id=1, source_target_pairs={{0,64},{1,17},{2,66},{3,19},{4,68},{5,21},{6,70},{7,23},{8,72},{9,... | collective-permute-start | bytes 2457608 | tf_op jit(solution)/shard_map/ppermute | solution.py:402
  83.1 23.0 %collective-permute-start.10 = (bf16[640,640]{1,0:T(8,128)(2,1)}, bf16[640,640]{1,0:T(8,128)(2,1)S(1)}, u32[]{:S(2)}, u32[]{:S(2)}) collective-permute-start(bf16[640,640]{1,0:T(8,128)(2,1)} %bitcast.5.refs_10_), channel_id=1, source_target_pairs={{0,192},{1,49},{2,194},{3,51},{4,196},{5,53},{6,198},{7,55},{8,200... | collective-permute-start | bytes 2457608 | tf_op jit(solution)/shard_map/ppermute | solution.py:403
  85.8 1.2 copy-start
  87.0 1.1 copy-start.1
  96.3 0.9 copy-start.6
  106.1 14.7 %copy-start.14 = (f32[2,1280]{1,0:T(2,128)S(1)}, f32[2,1280]{1,0:T(2,128)}, u32[]{:S(2)}) copy-start(f32[2,1280]{1,0:T(2,128)} %param.23) | copy-start | bytes 30724
  106.1 18.5 %collective-permute-start.11 = (bf16[640,640]{1,0:T(8,128)(2,1)}, bf16[640,640]{1,0:T(8,128)(2,1)}, u32[]{:S(2)}, u32[]{:S(2)}) collective-permute-start(bf16[640,640]{1,0:T(8,128)(2,1)} %ffn.4), channel_id=1, source_target_pairs={{0,128},{1,33},{2,130},{3,35},{4,132},{5,37},{6,134},{7,39},{8,136... | collective-permute-start | bytes 2457608 | tf_op jit(solution)/shard_map/ppermute | solution.py:411
  118.1 13.0 %collective-permute-start.13 = (bf16[640,640]{1,0:T(8,128)(2,1)}, bf16[640,640]{1,0:T(8,128)(2,1)S(1)}, u32[]{:S(2)}, u32[]{:S(2)}) collective-permute-start(bf16[640,640]{1,0:T(8,128)(2,1)} %get-tuple-element.30), channel_id=1, source_target_pairs={{0,64},{1,17},{2,66},{3,19},{4,68},{5,21},{6,70},{7,23},{8,72},{9,... | collective-permute-start | bytes 2457608 | tf_op jit(solution)/shard_map/ppermute | solution.py:413
  118.9 12.2 %collective-permute-start.12 = (bf16[640,640]{1,0:T(8,128)(2,1)}, bf16[640,640]{1,0:T(8,128)(2,1)}, u32[]{:S(2)}, u32[]{:S(2)}) collective-permute-start(bf16[640,640]{1,0:T(8,128)(2,1)} %get-tuple-element.29), channel_id=1, source_target_pairs={{0,192},{1,49},{2,194},{3,51},{4,196},{5,53},{6,198},{7,55},{8,200... | collective-permute-start | bytes 2457608 | tf_op jit(solution)/shard_map/ppermute | solution.py:412
  122.6 1.9 %copy-start.7 = (bf16[640,640]{1,0:T(8,128)(2,1)S(1)}, bf16[640,640]{1,0:T(8,128)(2,1)}, u32[]{:S(2)}) copy-start(bf16[640,640]{1,0:T(8,128)(2,1)} %copy-done.6) | copy-start | bytes 2457604
  133.5 13.0 %copy-start.15 = (f32[1,4,64]{2,1,0:T(4,128)S(1)}, f32[1,4,64]{2,1,0:T(4,128)}, u32[]{:S(2)}) copy-start(f32[1,4,64]{2,1,0:T(4,128)} %param.15) | copy-start | bytes 3076
  133.5 36.4 %copy-start.4 = (f32[256,1280]{1,0:T(8,128)S(1)}, f32[256,1280]{1,0:T(8,128)}, u32[]{:S(2)}) copy-start(f32[256,1280]{1,0:T(8,128)} %copy-done.3) | copy-start | bytes 3932164
  133.5 36.4 %all-to-all-start.1 = ((bf16[16,40,640]{2,1,0:T(8,128)(2,1)}), bf16[16,40,640]{2,1,0:T(8,128)(2,1)S(1)}, u32[]{:S(2)}, u32[]{:S(2)}) async-start(bf16[16,40,640]{2,1,0:T(8,128)(2,1)} %bitcast.8), calls=%async_computation.1 | async-start | bytes 1638400 | tf_op jit(solution)/shard_map/all_to_all | solution.py:398

commit v3 on v2

v3 whole, which is shorter than its diff:
```python
import functools
import jax
import jax.numpy as jnp
import numpy as np
from jax import lax
from jax.experimental import pallas as pl
from jax.experimental.pallas import tpu as pltpu
from jax.sharding import PartitionSpec as P

SIDE = 4
AXES = ("seq", "exp")
VMEM = pl.BlockSpec(memory_space=pltpu.VMEM)
ANY = pl.BlockSpec(memory_space=pl.ANY)
HBM = pl.BlockSpec(memory_space=pltpu.HBM)
MIX_COST = 60000


def ring(shift, weights, exp_size):
    pairs = []
    for y in range(SIDE):
        for x in range(SIDE):
            for e in range(exp_size):
                along_x = (e % 2 == 0) == weights
                to_y = y if along_x else (y + shift) % SIDE
                to_x = (x + shift) % SIDE if along_x else x
                pairs.append(((y * SIDE + x) * exp_size + e, (to_y * SIDE + to_x) * exp_size + e))
    return pairs


def weight_groups(exp_size):
    groups = []
    for e in range(exp_size):
        for a in range(SIDE):
            if e % 2 == 0:
                groups.append([(a * SIDE + b) * exp_size + e for b in range(SIDE)])
            else:
                groups.append([(b * SIDE + a) * exp_size + e for b in range(SIDE)])
    return groups


def chunk_sizes(slots):
    second = (slots * 3 // 5) // 2 * 2
    return slots - second, second


def unpack_table(holders, slots):
    pick = np.zeros((2, 2 * holders * slots, 4 * holders * slots), np.float32)
    chunks = chunk_sizes(slots)
    for half in range(2):
        row = 0
        for j in range(2):
            for k, n in enumerate(chunks):
                for s in range(holders):
                    for c in range(n):
                        slot = c + k * chunks[0]
                        pick[half, row, s * 4 * slots + half * 2 * slots + j * slots + slot] = 1.0
                        row += 1
    return pick.astype(jnp.bfloat16)


def pack_table(holders, n):
    place = np.zeros((2, 4 * holders * n, 2 * holders * n), np.float32)
    for half in range(2):
        for j in range(2):
            for s in range(holders):
                for c in range(n):
                    row = (j * holders + s) * n + c
                    place[half, s * 4 * n + half * 2 * n + j * n + c, row] = 1.0
    return place.astype(jnp.bfloat16)


def normalize(values, scales):
    row_mean = jnp.mean(values, axis=-1, keepdims=True)
    centred = values - row_mean
    row_var = jnp.mean(centred * centred, axis=-1, keepdims=True)
    return centred * lax.rsqrt(row_var + 1e-06) * scales


def gelu(v):
    return 0.5 * v * (1.0 + lax.erf(v * 0.7071067811865476))


def mix_kernel(
    holders,
    slots,
    tok_ref,
    up_ref,
    down_ref,
    ids_ref,
    mixer_gain,
    expert_gain,
    conv_weight,
    conv_bias,
    mixed_ref,
    msg_ref,
    column_ref,
    norm_v,
    in_v,
    mixed_v,
    msg_v,
    sems,
):
    rows, cols, width = tok_ref.shape
    tokens = rows * cols
    gain = mixer_gain[...].reshape(1, width)
    out_gain = expert_gain[...].reshape(1, width)
    shift = conv_bias[...].reshape(1, width)
    for r in range(rows):
        norm_v[r + 1] = normalize(tok_ref[r].astype(jnp.float32), gain).astype(jnp.bfloat16)
    norm_v[0] = normalize(up_ref[0].astype(jnp.float32), gain).astype(jnp.bfloat16)
    norm_v[rows + 1] = normalize(down_ref[0].astype(jnp.float32), gain).astype(jnp.bfloat16)
    place = lax.broadcasted_iota(jnp.int32, (cols, 1), 0)
    copies = []
    for r in range(rows):
        sums = []
        for b in range(3):
            total = None
            for a in range(3):
                term = norm_v[r + a].astype(jnp.float32) * conv_weight[a, b : b + 1]
                total = term if total is None else total + term
            sums.append(total)
        left = jnp.where(place == 0, 0.0, pltpu.roll(sums[0], 1, 0))
        right = jnp.where(place == cols - 1, 0.0, pltpu.roll(sums[2], cols - 1, 0))
        mixed = tok_ref[r].astype(jnp.float32) + shift + sums[1] + left + right
        at = pl.ds(r * cols, cols)
        mixed_v[at] = mixed
        in_v[at] = normalize(mixed, out_gain).astype(jnp.bfloat16)
    copies.append(pltpu.make_async_copy(mixed_v, mixed_ref, sems.at[0]))
    copies[0].start()
    ids = ids_ref[...]
    experts = 2 * holders
    kinds = lax.broadcasted_iota(jnp.int32, (experts, tokens), 0)
    hot = kinds == ids
    before = lax.broadcasted_iota(jnp.int32, (tokens, tokens), 0) < lax.broadcasted_iota(
        jnp.int32, (tokens, tokens), 1
    )
    earlier = jnp.dot(
        hot.astype(jnp.float32).astype(jnp.bfloat16),
        before.astype(jnp.float32).astype(jnp.bfloat16),
        preferred_element_type=jnp.float32,
    )
    rank = jnp.sum(jnp.where(hot, earlier, 0.0), axis=0, keepdims=True).astype(jnp.int32)
    holder = lax.shift_right_logical(ids, 1)
    which = ids & 1
    col = holder * (4 * slots) + which * slots + rank
    low = 0
    for k, n in enumerate(chunk_sizes(slots)):
        place_of = holder * (4 * n) + which * n + rank - low
        column_ref[k : k + 1] = jnp.where((rank >= low) & (rank < low + n), place_of, -4 * n)
        low += n
    at = lax.broadcasted_iota(jnp.int32, (4 * slots * holders, tokens), 0)
    pick_left = (at == col).astype(jnp.float32).astype(jnp.bfloat16)
    pick_right = (at == col + 2 * slots).astype(jnp.float32).astype(jnp.bfloat16)
    msg_v[...] = (
        jnp.dot(pick_left, in_v[:, : width // 2], preferred_element_type=jnp.float32)
        + jnp.dot(pick_right, in_v[:, width // 2 :], preferred_element_type=jnp.float32)
    ).astype(jnp.bfloat16)
    copies.append(pltpu.make_async_copy(msg_v, msg_ref, sems.at[1]))
    copies[1].start()
    for copy in copies:
        copy.wait()


def mix(holders, slots, tokens, up, down, ids, mixer_gain, expert_gain, conv_weight, conv_bias):
    rows, cols, width = tokens.shape
    size = rows * cols * width
    message = (4 * slots * holders, width // 2)
    return pl.pallas_call(
        functools.partial(mix_kernel, holders, slots),
        out_shape=[
            jax.ShapeDtypeStruct((rows * cols, width), jnp.float32),
            jax.ShapeDtypeStruct(message, jnp.bfloat16),
            jax.ShapeDtypeStruct((2, rows * cols), jnp.int32),
        ],
        in_specs=[VMEM] * 8,
        out_specs=[HBM, HBM, VMEM],
        scratch_shapes=[
            pltpu.VMEM((rows + 2, cols, width), jnp.bfloat16),
            pltpu.VMEM((rows * cols, width), jnp.bfloat16),
            pltpu.VMEM((rows * cols, width), jnp.float32),
            pltpu.VMEM(message, jnp.bfloat16),
            pltpu.SemaphoreType.DMA((2,)),
        ],
        compiler_params=pltpu.CompilerParams(vmem_limit_bytes=16 * 1024 * 1024),
        cost_estimate=pl.CostEstimate(flops=MIX_COST * size, transcendentals=0, bytes_accessed=6 * size),
        name="mix",
    )(tokens, up, down, ids, mixer_gain, expert_gain, conv_weight, conv_bias)


def ffn_kernel(*refs):
    msgs, wis, wos = refs[0:4], refs[4:8], refs[8:12]
    bias, pick, place_first, place_second = refs[12:16]
    outs, refs = (refs[16:20], refs[20:24]), refs[24:]
    r_v, x_v, wi_v, wo_v, y_first, y_second, o_first, o_second, msg_sem, w_sem, out_sem = refs
    experts, total, width = x_v.shape
    rows = total // SIDE
    units = wos[0].shape[1]
    half = width // 2
    places, ys, os = (place_first, place_second), (y_first, y_second), (o_first, o_second)
    sizes = [y.shape[1] // experts for y in ys]
    msg_copies = []
    for k in range(SIDE):
        copy = pltpu.make_async_copy(msgs[k], r_v.at[k], msg_sem.at[k])
        copy.start()
        msg_copies.append(copy)
    w_copies = {}
    for j in range(experts):
        for what, (sources, target) in enumerate(((wis, wi_v), (wos, wo_v))):
            group = []
            for k in range(SIDE):
                copy = pltpu.make_async_copy(
                    sources[k].at[j], target.at[j, pl.ds(k * units, units)], w_sem.at[j, what, k]
                )
                copy.start()
                group.append(copy)
            w_copies[j, what] = group
    for k in range(SIDE):
        msg_copies[k].wait()
        for side in range(2):
            found = jnp.dot(pick[side], r_v[k], preferred_element_type=jnp.float32).astype(
                jnp.bfloat16
            )
            row = 0
            for j in range(experts):
                base = 0
                for size in sizes:
                    x_v[
                        j,
                        base + k * size : base + (k + 1) * size,
                        side * half : (side + 1) * half,
                    ] = found[row : row + size]
                    row += size
                    base += SIDE * size
    for j in range(experts):
        for copy in w_copies[j, 0]:
            copy.wait()
        base = 0
        for c, size in enumerate(sizes):
            at = slice(base, base + SIDE * size)
            base += SIDE * size
            hidden = lax.dot_general(
                x_v[j, at], wi_v[j], (((1,), (1,)), ((), ())), preferred_element_type=jnp.float32
            )
            hidden = gelu(hidden + bias[j : j + 1]).astype(jnp.bfloat16)
            if c == 0:
                for copy in w_copies[j, 1]:
                    copy.wait()
            part = jnp.dot(hidden, wo_v[j], preferred_element_type=jnp.float32)
            part = part.astype(jnp.bfloat16)
            for k in range(SIDE):
                ys[c][k, j * size : (j + 1) * size] = part[k * size : (k + 1) * size]
            if j == experts - 1:
                for k in range(SIDE):
                    os[c][k] = (
                        jnp.dot(places[c][0], ys[c][k, :, :half], preferred_element_type=jnp.float32)
                        + jnp.dot(
                            places[c][1], ys[c][k, :, half:], preferred_element_type=jnp.float32
                        )
                    ).astype(jnp.bfloat16)
                    copy = pltpu.make_async_copy(os[c].at[k], outs[c][k], out_sem.at[c, k])
                    copy.start()
    for c in range(2):
        for k in range(SIDE):
            pltpu.make_async_copy(os[c].at[k], outs[c][k], out_sem.at[c, k]).wait()


def ffn(msgs, wis, wos, bias, pick, places):
    experts, units, width = wos[0].shape
    rows = pick.shape[1] // experts
    total = SIDE * rows
    shapes = [(place.shape[1], width // 2) for place in places]
    flops = 4 * experts * total * SIDE * units * width
    moved = 2 * experts * width * (4 * total + 2 * SIDE * units)
    outs = pl.pallas_call(
        ffn_kernel,
        out_shape=[
            jax.ShapeDtypeStruct(shape, jnp.bfloat16) for shape in shapes for _ in range(SIDE)
        ],
        in_specs=[ANY] * 12 + [VMEM] * 4,
        out_specs=[ANY] * (2 * SIDE),
        scratch_shapes=[
            pltpu.VMEM((SIDE,) + msgs[0].shape, jnp.bfloat16),
            pltpu.VMEM((experts, total, width), jnp.bfloat16),
            pltpu.VMEM((experts, SIDE * units, width), jnp.bfloat16),
            pltpu.VMEM((experts, SIDE * units, width), jnp.bfloat16),
            pltpu.VMEM((SIDE, places[0].shape[2], width), jnp.bfloat16),
            pltpu.VMEM((SIDE, places[1].shape[2], width), jnp.bfloat16),
            pltpu.VMEM((SIDE,) + shapes[0], jnp.bfloat16),
            pltpu.VMEM((SIDE,) + shapes[1], jnp.bfloat16),
            pltpu.SemaphoreType.DMA((SIDE,)),
            pltpu.SemaphoreType.DMA((experts, 2, SIDE)),
            pltpu.SemaphoreType.DMA((2, SIDE)),
        ],
        compiler_params=pltpu.CompilerParams(vmem_limit_bytes=40 * 1024 * 1024),
        cost_estimate=pl.CostEstimate(flops=2 * flops, transcendentals=0, bytes_accessed=moved),
        name="ffn",
    )(*msgs, *wis, *wos, bias, pick, *places)
    return outs[:SIDE], outs[SIDE:]


def combine_kernel(mixed_ref, gate_ref, col_ref, first_ref, second_ref, out_ref):
    tokens, width = mixed_ref.shape
    gate = gate_ref[...]
    for side in range(2):
        at = slice(side * width // 2, (side + 1) * width // 2)
        total = None
        for k, ref in enumerate((first_ref, second_ref)):
            count = ref.shape[0]
            step = 2 * (count // 64) * side
            col = col_ref[:, k : k + 1] + step
            pick = lax.broadcasted_iota(jnp.int32, (tokens, count), 1) == col
            term = jnp.dot(
                pick.astype(jnp.float32).astype(jnp.bfloat16),
                ref[...],
                preferred_element_type=jnp.float32,
            )
            total = term if total is None else total + term
        out_ref[:, at] = (mixed_ref[:, at] + gate * total).astype(jnp.bfloat16)


def combine(mixed, gate, columns, first, second):
    return pl.pallas_call(
        combine_kernel,
        out_shape=jax.ShapeDtypeStruct(mixed.shape, jnp.bfloat16),
        in_specs=[VMEM] * 5,
        out_specs=VMEM,
        compiler_params=pltpu.CompilerParams(vmem_limit_bytes=16 * 1024 * 1024),
        name="combine",
    )(mixed, gate, columns, first, second)


def body(
    tokens,
    expert_ids,
    gate_values,
    mixer_gain,
    expert_gain,
    conv_weight,
    conv_bias,
    w_in,
    b_in,
    w_out,
    b_out,
):
    exp_size = lax.axis_size("exp")
    seq_size = lax.axis_size("seq")
    send_w = functools.partial(ring, weights=True, exp_size=exp_size)
    send_t = functools.partial(ring, weights=False, exp_size=exp_size)
    _, row_count, col_count, width = tokens.shape
    tok_rows = row_count * col_count
    per_device = w_in.shape[0]
    slots = 5 * tok_rows // (4 * per_device * exp_size)

    together = lax.optimization_barrier
    head, tail = tokens[0, 0:1], tokens[0, row_count - 1 : row_count]
    wi, wo = jnp.swapaxes(w_in, 1, 2), w_out
    up = lax.ppermute(tail, "seq", [(i, i + 1) for i in range(seq_size - 1)])
    down = lax.ppermute(head, "seq", [(i + 1, i) for i in range(seq_size - 1)])
    wi_prev = lax.ppermute(wi, AXES, send_w(1))
    wi_next = lax.ppermute(wi, AXES, send_w(-1))
    wo_prev = lax.ppermute(wo, AXES, send_w(1))
    wo_next = lax.ppermute(wo, AXES, send_w(-1))
    mixed, msg, columns = mix(
        exp_size,
        slots,
        tokens[0],
        up,
        down,
        expert_ids.reshape(1, tok_rows),
        mixer_gain,
        expert_gain,
        conv_weight,
        conv_bias,
    )

    def exchange(msg):
        shape = msg.shape
        msg = msg.reshape(exp_size, shape[0] // exp_size, shape[1])
        return lax.all_to_all(msg, "exp", split_axis=0, concat_axis=0, tiled=True).reshape(shape)

    def returned(parts, n):
        own, far, prev, nxt = parts
        far = lax.ppermute(far, AXES, send_t(2))
        prev = lax.ppermute(prev, AXES, send_t(-1))
        nxt = lax.ppermute(nxt, AXES, send_t(1))
        shift = jnp.transpose(b_out.reshape(per_device, 2, width // 2), (1, 0, 2))
        shift = jnp.broadcast_to(shift[None, :, :, None], (exp_size, 2, per_device, n, width // 2))
        total = sum(part.astype(jnp.float32) for part in (own, far, prev, nxt))
        return (total + shift.reshape(total.shape)).astype(jnp.bfloat16)

    msg = exchange(msg)
    msg_far = lax.ppermute(msg, AXES, send_t(2))
    msg_prev = lax.ppermute(msg, AXES, send_t(1))
    msg_next = lax.ppermute(msg, AXES, send_t(-1))
    wi_on, wo_on, bias_in, _ = together((wi_prev, wo_next, b_in, msg))
    wi_far = lax.ppermute(wi_on, AXES, send_w(1))
    wo_far = lax.ppermute(wo_on, AXES, send_w(-1))
    biases = lax.all_gather(bias_in, AXES, axis_index_groups=weight_groups(exp_size))
    seq = lax.axis_index("seq")
    place = jnp.where(lax.axis_index("exp") % 2 == 0, seq % SIDE, seq // SIDE)
    bias = jnp.concatenate(
        [
            sum(jnp.where((place + shift) % SIDE == k, biases[k], 0.0) for k in range(SIDE))
            for shift in (0, SIDE - 1, 1, 2)
        ],
        axis=1,
    )
    sizes = chunk_sizes(slots)
    first, second = ffn(
        (msg, msg_far, msg_prev, msg_next),
        (wi, wi_prev, wi_next, wi_far),
        (wo, wo_prev, wo_next, wo_far),
        bias,
        unpack_table(exp_size, slots),
        [pack_table(exp_size, n) for n in sizes],
    )
    first = exchange(returned(first, sizes[0]))
    second, first = together((returned(second, sizes[1]), first))
    second = exchange(second)
    result = combine(mixed, gate_values.reshape(tok_rows, 1), columns.T, first, second)
    return result.reshape(tokens.shape)


def solution(mesh):
    in_specs = (
        P(("dp", "exp"), "seq", None, None),
        P(("dp", "exp"), "seq", None, None),
        P(("dp", "exp"), "seq", None),
        P(),
        P(),
        P(),
        P(),
        P("exp", None, "seq"),
        P("exp", "seq"),
        P("exp", "seq", None),
        P("exp", None),
    )
    out_specs = P(("dp", "exp"), "seq", None, None)
    return jax.shard_map(body, mesh=mesh, in_specs=in_specs, out_specs=out_specs, check_vma=False)
```

time: 172 us -> 185 us (1.076)
  blocking collectives: 0 us -> 40 us
  waiting for transfers between devices: 71.1 us -> 44 us
  Pallas kernels: 36.6 us -> 25.1 us
  local copies, waits for them, and re-layouts: 14.8 us -> 20.9 us
  other arithmetic: 3.03 us -> 6.34 us
    all_gather x0 -> x1, blocking collectives: none -> 40 us  [body(): lax.all_gather(bias_in, AXES, axis_index_groups=weight_groups(exp_size))]
    ppermute x1, waiting for transfers between devices: 25.8 us -> 0.01 us  [body(): wo_next = lax.ppermute(wo, AXES, send_w(-1))]
    pallas_call x5 -> x1, Pallas kernels: 30.4 us -> 19.1 us  [ffn(): pl.pallas_call(ffn_kernel, out_shape=[jax.ShapeDtypeStruct(shape, jnp.bfl...]
    unnamed x35, local copies, waits for them, and re-layouts: 9.02 us -> 12.7 us
    ppermute x1, starting transfers between devices: 1.69 us -> 4.35 us  [body(): wi_prev = lax.ppermute(wi, AXES, send_w(1))]
    ppermute x5 -> x8, waiting for transfers between devices: 5.14 us -> 2.54 us  [the longest x2 1.57 us: returned(): nxt = lax.ppermute(nxt, AXES, send_t(1))]
    convert_element_type x1 -> x2, other arithmetic: 2.37 us -> 4.97 us  [returned(): return (total + shift.reshape(total.shape)).astype(jnp.bfloat16)]
    all_to_all x2 -> x3, starting transfers between devices: 21.7 us -> 19.1 us  [exchange(): lax.all_to_all(msg, 'exp', split_axis=0, concat_axis=0, tiled=True)]
  transfers between devices with their start and end apart: 16 -> 20, of which waited for: 5 -> 5; matrix products, arithmetic and copies ran while one was open for 3% -> 8% of each run, Pallas kernels for 20% -> 2%
where the time goes in v3:
time: 185 us; the launch traced here: 184 us
  starting transfers between devices  47.5 us (26%)
  waiting for transfers between devices  44 us (24%)
  blocking collectives  40 us (22%)
  Pallas kernels  25.1 us (14%)
  local copies, waits for them, and re-layouts  20.9 us (11%)
  other arithmetic  6.34 us (3%)
    all_to_all x3, waiting for transfers between devices, exchange(): lax.all_to_all(msg, 'exp', split_axis=0, concat_axis=0, tiled=True)  41.5 us
    all_gather x1, blocking collectives, body(): lax.all_gather(bias_in, AXES, axis_index_groups=weight_groups(exp_size))  40 us
    all_to_all x3, starting transfers between devices, exchange(): lax.all_to_all(msg, 'exp', split_axis=0, concat_axis=0, tiled=True)  19.1 us
    pallas_call x1, Pallas kernels, ffn(): pl.pallas_call(ffn_kernel, out_shape=[jax.ShapeDtypeStruct(shape, jnp.bfl...  19.1 us
    unnamed x35, local copies, waits for them, and re-layouts  12.7 us
    convert_element_type x2, other arithmetic, returned(): return (total + shift.reshape(total.shape)).astype(jnp.bfloat16)  4.97 us
    reshape x2, local copies, waits for them, and re-layouts, returned(): return (total + shift.reshape(total.shape)).astype(jnp.bfloat16)  4.54 us
    pallas_call x1, Pallas kernels, mix(): pl.pallas_call(functools.partial(mix_kernel, holders, slots), out_shape=[...  4.39 us
  transfers between devices with their start and end apart: 20, of which 5 were waited for; matrix products, arithmetic and copies ran while one was open for 8% of the time, Pallas kernels for 2%

profile of v3, /device:TPU:1, one launch (start us, length us, event | category | flops | bytes accessed | tf_op | source)
XLA Modules:
  0.0 184.1 jit_solution(13871851049968698655)
XLA Ops:
  0.0 1.0 slice_bitcast_fusion
  1.0 4.0 %collective-permute-start = (bf16[1,64,1280]{2,1,0:T(8,128)(2,1)S(1)}, bf16[1,64,1280]{2,1,0:T(8,128)(2,1)S(1)}, u32[]{:S(2)}, u32[]{:S(2)}) collective-permute-start(bf16[1,64,1280]{2,1,0:T(8,128)(2,1)S(1)} %get-tuple-element.38), channel_id=1, source_target_pairs={{0,16},{16,32},{32,48},{48,64},{64,80},{80,96},{96,112},{112,128},... | collective-permute-start | bytes 491528 | tf_op jit(solution)/shard_map/ppermute | solution.py:357
  5.0 1.3 collective-permute-start.1
  6.3 4.3 %collective-permute-start.5 = (bf16[2,320,1280]{2,1,0:T(8,128)(2,1)}, bf16[2,320,1280]{2,1,0:T(8,128)(2,1)}, u32[]{:S(2)}, u32[]{:S(2)}) collective-permute-start(bf16[2,320,1280]{2,1,0:T(8,128)(2,1)} %bitcast.41), channel_id=1, source_target_pairs={{0,16},{1,65},{2,18},{3,67},{4,20},{5,69},{6,22},{7,71},{8,24},{9,... | collective-permute-start | bytes 4915208 | tf_op jit(solution)/shard_map/ppermute | solution.py:359
  10.6 1.5 collective-permute-start.7
  12.2 0.5 broadcast.178
  12.7 1.3 reduce.3
  14.0 0.1 reshape.98.ids_ref
  14.1 0.0 collective-permute-done.up_ref
  14.1 1.1 copy-done
  15.2 0.8 copy-done.7
  16.0 0.7 copy-done.8
  16.7 0.7 copy-done.9
  17.4 0.7 copy-done.10
  18.1 4.4 %mix.1 = (f32[256,1280]{1,0:T(8,128)S(1)}, bf16[640,640]{1,0:T(8,128)(2,1)}, s32[2,256]{1,0:T(2,128)S(1)}) custom-call(bf16[4,64,1280]{2,1,0:T(8,128)(2,1)S(1)} %bitcast.40, bf16[1,64,1280]{2,1,0:T(8,128)(2,1)S(1)} %collective-permute-done.up_ref, bf16[1,64,1280]{2,1,0:T(8,128)(2,1)S(1)} %collective-permute-done.1.down_ref, s32[1,256]{1,0:T(1,128)S(1)} %reshape.98.ids_ref, ...), custom_call_target="tpu_custom_call" | custom-call | flops 19660800000 | bytes 1966080 | tf_op jit(solution)/shard_map/mix/pallas_call | solution.py:168
  22.5 0.0 copy-start.15
  22.5 8.6 %all-to-all-start = ((bf16[16,40,640]{2,1,0:T(8,128)(2,1)}), bf16[16,40,640]{2,1,0:T(8,128)(2,1)S(1)}, u32[]{:S(2)}, u32[]{:S(2)}) async-start(bf16[16,40,640]{2,1,0:T(8,128)(2,1)} %bitcast.4), calls=%async_computation | async-start | bytes 1638400 | tf_op jit(solution)/shard_map/all_to_all | solution.py:379
  31.1 4.3 %collective-permute-start.6 = (bf16[2,320,1280]{2,1,0:T(8,128)(2,1)}, bf16[2,320,1280]{2,1,0:T(8,128)(2,1)}, u32[]{:S(2)}, u32[]{:S(2)}) collective-permute-start(bf16[2,320,1280]{2,1,0:T(8,128)(2,1)} %bitcast.42), channel_id=1, source_target_pairs={{0,48},{1,193},{2,50},{3,195},{4,52},{5,197},{6,54},{7,199},{8,56}... | collective-permute-start | bytes 4915208 | tf_op jit(solution)/shard_map/ppermute | solution.py:360
  35.4 19.0 %all-to-all-done = bf16[16,40,640]{2,1,0:T(8,128)(2,1)S(1)} async-done(((bf16[16,40,640]{2,1,0:T(8,128)(2,1)}), bf16[16,40,640]{2,1,0:T(8,128)(2,1)S(1)}, u32[]{:S(2)}, u32[]{:S(2)}) %all-to-all-start) | async-done | bytes 819232 | tf_op jit(solution)/shard_map/all_to_all | solution.py:379
  54.5 4.3 %collective-permute-start.10 = (bf16[2,320,1280]{2,1,0:T(8,128)(2,1)}, bf16[2,320,1280]{2,1,0:T(8,128)(2,1)}, u32[]{:S(2)}, u32[]{:S(2)}) collective-permute-start(bf16[2,320,1280]{2,1,0:T(8,128)(2,1)} %collective-permute-done.7.refs_10_), channel_id=1, source_target_pairs={{0,48},{1,193},{2,50},{3,195},{4,52},{5,197},{6,54},{7,199},{8,56}... | collective-permute-start | bytes 4915208 | tf_op jit(solution)/shard_map/ppermute | solution.py:397
  58.7 0.0 collective-permute-start.8
  58.7 0.2 collective-permute-start.2
  58.9 1.5 collective-permute-start.3
  60.5 1.1 collective-permute-start.4
  61.6 40.0 %all-gather.1 = f32[4,2,320]{2,1,0:T(2,128)S(1)} all-gather(f32[1,2,320]{2,1,0:T(2,128)S(1)} %bitcast.46), channel_id=2, replica_groups={{0,16,32,48},{64,80,96,112},{128,144,160,176},{192,208,224,240},{1,65,1..., dimensions={0}, use_global_device_ids=true | all-gather | bytes 12800 | tf_op jit(solution)/shard_map/all_gather | solution.py:398
  101.7 0.0 copy-start.14
  101.7 0.1 concatenate.3.refs_12_
  101.8 0.9 copy-done.2
  102.7 0.0 collective-permute-done.4.refs_3_
  102.7 0.0 collective-permute-done.10.refs_11_
  102.7 0.0 copy-start.1
  102.7 1.4 copy-done.1
  104.2 1.1 copy-done.3
  105.3 1.1 copy-done.11
  106.5 1.0 copy-done.12
  107.5 0.9 copy-done.13
  108.4 19.1 %ffn.1 = (bf16[256,640]{1,0:T(8,128)(2,1)S(1)}, bf16[256,640]{1,0:T(8,128)(2,1)}, bf16[256,640]{1,0:T(8,128)(2,1)}, bf16[256,640]{1,0:T(8,128)(2,1)}, bf16[384,6...) custom-call(bf16[640,640]{1,0:T(8,128)(2,1)S(1)} %bitcast.38, ...), custom_call_target="tpu_custom_call" | custom-call | flops 16777216000 | bytes 26214400 | tf_op jit(solution)/shard_map/ffn/pallas_call | solution.py:274
  127.5 0.8 copy-done.4
  128.3 0.8 copy-done.6
  129.1 0.8 collective-permute-start.14
  129.9 0.3 collective-permute-start.15
  130.1 1.2 collective-permute-start.16
  131.4 0.9 broadcast_in_dim.33
  132.3 2.2 %reshape.104 = f32[256,640]{1,0:T(8,128)} reshape(f32[16,2,2,4,640]{4,3,2,1,0:T(4,128)} %broadcast_in_dim.33) | data formatting | bytes 1310720 | tf_op jit(solution)/shard_map/reshape | solution.py:389
  134.4 2.2 %collective-permute-start.11 = (bf16[384,640]{1,0:T(8,128)(2,1)}, bf16[384,640]{1,0:T(8,128)(2,1)}, u32[]{:S(2)}, u32[]{:S(2)}) collective-permute-start(bf16[384,640]{1,0:T(8,128)(2,1)} %copy-done.6), channel_id=1, source_target_pairs={{0,128},{1,33},{2,130},{3,35},{4,132},{5,37},{6,134},{7,39},{8,136... | collective-permute-start | bytes 1474568 | tf_op jit(solution)/shard_map/ppermute | solution.py:383
  136.6 0.8 collective-permute-start.12
  137.4 0.0 collective-permute-done.14
  137.4 0.7 collective-permute-start.13
  138.1 1.0 collective-permute-done.15
  139.0 1.6 collective-permute-done.16
  140.6 2.2 %add_convert_fusion.1 = bf16[256,640]{1,0:T(8,128)(2,1)} fusion(f32[256,640]{1,0:T(8,128)} %reshape.104, bf16[256,640]{1,0:T(8,128)(2,1)} %collective-permute-done.16, bf16[256,640]{1,0:T(8,128)(2,1)} %collective-permute-done.15, bf16[256,640]{1,0:T(8,128)(2,1)S(1)} %collective-permute-done.14, bf16[256,640]{1,0:T(8,128)(2,1)S(1)} %get-tuple-element.31), kind=kLoop, calls=%fused_computation.1 | loop fusion | flops 1474560 | bytes 2293760 | tf_op jit(solution)/shard_map/convert_element_type | solution.py:389
  142.8 7.0 %all-to-all-start.1 = ((bf16[16,16,640]{2,1,0:T(8,128)(2,1)}), bf16[16,16,640]{2,1,0:T(8,128)(2,1)S(1)}, u32[]{:S(2)}, u32[]{:S(2)}) async-start(bf16[16,16,640]{2,1,0:T(8,128)(2,1)} %bitcast.44), calls=%async_computation.1 | async-start | bytes 655360 | tf_op jit(solution)/shard_map/all_to_all | solution.py:379
  149.9 1.2 broadcast_in_dim.32
  151.1 2.4 %reshape.103 = f32[384,640]{1,0:T(8,128)} reshape(f32[16,2,2,6,640]{4,3,2,1,0:T(8,128)} %broadcast_in_dim.32) | data formatting | bytes 1966080 | tf_op jit(solution)/shard_map/reshape | solution.py:389
  153.5 0.0 collective-permute-done.11
  153.5 0.0 collective-permute-done.12
  153.5 0.0 copy-start.16
  153.5 2.7 %add_convert_fusion = bf16[384,640]{1,0:T(8,128)(2,1)} fusion(f32[384,640]{1,0:T(8,128)} %reshape.103, bf16[384,640]{1,0:T(8,128)(2,1)} %collective-permute-done.13, bf16[384,640]{1,0:T(8,128)(2,1)} %collective-permute-done.12, bf16[384,640]{1,0:T(8,128)(2,1)} %collective-permute-done.11, bf16[384,640]{1,0:T(8,128)(2,1)S(1)} %get-tuple-element.27), kind=kLoop, calls=%fused_computation | loop fusion | flops 2211840 | bytes 3440640 | tf_op jit(solution)/shard_map/convert_element_type | solution.py:389
  156.3 6.7 %all-to-all-done.1 = bf16[16,16,640]{2,1,0:T(8,128)(2,1)S(1)} async-done(((bf16[16,16,640]{2,1,0:T(8,128)(2,1)}), bf16[16,16,640]{2,1,0:T(8,128)(2,1)S(1)}, u32[]{:S(2)}, u32[]{:S(2)}) %all-to-all-start.1) | async-done | bytes 327712 | tf_op jit(solution)/shard_map/all_to_all | solution.py:379
  163.0 3.5 %all-to-all-start.2 = ((bf16[16,24,640]{2,1,0:T(8,128)(2,1)}), bf16[16,24,640]{2,1,0:T(8,128)(2,1)S(1)}, u32[]{:S(2)}, u32[]{:S(2)}) async-start(bf16[16,24,640]{2,1,0:T(8,128)(2,1)} %bitcast.19), calls=%async_computation.2 | async-start | bytes 983040 | tf_op jit(solution)/shard_map/all_to_all | solution.py:379
  166.4 0.1 reshape.241.gate_ref
  166.6 0.1 copy.22
  166.7 15.7 %all-to-all-done.2 = bf16[16,24,640]{2,1,0:T(8,128)(2,1)S(1)} async-done(((bf16[16,24,640]{2,1,0:T(8,128)(2,1)}), bf16[16,24,640]{2,1,0:T(8,128)(2,1)S(1)}, u32[]{:S(2)}, u32[]{:S(2)}) %all-to-all-start.2) | async-done | bytes 491552 | tf_op jit(solution)/shard_map/all_to_all | solution.py:379
  182.5 1.7 combine.1
  (31 shorter events, 0.1 us)
Async XLA Ops:
  1.0 13.1 %collective-permute-start = (bf16[1,64,1280]{2,1,0:T(8,128)(2,1)S(1)}, bf16[1,64,1280]{2,1,0:T(8,128)(2,1)S(1)}, u32[]{:S(2)}, u32[]{:S(2)}) collective-permute-start(bf16[1,64,1280]{2,1,0:T(8,128)(2,1)S(1)} %get-tuple-element.38), channel_id=1, source_target_pairs={{0,16},{16,32},{32,48},{48,64},{64,80},{80,96},{96,112},{112,128},... | collective-permute-start | bytes 491528 | tf_op jit(solution)/shard_map/ppermute | solution.py:357
  5.0 9.1 %collective-permute-start.1 = (bf16[1,64,1280]{2,1,0:T(8,128)(2,1)S(1)}, bf16[1,64,1280]{2,1,0:T(8,128)(2,1)S(1)}, u32[]{:S(2)}, u32[]{:S(2)}) collective-permute-start(bf16[1,64,1280]{2,1,0:T(8,128)(2,1)S(1)} %get-tuple-element.37), channel_id=1, source_target_pairs={{16,0},{32,16},{48,32},{64,48},{80,64},{96,80},{112,96},{128,112},... | collective-permute-start | bytes 491528 | tf_op jit(solution)/shard_map/ppermute | solution.py:358
  6.3 29.1 %collective-permute-start.5 = (bf16[2,320,1280]{2,1,0:T(8,128)(2,1)}, bf16[2,320,1280]{2,1,0:T(8,128)(2,1)}, u32[]{:S(2)}, u32[]{:S(2)}) collective-permute-start(bf16[2,320,1280]{2,1,0:T(8,128)(2,1)} %bitcast.41), channel_id=1, source_target_pairs={{0,16},{1,65},{2,18},{3,67},{4,20},{5,69},{6,22},{7,71},{8,24},{9,... | collective-permute-start | bytes 4915208 | tf_op jit(solution)/shard_map/ppermute | solution.py:359
  10.6 24.8 %collective-permute-start.7 = (bf16[2,320,1280]{2,1,0:T(8,128)(2,1)}, bf16[2,320,1280]{2,1,0:T(8,128)(2,1)}, u32[]{:S(2)}, u32[]{:S(2)}) collective-permute-start(bf16[2,320,1280]{2,1,0:T(8,128)(2,1)} %refs_8_.1), channel_id=1, source_target_pairs={{0,48},{1,193},{2,50},{3,195},{4,52},{5,197},{6,54},{7,199},{8,56}... | collective-permute-start | bytes 4915208 | tf_op jit(solution)/shard_map/ppermute | solution.py:362
  14.1 1.1 copy-start
  15.2 0.8 copy-start.7
  16.0 0.7 copy-start.8
  16.7 0.7 copy-start.9
  17.4 0.7 copy-start.10
  22.5 39.1 %copy-start.15 = (f32[2,320]{1,0:T(2,128)S(1)}, f32[2,320]{1,0:T(2,128)}, u32[]{:S(2)}) copy-start(f32[2,320]{1,0:T(2,128)} %param.22) | copy-start | bytes 7684
  22.5 31.9 %all-to-all-start = ((bf16[16,40,640]{2,1,0:T(8,128)(2,1)}), bf16[16,40,640]{2,1,0:T(8,128)(2,1)S(1)}, u32[]{:S(2)}, u32[]{:S(2)}) async-start(bf16[16,40,640]{2,1,0:T(8,128)(2,1)} %bitcast.4), calls=%async_computation | async-start | bytes 1638400 | tf_op jit(solution)/shard_map/all_to_all | solution.py:379
  31.1 27.8 %collective-permute-start.6 = (bf16[2,320,1280]{2,1,0:T(8,128)(2,1)}, bf16[2,320,1280]{2,1,0:T(8,128)(2,1)}, u32[]{:S(2)}, u32[]{:S(2)}) collective-permute-start(bf16[2,320,1280]{2,1,0:T(8,128)(2,1)} %bitcast.42), channel_id=1, source_target_pairs={{0,48},{1,193},{2,50},{3,195},{4,52},{5,197},{6,54},{7,199},{8,56}... | collective-permute-start | bytes 4915208 | tf_op jit(solution)/shard_map/ppermute | solution.py:360
  35.4 25.1 %collective-permute-start.9 = (bf16[2,320,1280]{2,1,0:T(8,128)(2,1)}, bf16[2,320,1280]{2,1,0:T(8,128)(2,1)}, u32[]{:S(2)}, u32[]{:S(2)}) collective-permute-start(bf16[2,320,1280]{2,1,0:T(8,128)(2,1)} %refs_8_.1), channel_id=1, source_target_pairs={{0,16},{1,65},{2,18},{3,67},{4,20},{5,69},{6,22},{7,71},{8,24},{9,... | collective-permute-start | bytes 4915208 | tf_op jit(solution)/shard_map/ppermute | solution.py:361
  54.5 48.3 %collective-permute-start.10 = (bf16[2,320,1280]{2,1,0:T(8,128)(2,1)}, bf16[2,320,1280]{2,1,0:T(8,128)(2,1)}, u32[]{:S(2)}, u32[]{:S(2)}) collective-permute-start(bf16[2,320,1280]{2,1,0:T(8,128)(2,1)} %collective-permute-done.7.refs_10_), channel_id=1, source_target_pairs={{0,48},{1,193},{2,50},{3,195},{4,52},{5,197},{6,54},{7,199},{8,56}... | collective-permute-start | bytes 4915208 | tf_op jit(solution)/shard_map/ppermute | solution.py:397
  58.7 44.0 %collective-permute-start.8 = (bf16[2,320,1280]{2,1,0:T(8,128)(2,1)}, bf16[2,320,1280]{2,1,0:T(8,128)(2,1)}, u32[]{:S(2)}, u32[]{:S(2)}) collective-permute-start(bf16[2,320,1280]{2,1,0:T(8,128)(2,1)} %collective-permute-done.5.refs_5_), channel_id=1, source_target_pairs={{0,16},{1,65},{2,18},{3,67},{4,20},{5,69},{6,22},{7,71},{8,24},{9,... | collective-permute-start | bytes 4915208 | tf_op jit(solution)/shard_map/ppermute | solution.py:396
  58.7 43.1 %collective-permute-start.2 = (bf16[640,640]{1,0:T(8,128)(2,1)S(1)}, bf16[640,640]{1,0:T(8,128)(2,1)S(1)}, u32[]{:S(2)}, u32[]{:S(2)}) collective-permute-start(bf16[640,640]{1,0:T(8,128)(2,1)S(1)} %bitcast.35), channel_id=1, source_target_pairs={{0,128},{1,33},{2,130},{3,35},{4,132},{5,37},{6,134},{7,39},{8,136... | collective-permute-start | bytes 2457608 | tf_op jit(solution)/shard_map/ppermute | solution.py:392
  58.9 43.8 %collective-permute-start.3 = (bf16[640,640]{1,0:T(8,128)(2,1)S(1)}, bf16[640,640]{1,0:T(8,128)(2,1)}, u32[]{:S(2)}, u32[]{:S(2)}) collective-permute-start(bf16[640,640]{1,0:T(8,128)(2,1)S(1)} %bitcast.36), channel_id=1, source_target_pairs={{0,64},{1,17},{2,66},{3,19},{4,68},{5,21},{6,70},{7,23},{8,72},{9,... | collective-permute-start | bytes 2457608 | tf_op jit(solution)/shard_map/ppermute | solution.py:393
  60.5 42.3 %collective-permute-start.4 = (bf16[640,640]{1,0:T(8,128)(2,1)S(1)}, bf16[640,640]{1,0:T(8,128)(2,1)}, u32[]{:S(2)}, u32[]{:S(2)}) collective-permute-start(bf16[640,640]{1,0:T(8,128)(2,1)S(1)} %bitcast.37), channel_id=1, source_target_pairs={{0,192},{1,49},{2,194},{3,51},{4,196},{5,53},{6,198},{7,55},{8,200... | collective-permute-start | bytes 2457608 | tf_op jit(solution)/shard_map/ppermute | solution.py:394
  101.7 29.7 %copy-start.14 = (f32[2,1280]{1,0:T(2,128)S(1)}, f32[2,1280]{1,0:T(2,128)}, u32[]{:S(2)}) copy-start(f32[2,1280]{1,0:T(2,128)} %param.24) | copy-start | bytes 30724
  101.8 0.9 copy-start.2
  102.7 1.4 copy-start.1
  104.2 1.1 copy-start.3
  105.3 1.1 copy-start.11
  106.5 1.0 copy-start.12
  107.5 0.9 copy-start.13
  127.5 0.8 copy-start.4
  128.3 0.8 copy-start.6
  129.1 7.6 %copy-start.5 = (bf16[384,640]{1,0:T(8,128)(2,1)S(1)}, bf16[384,640]{1,0:T(8,128)(2,1)}, u32[]{:S(2)}) copy-start(bf16[384,640]{1,0:T(8,128)(2,1)} %copy-done.4) | copy-start | bytes 1474564
  129.1 8.3 %collective-permute-start.14 = (bf16[256,640]{1,0:T(8,128)(2,1)}, bf16[256,640]{1,0:T(8,128)(2,1)S(1)}, u32[]{:S(2)}, u32[]{:S(2)}) collective-permute-start(bf16[256,640]{1,0:T(8,128)(2,1)} %get-tuple-element.32), channel_id=1, source_target_pairs={{0,128},{1,33},{2,130},{3,35},{4,132},{5,37},{6,134},{7,39},{8,136... | collective-permute-start | bytes 983048 | tf_op jit(solution)/shard_map/ppermute | solution.py:383
  129.9 9.2 %collective-permute-start.15 = (bf16[256,640]{1,0:T(8,128)(2,1)}, bf16[256,640]{1,0:T(8,128)(2,1)}, u32[]{:S(2)}, u32[]{:S(2)}) collective-permute-start(bf16[256,640]{1,0:T(8,128)(2,1)} %get-tuple-element.33), channel_id=1, source_target_pairs={{0,192},{1,49},{2,194},{3,51},{4,196},{5,53},{6,198},{7,55},{8,200... | collective-permute-start | bytes 983048 | tf_op jit(solution)/shard_map/ppermute | solution.py:384
  130.1 10.5 %collective-permute-start.16 = (bf16[256,640]{1,0:T(8,128)(2,1)}, bf16[256,640]{1,0:T(8,128)(2,1)}, u32[]{:S(2)}, u32[]{:S(2)}) collective-permute-start(bf16[256,640]{1,0:T(8,128)(2,1)} %get-tuple-element.34), channel_id=1, source_target_pairs={{0,64},{1,17},{2,66},{3,19},{4,68},{5,21},{6,70},{7,23},{8,72},{9,... | collective-permute-start | bytes 983048 | tf_op jit(solution)/shard_map/ppermute | solution.py:385
  134.4 19.1 %collective-permute-start.11 = (bf16[384,640]{1,0:T(8,128)(2,1)}, bf16[384,640]{1,0:T(8,128)(2,1)}, u32[]{:S(2)}, u32[]{:S(2)}) collective-permute-start(bf16[384,640]{1,0:T(8,128)(2,1)} %copy-done.6), channel_id=1, source_target_pairs={{0,128},{1,33},{2,130},{3,35},{4,132},{5,37},{6,134},{7,39},{8,136... | collective-permute-start | bytes 1474568 | tf_op jit(solution)/shard_map/ppermute | solution.py:383
  136.6 16.9 %collective-permute-start.12 = (bf16[384,640]{1,0:T(8,128)(2,1)S(1)}, bf16[384,640]{1,0:T(8,128)(2,1)}, u32[]{:S(2)}, u32[]{:S(2)}) collective-permute-start(bf16[384,640]{1,0:T(8,128)(2,1)S(1)} %copy-done.5), channel_id=1, source_target_pairs={{0,192},{1,49},{2,194},{3,51},{4,196},{5,53},{6,198},{7,55},{8,200... | collective-permute-start | bytes 1474568 | tf_op jit(solution)/shard_map/ppermute | solution.py:384
  137.4 16.1 %collective-permute-start.13 = (bf16[384,640]{1,0:T(8,128)(2,1)S(1)}, bf16[384,640]{1,0:T(8,128)(2,1)}, u32[]{:S(2)}, u32[]{:S(2)}) collective-permute-start(bf16[384,640]{1,0:T(8,128)(2,1)S(1)} %get-tuple-element.30), channel_id=1, source_target_pairs={{0,64},{1,17},{2,66},{3,19},{4,68},{5,21},{6,70},{7,23},{8,72},{9,... | collective-permute-start | bytes 1474568 | tf_op jit(solution)/shard_map/ppermute | solution.py:385
  142.8 20.1 %all-to-all-start.1 = ((bf16[16,16,640]{2,1,0:T(8,128)(2,1)}), bf16[16,16,640]{2,1,0:T(8,128)(2,1)S(1)}, u32[]{:S(2)}, u32[]{:S(2)}) async-start(bf16[16,16,640]{2,1,0:T(8,128)(2,1)} %bitcast.44), calls=%async_computation.1 | async-start | bytes 655360 | tf_op jit(solution)/shard_map/all_to_all | solution.py:379
  153.5 12.9 %copy-start.16 = (f32[1,4,64]{2,1,0:T(4,128)S(1)}, f32[1,4,64]{2,1,0:T(4,128)}, u32[]{:S(2)}) copy-start(f32[1,4,64]{2,1,0:T(4,128)} %param.16) | copy-start | bytes 3076
  163.0 19.5 %all-to-all-start.2 = ((bf16[16,24,640]{2,1,0:T(8,128)(2,1)}), bf16[16,24,640]{2,1,0:T(8,128)(2,1)S(1)}, u32[]{:S(2)}, u32[]{:S(2)}) async-start(bf16[16,24,640]{2,1,0:T(8,128)(2,1)} %bitcast.19), calls=%async_computation.2 | async-start | bytes 983040 | tf_op jit(solution)/shard_map/all_to_all | solution.py:379

commit v4 on v2

--- a/solution.py
+++ b/solution.py
@@ -14,7 +14,8 @@
 HBM = pl.BlockSpec(memory_space=pltpu.HBM)
 PIECES = 3
 MIX_COST = 60000
-ADD_COST = 16000
+FFN_COST = 2
+ADD_COST = 64000
 EXTRA = 16
 
 
@@ -194,127 +195,159 @@
     )(tokens, up, down, ids, mixer_gain, expert_gain, conv_weight, conv_bias)
 
 
-def ffn_kernel(count, *refs):
-    wis, wos, refs = refs[0:4], refs[4:8], refs[8:]
-    pick, place, refs = refs[0], refs[1], refs[2:]
-    msgs, outs, refs = refs[:count], refs[count : 2 * count], refs[2 * count :]
-    r_v, x_v, wi_v, wo_v, b_v, y_v, o_v, msg_sem, w_sem, b_sem, out_sem = refs
-    experts, _, width = x_v.shape
-    rows = pick.shape[1] // experts
+def unpack_kernel(msg_ref, pick, *outs):
+    rows, width = outs[0].shape
+    half = width // 2
+    for side in range(2):
+        found = jnp.dot(pick[side], msg_ref[...], preferred_element_type=jnp.float32)
+        for j, out_ref in enumerate(outs):
+            out_ref[:, side * half : (side + 1) * half] = found[
+                j * rows : (j + 1) * rows
+            ].astype(jnp.bfloat16)
+
+
+def unpack(msg, pick):
+    rows = pick.shape[1] // 2
+    return pl.pallas_call(
+        unpack_kernel,
+        out_shape=[jax.ShapeDtypeStruct((rows, 2 * msg.shape[1]), jnp.bfloat16)] * 2,
+        in_specs=[VMEM] * 2,
+        out_specs=[VMEM] * 2,
+        compiler_params=pltpu.CompilerParams(vmem_limit_bytes=16 * 1024 * 1024),
+        name="unpack",
+    )(msg, pick)
+
+
+def ffn_kernel(expert, *refs):
+    xs, wis, wos, outs = refs[0:4], refs[4:8], refs[8:12], refs[12:16]
+    x_v, wi_v, wo_v, b_v, y_v, x_sem, w_sem, out_sem = refs[16:]
+    rows = xs[0].shape[0]
     units = wos[0].shape[1]
-    half = width // 2
-    msg_copies = []
-    for k in range(count):
-        copy = pltpu.make_async_copy(msgs[k], r_v.at[k], msg_sem.at[k])
+    first, second = [], []
+    for k in range(SIDE):
+        at = expert if k < SIDE - 1 else 0
+        first.append(
+            pltpu.make_async_copy(xs[k], x_v.at[pl.ds(k * rows, rows)], x_sem.at[k])
+        )
+        first.append(
+            pltpu.make_async_copy(
+                wis[k].at[at, pl.ds(0, units)], wi_v.at[pl.ds(k * units, units)], w_sem.at[0, k]
+            )
+        )
+        first.append(
+            pltpu.make_async_copy(
+                wis[k].at[at, pl.ds(units, EXTRA)], b_v.at[k], w_sem.at[2, k]
+            )
+        )
+        second.append(
+            pltpu.make_async_copy(
+                wos[k].at[at], wo_v.at[pl.ds(k * units, units)], w_sem.at[1, k]
+            )
+        )
+    for copy in first + second:
         copy.start()
-        msg_copies.append(copy)
-    w_copies = {}
-    for j in range(experts):
-        for what, (sources, target) in enumerate(((wis, wi_v), (wos, wo_v))):
-            group = []
-            for k in range(SIDE):
-                copy = pltpu.make_async_copy(
-                    sources[k].at[j, pl.ds(0, units)],
-                    target.at[j, pl.ds(k * units, units)],
-                    w_sem.at[j, what, k],
-                )
-                copy.start()
-                group.append(copy)
-                if what == 0:
-                    copy = pltpu.make_async_copy(
-                        wis[k].at[j, pl.ds(units, EXTRA)], b_v.at[j, k], b_sem.at[j, k]
-                    )
-                    copy.start()
-                    group.append(copy)
-            w_copies[j, what] = group
-    for k in range(count):
-        msg_copies[k].wait()
-        for side in range(2):
-            rows_of = jnp.dot(pick[side], r_v[k], preferred_element_type=jnp.float32).astype(
-                jnp.bfloat16
-            )
-            for j in range(experts):
-                x_v[j, k * rows : (k + 1) * rows, side * half : (side + 1) * half] = rows_of[
-                    j * rows : (j + 1) * rows
-                ]
-    for j in range(experts):
-        for copy in w_copies[j, 0]:
-            copy.wait()
-        hidden = lax.dot_general(
-            x_v[j], wi_v[j], (((1,), (1,)), ((), ())), preferred_element_type=jnp.float32
-        )
-        bias = sum(
-            jnp.sum(
-                b_v[j, k].astype(jnp.float32)[PIECES * k : PIECES * (k + 1)], axis=0, keepdims=True
-            )
-            for k in range(SIDE)
-        )
-        hidden = gelu(hidden + bias).astype(jnp.bfloat16)
-        for copy in w_copies[j, 1]:
-            copy.wait()
-        part = jnp.dot(hidden, wo_v[j], preferred_element_type=jnp.float32).astype(jnp.bfloat16)
-        for k in range(count):
-            y_v[k, j * rows : (j + 1) * rows] = part[k * rows : (k + 1) * rows]
+    for copy in first:
+        copy.wait()
+    bias = sum(
+        jnp.sum(b_v[k].astype(jnp.float32)[PIECES * k : PIECES * (k + 1)], axis=0, keepdims=True)
+        for k in range(SIDE)
+    )
+    top, low = slice(0, 2 * rows), slice(2 * rows, 4 * rows)
+    nt = (((1,), (1,)), ((), ()))
+    first_hidden = lax.dot_general(
+        x_v[top], wi_v[...], nt, preferred_element_type=jnp.float32
+    )
+    for copy in second:
+        copy.wait()
+    next_hidden = lax.dot_general(x_v[low], wi_v[...], nt, preferred_element_type=jnp.float32)
+    first_hidden = gelu(first_hidden + bias).astype(jnp.bfloat16)
+    part = jnp.dot(first_hidden, wo_v[...], preferred_element_type=jnp.float32)
+    next_hidden = gelu(next_hidden + bias).astype(jnp.bfloat16)
+    next_part = jnp.dot(next_hidden, wo_v[...], preferred_element_type=jnp.float32)
+    y_v[top] = part.astype(jnp.bfloat16)
+    y_v[low] = next_part.astype(jnp.bfloat16)
     out_copies = []
-    for k in range(count):
-        o_v[k] = (
-            jnp.dot(place[0], y_v[k, :, :half], preferred_element_type=jnp.float32)
-            + jnp.dot(place[1], y_v[k, :, half:], preferred_element_type=jnp.float32)
-        ).astype(jnp.bfloat16)
-        copy = pltpu.make_async_copy(o_v.at[k], outs[k], out_sem.at[k])
+    for k in range(SIDE):
+        copy = pltpu.make_async_copy(y_v.at[pl.ds(k * rows, rows)], outs[k], out_sem.at[k])
         copy.start()
         out_copies.append(copy)
     for copy in out_copies:
         copy.wait()
 
 
-def ffn(msgs, wis, wos, pick, place):
-    experts, units, width = wos[0].shape
-    count = len(msgs)
-    rows = pick.shape[1] // experts
-    total = count * rows
-    flops = 4 * experts * total * SIDE * units * width
-    moved = 2 * experts * width * (4 * total + 2 * SIDE * units)
-    return pl.pallas_call(
-        functools.partial(ffn_kernel, count),
-        out_shape=[jax.ShapeDtypeStruct(msgs[0].shape, jnp.bfloat16)] * count,
-        in_specs=[ANY] * 8 + [VMEM] * 2 + [ANY] * count,
-        out_specs=[ANY] * count,
+def ffn(expert, xs, wis, wos):
+    rows, width = xs[0].shape
+    units = wos[0].shape[1]
+    flops = 4 * SIDE * rows * SIDE * units * width
+    moved = 2 * width * (2 * SIDE * rows + 2 * SIDE * units)
+    return pl.pallas_call(
+        functools.partial(ffn_kernel, expert),
+        out_shape=[jax.ShapeDtypeStruct((rows, width), jnp.bfloat16)] * SIDE,
+        in_specs=[ANY] * 12,
+        out_specs=[ANY] * SIDE,
         scratch_shapes=[
-            pltpu.VMEM((count,) + msgs[0].shape, jnp.bfloat16),
-            pltpu.VMEM((experts, total, width), jnp.bfloat16),
-            pltpu.VMEM((experts, SIDE * units, width), jnp.bfloat16),
-            pltpu.VMEM((experts, SIDE * units, width), jnp.bfloat16),
-            pltpu.VMEM((experts, SIDE, EXTRA, width), jnp.bfloat16),
-            pltpu.VMEM((count, experts * rows, width), jnp.bfloat16),
-            pltpu.VMEM((count,) + msgs[0].shape, jnp.bfloat16),
-            pltpu.SemaphoreType.DMA((count,)),
-            pltpu.SemaphoreType.DMA((experts, 2, SIDE)),
-            pltpu.SemaphoreType.DMA((experts, SIDE)),
-            pltpu.SemaphoreType.DMA((count,)),
+            pltpu.VMEM((SIDE * rows, width), jnp.bfloat16),
+            pltpu.VMEM((SIDE * units, width), jnp.bfloat16),
+            pltpu.VMEM((SIDE * units, width), jnp.bfloat16),
+            pltpu.VMEM((SIDE, EXTRA, width), jnp.bfloat16),
+            pltpu.VMEM((SIDE * rows, width), jnp.bfloat16),
+            pltpu.SemaphoreType.DMA((SIDE,)),
+            pltpu.SemaphoreType.DMA((3, SIDE)),
+            pltpu.SemaphoreType.DMA((SIDE,)),
         ],
-        compiler_params=pltpu.CompilerParams(vmem_limit_bytes=32 * 1024 * 1024),
-        cost_estimate=pl.CostEstimate(flops=2 * flops, transcendentals=0, bytes_accessed=moved),
+        compiler_params=pltpu.CompilerParams(vmem_limit_bytes=20 * 1024 * 1024),
+        cost_estimate=pl.CostEstimate(
+            flops=FFN_COST * flops, transcendentals=0, bytes_accessed=moved
+        ),
         name="ffn",
-    )(*wis, *wos, pick, place, *msgs)
-
-
-def add_kernel(a_ref, b_ref, c_ref, out_ref):
-    out_ref[...] = a_ref[...].astype(jnp.float32) + b_ref[...].astype(jnp.float32) + c_ref[...]
-
-
-def add_parts(a, b, c):
+    )(*xs, *wis, *wos)
+
+
+def add_kernel(bias, *refs):
+    parts, out_ref = refs[:-1], refs[-1]
+    total = sum(part[...].astype(jnp.float32) for part in parts)
+    out_ref[...] = (total + bias[0:1]).astype(jnp.bfloat16)
+
+
+def add_parts(bias, parts):
+    size = parts[0].size
     return pl.pallas_call(
         add_kernel,
-        out_shape=jax.ShapeDtypeStruct(a.shape, jnp.float32),
-        in_specs=[VMEM] * 3,
+        out_shape=jax.ShapeDtypeStruct(parts[0].shape, jnp.bfloat16),
+        in_specs=[VMEM] * (1 + len(parts)),
         out_specs=VMEM,
+        compiler_params=pltpu.CompilerParams(vmem_limit_bytes=8 * 1024 * 1024),
         cost_estimate=pl.CostEstimate(
-            flops=ADD_COST * a.size, transcendentals=0, bytes_accessed=12 * a.size
+            flops=ADD_COST * size, transcendentals=0, bytes_accessed=10 * size
         ),
+        name="add_parts",
+    )(bias, *parts)
+
+
+def pack_kernel(place, bias, done_ref, *refs):
+    parts, out_ref, sum_v = refs[:-2], refs[-2], refs[-1]
+    rows, width = parts[0].shape
+    half = width // 2
+    total = sum(part[...].astype(jnp.float32) for part in parts)
+    sum_v[...] = (total + bias[1:2]).astype(jnp.bfloat16)
+    out_ref[...] = sum(
+        jnp.dot(place[side, :, low : low + rows], ref[:, at], preferred_element_type=jnp.float32)
+        for side, at in enumerate((slice(0, half), slice(half, width)))
+        for low, ref in ((0, done_ref), (rows, sum_v))
+    ).astype(jnp.bfloat16)
+
+
+def pack(place, bias, done, parts):
+    rows, width = parts[0].shape
+    return pl.pallas_call(
+        pack_kernel,
+        out_shape=jax.ShapeDtypeStruct((place.shape[1], width // 2), jnp.bfloat16),
+        in_specs=[VMEM] * (3 + len(parts)),
+        out_specs=VMEM,
+        scratch_shapes=[pltpu.VMEM((rows, width), jnp.bfloat16)],
         compiler_params=pltpu.CompilerParams(vmem_limit_bytes=16 * 1024 * 1024),
-        name="add_parts",
-    )(a, b, c)
+        name="pack",
+    )(place, bias, done, *parts)
 
 
 def combine_kernel(mixed_ref, gate_ref, col_ref, msg_ref, out_ref):
@@ -370,15 +403,13 @@
     together = lax.optimization_barrier
     head, tail = tokens[0, 0:1], tokens[0, row_count - 1 : row_count]
     wi = append_rows(jnp.swapaxes(w_in, 1, 2), b_in)
-    head, tail, wo = together((head, tail, w_out))
+    wo = w_out
     up = lax.ppermute(tail, "seq", [(i, i + 1) for i in range(seq_size - 1)])
     down = lax.ppermute(head, "seq", [(i + 1, i) for i in range(seq_size - 1)])
     wo_prev = lax.ppermute(wo, AXES, send_w(1))
     wo_next = lax.ppermute(wo, AXES, send_w(-1))
     wi_prev = lax.ppermute(wi, AXES, send_w(1))
     wi_next = lax.ppermute(wi, AXES, send_w(-1))
-    wo_far = lax.ppermute(wo_prev, AXES, send_w(1))
-    wi_far = lax.ppermute(wi_next, AXES, send_w(-1))
     mixed, msg, columns = mix(
         exp_size,
         slots,
@@ -391,30 +422,44 @@
         conv_weight,
         conv_bias,
     )
+    columns, wo_on, wi_on, *_ = together((columns, wo_prev, wi_next, wo_next, wi_prev))
+    wo_far_0 = lax.ppermute(wo_on[0:1], AXES, send_w(1))
+    wi_far_0 = lax.ppermute(wi_on[0:1], AXES, send_w(-1))
 
     def exchange(msg):
         shape = msg.shape
         msg = msg.reshape(exp_size, shape[0] // exp_size, shape[1])
         return lax.all_to_all(msg, "exp", split_axis=0, concat_axis=0, tiled=True).reshape(shape)
 
-    msg = exchange(msg)
-    msg_far = lax.ppermute(msg, AXES, send_t(2))
-    msg_prev = lax.ppermute(msg, AXES, send_t(1))
-    msg_next = lax.ppermute(msg, AXES, send_t(-1))
-    weights = ((wi, wi_prev, wi_next, wi_far), (wo, wo_prev, wo_next, wo_far))
-    lists = tables(exp_size, slots)
-    (own,) = ffn((msg,), *weights, *lists)
-    msg_far, own = together((msg_far, own))
-    (far,) = ffn((msg_far,), *weights, *lists)
-    msg_prev, msg_next, far = together((msg_prev, msg_next, far))
-    prev, nxt = ffn((msg_prev, msg_next), *weights, *lists)
-    far = lax.ppermute(far, AXES, send_t(2))
-    prev = lax.ppermute(prev, AXES, send_t(-1))
-    nxt = lax.ppermute(nxt, AXES, send_t(1))
-    shift = jnp.transpose(b_out.reshape(per_device, 2, width // 2), (1, 0, 2))
-    shift = jnp.broadcast_to(shift[None, :, :, None], (exp_size, 2, per_device, slots, width // 2))
-    early = add_parts(own, far, shift.reshape(own.shape))
-    back = (early + prev.astype(jnp.float32) + nxt.astype(jnp.float32)).astype(jnp.bfloat16)
+    def spread(rows, forward):
+        prev = lax.ppermute(rows, AXES, send_t(1))
+        nxt = lax.ppermute(rows, AXES, send_t(-1))
+        far = lax.ppermute(prev if forward else rows, AXES, send_t(1 if forward else 2))
+        return far, prev, nxt, rows
+
+    def returned(parts):
+        far, prev, nxt, own = parts
+        return (
+            own,
+            lax.ppermute(far, AXES, send_t(2)),
+            lax.ppermute(prev, AXES, send_t(-1)),
+            lax.ppermute(nxt, AXES, send_t(1)),
+        )
+
+    pick, place = tables(exp_size, slots)
+    rows_0, rows_1 = unpack(exchange(msg), pick)
+    rows_0 = spread(rows_0, True)
+    rows_1, rows_0, wo_on, wi_on = together((rows_1, rows_0, wo_on, wi_on))
+    wo_far_1 = lax.ppermute(wo_on[1:2], AXES, send_w(1))
+    wi_far_1 = lax.ppermute(wi_on[1:2], AXES, send_w(-1))
+    weights_0 = ((wi, wi_prev, wi_next, wi_far_0), (wo, wo_prev, wo_next, wo_far_0))
+    weights_1 = ((wi, wi_prev, wi_next, wi_far_1), (wo, wo_prev, wo_next, wo_far_1))
+    rows_1 = spread(rows_1, False)
+    parts_0 = ffn(0, rows_0, *weights_0)
+    rows_1, _ = together((rows_1, parts_0[0]))
+    parts_1 = ffn(1, rows_1, *weights_1)
+    early = add_parts(b_out, returned(parts_0))
+    back = pack(place, b_out, early, returned(parts_1))
     back = exchange(back)
     result = combine(mixed, gate_values.reshape(tok_rows, 1), columns.reshape(tok_rows, 1), back)
     return result.reshape(tokens.shape)

time: 172 us -> 167 us (0.971)
  blocking collectives: 0 us -> 32.2 us
  waiting for transfers between devices: 71.1 us -> 59 us
  Pallas kernels: 36.6 us -> 27 us
  starting transfers between devices: 45.8 us -> 38 us
  local copies, waits for them, and re-layouts: 14.8 us -> 9.43 us
  other arithmetic: 3.03 us -> 0.59 us
    all_to_all x0 -> x1, blocking collectives: none -> 32.2 us  [exchange(): lax.all_to_all(msg, 'exp', split_axis=0, concat_axis=0, tiled=True)]
    ppermute x8 -> x16, waiting for transfers between devices: 5.15 us -> 35.9 us  [the longest x2 9.35 us: spread(): nxt = lax.ppermute(rows, AXES, send_t(-1))]
    ppermute x1, waiting for transfers between devices: 25.8 us -> 0.01 us  [body(): wo_next = lax.ppermute(wo, AXES, send_w(-1))]
    all_to_all x2 -> x1, waiting for transfers between devices: 40.1 us -> 23.1 us  [exchange(): lax.all_to_all(msg, 'exp', split_axis=0, concat_axis=0, tiled=True)]
    all_to_all x2 -> x1, starting transfers between devices: 21.7 us -> 6.03 us  [exchange(): lax.all_to_all(msg, 'exp', split_axis=0, concat_axis=0, tiled=True)]
    pallas_call x4 -> x5, Pallas kernels: 30 us -> 20.4 us  [the longest x2 17.1 us: ffn(): pl.pallas_call(functools.partial(ffn_kernel, expert), out_shape=[jax.Shap...]
    ppermute x8 -> x16, starting transfers between devices: 11.4 us -> 19.3 us  [the longest x2 5.09 us: spread(): nxt = lax.ppermute(rows, AXES, send_t(-1))]
    unnamed x35 -> x31, local copies, waits for them, and re-layouts: 9.02 us -> 4.83 us
  transfers between devices with their start and end apart: 16 -> 23, of which waited for: 5 -> 9; matrix products, arithmetic and copies ran while one was open for 3% -> 2% of each run, Pallas kernels for 20% -> 14%
where the time goes in v4:
time: 167 us; the launch traced here: 166 us
  waiting for transfers between devices  59 us (35%)
  starting transfers between devices  38 us (23%)
  blocking collectives  32.2 us (19%)
  Pallas kernels  27 us (16%)
  local copies, waits for them, and re-layouts  9.43 us (6%)
    all_to_all x1, blocking collectives, exchange(): lax.all_to_all(msg, 'exp', split_axis=0, concat_axis=0, tiled=True)  32.2 us
    all_to_all x1, waiting for transfers between devices, exchange(): lax.all_to_all(msg, 'exp', split_axis=0, concat_axis=0, tiled=True)  23.1 us
    pallas_call x2, Pallas kernels, ffn(): pl.pallas_call(functools.partial(ffn_kernel, expert), out_shape=[jax.Shap...  17.1 us
    ppermute x2, waiting for transfers between devices, spread(): nxt = lax.ppermute(rows, AXES, send_t(-1))  9.35 us
    ppermute x2, waiting for transfers between devices, returned(): lax.ppermute(far, AXES, send_t(2))  6.81 us
    all_to_all x1, starting transfers between devices, exchange(): lax.all_to_all(msg, 'exp', split_axis=0, concat_axis=0, tiled=True)  6.03 us
    ppermute x1, waiting for transfers between devices, body(): wo_far_1 = lax.ppermute(wo_on[1:2], AXES, send_w(1))  5.31 us
    ppermute x2, waiting for transfers between devices, spread(): lax.ppermute(prev if forward else rows, AXES, send_t(1 if forward else 2))  5.15 us
  transfers between devices with their start and end apart: 23, of which 9 were waited for; matrix products, arithmetic and copies ran while one was open for 2% of the time, Pallas kernels for 14%

profile of v4, /device:TPU:1, one launch (start us, length us, event | category | flops | bytes accessed | tf_op | source)
XLA Modules:
  0.0 166.4 jit_solution(656492854685476785)
XLA Ops:
  0.0 1.7 %slice_bitcast_fusion = (bf16[1,64,1280]{2,1,0:T(8,128)(2,1)}, bf16[1,64,1280]{2,1,0:T(8,128)(2,1)}) fusion(bf16[1,4,64,1280]{3,2,1,0:T(8,128)(2,1)} %param.13), kind=kLoop, calls=%fused_computation | loop fusion | bytes 655360 | tf_op jit(solution)/shard_map/squeeze | solution.py:404
  1.7 4.6 %collective-permute-start = (bf16[1,64,1280]{2,1,0:T(8,128)(2,1)}, bf16[1,64,1280]{2,1,0:T(8,128)(2,1)}, u32[]{:S(2)}, u32[]{:S(2)}) collective-permute-start(bf16[1,64,1280]{2,1,0:T(8,128)(2,1)} %get-tuple-element.60), channel_id=1, source_target_pairs={{0,16},{16,32},{32,48},{48,64},{64,80},{80,96},{96,112},{112,128},... | collective-permute-start | bytes 491528 | tf_op jit(solution)/shard_map/ppermute | solution.py:407
  6.3 1.3 collective-permute-start.1
  7.6 3.7 %collective-permute-start.2 = (bf16[2,320,1280]{2,1,0:T(8,128)(2,1)}, bf16[2,320,1280]{2,1,0:T(8,128)(2,1)}, u32[]{:S(2)}, u32[]{:S(2)}) collective-permute-start(bf16[2,320,1280]{2,1,0:T(8,128)(2,1)} %refs_8_.3), channel_id=1, source_target_pairs={{0,16},{1,65},{2,18},{3,67},{4,20},{5,69},{6,22},{7,71},{8,24},{9,... | collective-permute-start | bytes 4915208 | tf_op jit(solution)/shard_map/ppermute | solution.py:409
  11.3 1.5 collective-permute-start.4
  12.9 1.4 copy-done
  14.3 0.7 copy-done.7
  15.0 0.0 copy-start.12
  15.0 0.4 append_rows.1.refs_4_
  15.4 1.4 collective-permute-start.3
  16.8 0.5 broadcast.3
  17.4 0.6 reduce.3
  17.9 0.1 reshape.24.ids_ref
  18.0 0.0 collective-permute-done.up_ref
  18.0 0.1 collective-permute-start.5
  18.1 0.0 collective-permute-done.1.down_ref
  18.2 0.0 copy-start.5
  18.2 1.1 copy-done.5
  19.3 4.6 %mix.1 = (f32[256,1280]{1,0:T(8,128)S(1)}, bf16[640,640]{1,0:T(8,128)(2,1)S(1)}, s32[1,256]{1,0:T(1,128)S(1)}) custom-call(bf16[4,64,1280]{2,1,0:T(8,128)(2,1)S(1)} %bitcast.17, bf16[1,64,1280]{2,1,0:T(8,128)(2,1)} %collective-permute-done.up_ref, bf16[1,64,1280]{2,1,0:T(8,128)(2,1)} %collective-permute-done.1.down_ref, s32[1,256]{1,0:T(1,128)S(1)} %reshape.24.ids_ref, ...), custom_call_target="tpu_custom_call" | custom-call | flops 19660800000 | bytes 1966080 | tf_op jit(solution)/shard_map/mix/pallas_call | solution.py:176
  23.8 1.1 copy-done.1
  24.9 32.2 %all_to_all.10 = bf16[16,40,640]{2,1,0:T(8,128)(2,1)S(1)} all-to-all(bf16[16,40,640]{2,1,0:T(8,128)(2,1)S(1)} %bitcast.16), channel_id=1, replica_groups=mesh['seq'=16,'exp'=16,'dp'=1] {'exp'}, dimensions={0} | all-to-all | bytes 1638400 | tf_op jit(solution)/shard_map/all_to_all | solution.py:432
  57.1 0.9 unpack.1
  58.0 0.7 collective-permute-start.6
  58.7 0.0 collective-permute-done.2.refs_9_
  58.7 0.0 collective-permute-done.4.refs_10_
  58.7 0.0 collective-permute-done.3.refs_6_
  58.7 0.1 slice.20
  58.7 4.3 %collective-permute-start.9 = (bf16[1,336,1280]{2,1,0:T(8,128)(2,1)S(1)}, bf16[1,336,1280]{2,1,0:T(8,128)(2,1)S(1)}, u32[]{:S(2)}, u32[]{:S(2)}) collective-permute-start(bf16[1,336,1280]{2,1,0:T(8,128)(2,1)S(1)} %slice.20), channel_id=1, source_target_pairs={{0,48},{1,193},{2,50},{3,195},{4,52},{5,197},{6,54},{7,199},{8,56}... | collective-permute-start | bytes 2580488 | tf_op jit(solution)/shard_map/ppermute | solution.py:427
  63.1 1.2 slice.21
  64.3 0.1 collective-permute-start.10
  64.4 2.7 %collective-permute-start.8 = (bf16[160,1280]{1,0:T(8,128)(2,1)S(1)}, bf16[160,1280]{1,0:T(8,128)(2,1)S(1)}, u32[]{:S(2)}, u32[]{:S(2)}) collective-permute-start(bf16[160,1280]{1,0:T(8,128)(2,1)S(1)} %get-tuple-element.43.refs_3_), channel_id=1, source_target_pairs={{0,192},{1,49},{2,194},{3,51},{4,196},{5,53},{6,198},{7,55},{8,200... | collective-permute-start | bytes 1228808 | tf_op jit(solution)/shard_map/ppermute | solution.py:436
  67.1 9.3 %collective-permute-done.8.refs_2_ = bf16[160,1280]{1,0:T(8,128)(2,1)S(1)} collective-permute-done((bf16[160,1280]{1,0:T(8,128)(2,1)S(1)}, bf16[160,1280]{1,0:T(8,128)(2,1)S(1)}, u32[]{:S(2)}, u32[]{:S(2)}) %collective-permute-start.8) | collective-permute-done | bytes 409632 | tf_op jit(solution)/shard_map/ppermute | solution.py:436
  76.4 3.4 %collective-permute-done.7.refs_0_ = bf16[160,1280]{1,0:T(8,128)(2,1)S(1)} collective-permute-done((bf16[160,1280]{1,0:T(8,128)(2,1)S(1)}, bf16[160,1280]{1,0:T(8,128)(2,1)S(1)}, u32[]{:S(2)}, u32[]{:S(2)}) %collective-permute-start.7) | collective-permute-done | bytes 409632 | tf_op jit(solution)/shard_map/ppermute | solution.py:437
  79.8 0.1 slice.22
  79.9 4.5 %collective-permute-start.17 = (bf16[1,336,1280]{2,1,0:T(8,128)(2,1)S(1)}, bf16[1,336,1280]{2,1,0:T(8,128)(2,1)S(1)}, u32[]{:S(2)}, u32[]{:S(2)}) collective-permute-start(bf16[1,336,1280]{2,1,0:T(8,128)(2,1)S(1)} %slice.22), channel_id=1, source_target_pairs={{0,48},{1,193},{2,50},{3,195},{4,52},{5,197},{6,54},{7,199},{8,56}... | collective-permute-start | bytes 2580488 | tf_op jit(solution)/shard_map/ppermute | solution.py:454
  84.4 1.2 slice.23
  85.6 0.1 collective-permute-start.18
  85.7 0.1 collective-permute-start.14
  85.8 0.4 collective-permute-start.15
  86.2 0.0 collective-permute-done.9.refs_7_
  86.2 2.4 %collective-permute-start.16 = (bf16[160,1280]{1,0:T(8,128)(2,1)S(1)}, bf16[160,1280]{1,0:T(8,128)(2,1)S(1)}, u32[]{:S(2)}, u32[]{:S(2)}) collective-permute-start(bf16[160,1280]{1,0:T(8,128)(2,1)S(1)} %get-tuple-element.52.refs_3_), channel_id=1, source_target_pairs={{0,192},{1,49},{2,194},{3,51},{4,196},{5,53},{6,198},{7,55},{8,200... | collective-permute-start | bytes 1228808 | tf_op jit(solution)/shard_map/ppermute | solution.py:436
  88.5 8.5 %ffn.2 = (bf16[160,1280]{1,0:T(8,128)(2,1)S(1)}, bf16[160,1280]{1,0:T(8,128)(2,1)S(1)}, bf16[160,1280]{1,0:T(8,128)(2,1)S(1)}, bf16[160,1280]{1,0:T(8,128)(2,1)S(1)}) custom-call(bf16[160,1280]{1,0:T(8,128)(2,1)S(1)} %collective-permute-done.7.refs_0_, bf16[160,1280]{1,0:T(8,128)(2,1)S(1)} %collective-permute-done.6.refs_1_, ...), custom_call_target="tpu_custom_call" | custom-call | flops 8388608000 | bytes 9830400 | tf_op jit(solution)/shard_map/ffn/pallas_call | solution.py:283
  97.1 1.7 %collective-permute-done.14.refs_0_ = bf16[160,1280]{1,0:T(8,128)(2,1)S(1)} collective-permute-done((bf16[160,1280]{1,0:T(8,128)(2,1)S(1)}, bf16[160,1280]{1,0:T(8,128)(2,1)S(1)}, u32[]{:S(2)}, u32[]{:S(2)}) %collective-permute-start.14) | collective-permute-done | bytes 409632 | tf_op jit(solution)/shard_map/ppermute | solution.py:437
  98.8 0.0 collective-permute-start.11
  98.8 4.9 %collective-permute-done.15.refs_1_ = bf16[160,1280]{1,0:T(8,128)(2,1)S(1)} collective-permute-done((bf16[160,1280]{1,0:T(8,128)(2,1)S(1)}, bf16[160,1280]{1,0:T(8,128)(2,1)S(1)}, u32[]{:S(2)}, u32[]{:S(2)}) %collective-permute-start.15) | collective-permute-done | bytes 409632 | tf_op jit(solution)/shard_map/ppermute | solution.py:435
  103.7 1.9 %collective-permute-start.12 = (bf16[160,1280]{1,0:T(8,128)(2,1)S(1)}, bf16[160,1280]{1,0:T(8,128)(2,1)S(1)}, u32[]{:S(2)}, u32[]{:S(2)}) collective-permute-start(bf16[160,1280]{1,0:T(8,128)(2,1)S(1)} %get-tuple-element.46), channel_id=1, source_target_pairs={{0,192},{1,49},{2,194},{3,51},{4,196},{5,53},{6,198},{7,55},{8,200... | collective-permute-start | bytes 1228808 | tf_op jit(solution)/shard_map/ppermute | solution.py:445
  105.6 0.6 collective-permute-start.13
  106.2 5.3 %collective-permute-done.18.refs_11_ = bf16[1,320,1280]{2,1,0:T(8,128)(2,1)S(1)} collective-permute-done((bf16[1,320,1280]{2,1,0:T(8,128)(2,1)S(1)}, bf16[1,320,1280]{2,1,0:T(8,128)(2,1)S(1)}, u32[]{:S(2)}, u32[]{:S(2)}) %collective-permute-start.18) | collective-permute-done | bytes 819232 | tf_op jit(solution)/shard_map/ppermute | solution.py:453
  111.5 0.0 collective-permute-done.17.refs_7_
  111.5 8.5 %ffn.3 = (bf16[160,1280]{1,0:T(8,128)(2,1)S(1)}, bf16[160,1280]{1,0:T(8,128)(2,1)S(1)}, bf16[160,1280]{1,0:T(8,128)(2,1)S(1)}, bf16[160,1280]{1,0:T(8,128)(2,1)S(1)}) custom-call(bf16[160,1280]{1,0:T(8,128)(2,1)S(1)} %collective-permute-done.14.refs_0_, bf16[160,1280]{1,0:T(8,128)(2,1)S(1)} %collective-permute-done.15.refs_1_, ...), custom_call_target="tpu_custom_call" | custom-call | flops 8388608000 | bytes 9830400 | tf_op jit(solution)/shard_map/ffn/pallas_call | solution.py:283
  120.0 0.1 collective-permute-start.19
  120.1 0.9 collective-permute-start.20
  121.0 0.7 collective-permute-start.21
  121.7 0.0 copy-start.3
  121.7 0.3 add_parts.1.done_ref
  122.0 6.8 %collective-permute-done.19.refs_1_ = bf16[160,1280]{1,0:T(8,128)(2,1)S(1)} collective-permute-done((bf16[160,1280]{1,0:T(8,128)(2,1)S(1)}, bf16[160,1280]{1,0:T(8,128)(2,1)S(1)}, u32[]{:S(2)}, u32[]{:S(2)}) %collective-permute-start.19) | collective-permute-done | bytes 409632 | tf_op jit(solution)/shard_map/ppermute | solution.py:444
  128.8 1.5 collective-permute-done.20.refs_2_
  130.3 2.8 %collective-permute-done.21.refs_3_ = bf16[160,1280]{1,0:T(8,128)(2,1)S(1)} collective-permute-done((bf16[160,1280]{1,0:T(8,128)(2,1)S(1)}, bf16[160,1280]{1,0:T(8,128)(2,1)S(1)}, u32[]{:S(2)}, u32[]{:S(2)}) %collective-permute-start.21) | collective-permute-done | bytes 409632 | tf_op jit(solution)/shard_map/ppermute | solution.py:446
  133.1 2.2 %pack.1 = bf16[640,640]{1,0:T(8,128)(2,1)} custom-call(bf16[2,640,320]{2,1,0:T(8,128)(2,1)S(1)} %copy-done.3, f32[2,1280]{1,0:T(2,128)S(1)} %copy-done.6, bf16[160,1280]{1,0:T(8,128)(2,1)S(1)} %add_parts.1.done_ref, bf16[160,1280]{1,0:T(8,128)(2,1)S(1)} %get-tuple-element.55.refs_0_, bf16[160,1280]{1,0:T(8,128)(2,1)S(1)} %collective-permute-done.19.refs_1_, ...), custom_call_target="tpu_custom_call" | custom-call | tf_op jit(solution)/shard_map/pack/pallas_call | solution.py:342
  135.3 6.0 %all-to-all-start.1 = ((bf16[16,40,640]{2,1,0:T(8,128)(2,1)}), bf16[16,40,640]{2,1,0:T(8,128)(2,1)S(1)}, u32[]{:S(2)}, u32[]{:S(2)}) async-start(bf16[16,40,640]{2,1,0:T(8,128)(2,1)} %bitcast.7), calls=%async_computation.1 | async-start | bytes 1638400 | tf_op jit(solution)/shard_map/all_to_all | solution.py:432
  141.4 0.1 reshape.32.gate_ref
  141.5 0.1 copy.15.col_ref
  141.6 23.1 %all-to-all-done.1 = bf16[16,40,640]{2,1,0:T(8,128)(2,1)S(1)} async-done(((bf16[16,40,640]{2,1,0:T(8,128)(2,1)}), bf16[16,40,640]{2,1,0:T(8,128)(2,1)S(1)}, u32[]{:S(2)}, u32[]{:S(2)}) %all-to-all-start.1) | async-done | bytes 819232 | tf_op jit(solution)/shard_map/all_to_all | solution.py:432
  164.7 1.7 %combine.1 = bf16[256,1280]{1,0:T(8,128)(2,1)} custom-call(f32[256,1280]{1,0:T(8,128)S(1)} %copy-done.2, f32[256,1]{1,0:T(8,128)S(1)} %reshape.32.gate_ref, s32[256,1]{1,0:T(8,128)S(1)} %copy.15.col_ref, bf16[640,640]{1,0:T(8,128)(2,1)S(1)} %bitcast.13), custom_call_target="tpu_custom_call" | custom-call | tf_op jit(solution)/shard_map/combine/pallas_call | solution.py:371
  (31 shorter events, 0.1 us)
Async XLA Ops:
  1.7 16.3 %collective-permute-start = (bf16[1,64,1280]{2,1,0:T(8,128)(2,1)}, bf16[1,64,1280]{2,1,0:T(8,128)(2,1)}, u32[]{:S(2)}, u32[]{:S(2)}) collective-permute-start(bf16[1,64,1280]{2,1,0:T(8,128)(2,1)} %get-tuple-element.60), channel_id=1, source_target_pairs={{0,16},{16,32},{32,48},{48,64},{64,80},{80,96},{96,112},{112,128},... | collective-permute-start | bytes 491528 | tf_op jit(solution)/shard_map/ppermute | solution.py:407
  6.3 11.8 %collective-permute-start.1 = (bf16[1,64,1280]{2,1,0:T(8,128)(2,1)}, bf16[1,64,1280]{2,1,0:T(8,128)(2,1)}, u32[]{:S(2)}, u32[]{:S(2)}) collective-permute-start(bf16[1,64,1280]{2,1,0:T(8,128)(2,1)} %get-tuple-element.59), channel_id=1, source_target_pairs={{16,0},{32,16},{48,32},{64,48},{80,64},{96,80},{112,96},{128,112},... | collective-permute-start | bytes 491528 | tf_op jit(solution)/shard_map/ppermute | solution.py:408
  7.6 51.0 %collective-permute-start.2 = (bf16[2,320,1280]{2,1,0:T(8,128)(2,1)}, bf16[2,320,1280]{2,1,0:T(8,128)(2,1)}, u32[]{:S(2)}, u32[]{:S(2)}) collective-permute-start(bf16[2,320,1280]{2,1,0:T(8,128)(2,1)} %refs_8_.3), channel_id=1, source_target_pairs={{0,16},{1,65},{2,18},{3,67},{4,20},{5,69},{6,22},{7,71},{8,24},{9,... | collective-permute-start | bytes 4915208 | tf_op jit(solution)/shard_map/ppermute | solution.py:409
  11.3 47.3 %collective-permute-start.4 = (bf16[2,320,1280]{2,1,0:T(8,128)(2,1)}, bf16[2,320,1280]{2,1,0:T(8,128)(2,1)}, u32[]{:S(2)}, u32[]{:S(2)}) collective-permute-start(bf16[2,320,1280]{2,1,0:T(8,128)(2,1)} %refs_8_.3), channel_id=1, source_target_pairs={{0,48},{1,193},{2,50},{3,195},{4,52},{5,197},{6,54},{7,199},{8,56}... | collective-permute-start | bytes 4915208 | tf_op jit(solution)/shard_map/ppermute | solution.py:410
  12.9 1.4 copy-start
  14.3 0.7 copy-start.7
  15.0 2.4 %copy-start.14 = (s32[1,4,64,1]{2,3,1,0:T(1,128)S(1)}, s32[1,4,64,1]{2,3,1,0:T(1,128)}, u32[]{:S(2)}) copy-start(s32[1,4,64,1]{2,3,1,0:T(1,128)} %param.14) | copy-start | bytes 3076
  15.0 3.2 %copy-start.9 = (f32[3,3,1280]{2,1,0:T(4,128)S(1)}, f32[3,3,1280]{2,1,0:T(4,128)}, u32[]{:S(2)}) copy-start(f32[3,3,1280]{2,1,0:T(4,128)} %conv_weight.1) | copy-start | bytes 138244
  15.0 3.2 %copy-start.10 = (f32[1280]{0:T(1024)S(1)}, f32[1280]{0:T(1024)}, u32[]{:S(2)}) copy-start(f32[1280]{0:T(1024)} %mixer_gain.1) | copy-start | bytes 15364
  15.0 3.2 %copy-start.11 = (f32[1280]{0:T(1024)S(1)}, f32[1280]{0:T(1024)}, u32[]{:S(2)}) copy-start(f32[1280]{0:T(1024)} %expert_gain.1) | copy-start | bytes 15364
  15.0 3.2 %copy-start.12 = (f32[1280]{0:T(1024)S(1)}, f32[1280]{0:T(1024)}, u32[]{:S(2)}) copy-start(f32[1280]{0:T(1024)} %conv_bias.1) | copy-start | bytes 15364
  15.4 43.3 %collective-permute-start.3 = (bf16[2,336,1280]{2,1,0:T(8,128)(2,1)S(1)}, bf16[2,336,1280]{2,1,0:T(8,128)(2,1)S(1)}, u32[]{:S(2)}, u32[]{:S(2)}) collective-permute-start(bf16[2,336,1280]{2,1,0:T(8,128)(2,1)S(1)} %append_rows.1.refs_4_), channel_id=1, source_target_pairs={{0,48},{1,193},{2,50},{3,195},{4,52},{5,197},{6,54},{7,199},{8,56}... | collective-permute-start | bytes 5160968 | tf_op jit(solution)/shard_map/ppermute | solution.py:412
  18.0 40.6 %collective-permute-start.5 = (bf16[2,336,1280]{2,1,0:T(8,128)(2,1)S(1)}, bf16[2,336,1280]{2,1,0:T(8,128)(2,1)S(1)}, u32[]{:S(2)}, u32[]{:S(2)}) collective-permute-start(bf16[2,336,1280]{2,1,0:T(8,128)(2,1)S(1)} %append_rows.1.refs_4_), channel_id=1, source_target_pairs={{0,16},{1,65},{2,18},{3,67},{4,20},{5,69},{6,22},{7,71},{8,24},{9,... | collective-permute-start | bytes 5160968 | tf_op jit(solution)/shard_map/ppermute | solution.py:411
  18.2 1.1 copy-start.5
  23.8 1.1 copy-start.1
  24.9 32.2 %copy-start.4 = (bf16[2,320,640]{2,1,0:T(8,128)(2,1)S(1)}, bf16[2,320,640]{2,1,0:T(8,128)(2,1)}, u32[]{:S(2)}) copy-start(bf16[2,320,640]{2,1,0:T(8,128)(2,1)} %constant.4.clone.pick) | copy-start | bytes 2457604
  58.0 9.1 %collective-permute-start.6 = (bf16[160,1280]{1,0:T(8,128)(2,1)S(1)}, bf16[160,1280]{1,0:T(8,128)(2,1)S(1)}, u32[]{:S(2)}, u32[]{:S(2)}) collective-permute-start(bf16[160,1280]{1,0:T(8,128)(2,1)S(1)} %get-tuple-element.43.refs_3_), channel_id=1, source_target_pairs={{0,64},{1,17},{2,66},{3,19},{4,68},{5,21},{6,70},{7,23},{8,72},{9,... | collective-permute-start | bytes 1228808 | tf_op jit(solution)/shard_map/ppermute | solution.py:435
  58.7 27.4 %collective-permute-start.9 = (bf16[1,336,1280]{2,1,0:T(8,128)(2,1)S(1)}, bf16[1,336,1280]{2,1,0:T(8,128)(2,1)S(1)}, u32[]{:S(2)}, u32[]{:S(2)}) collective-permute-start(bf16[1,336,1280]{2,1,0:T(8,128)(2,1)S(1)} %slice.20), channel_id=1, source_target_pairs={{0,48},{1,193},{2,50},{3,195},{4,52},{5,197},{6,54},{7,199},{8,56}... | collective-permute-start | bytes 2580488 | tf_op jit(solution)/shard_map/ppermute | solution.py:427
  64.3 21.5 %collective-permute-start.10 = (bf16[1,320,1280]{2,1,0:T(8,128)(2,1)S(1)}, bf16[1,320,1280]{2,1,0:T(8,128)(2,1)S(1)}, u32[]{:S(2)}, u32[]{:S(2)}) collective-permute-start(bf16[1,320,1280]{2,1,0:T(8,128)(2,1)S(1)} %slice.21), channel_id=1, source_target_pairs={{0,16},{1,65},{2,18},{3,67},{4,20},{5,69},{6,22},{7,71},{8,24},{9,... | collective-permute-start | bytes 2457608 | tf_op jit(solution)/shard_map/ppermute | solution.py:426
  64.4 12.1 %collective-permute-start.8 = (bf16[160,1280]{1,0:T(8,128)(2,1)S(1)}, bf16[160,1280]{1,0:T(8,128)(2,1)S(1)}, u32[]{:S(2)}, u32[]{:S(2)}) collective-permute-start(bf16[160,1280]{1,0:T(8,128)(2,1)S(1)} %get-tuple-element.43.refs_3_), channel_id=1, source_target_pairs={{0,192},{1,49},{2,194},{3,51},{4,196},{5,53},{6,198},{7,55},{8,200... | collective-permute-start | bytes 1228808 | tf_op jit(solution)/shard_map/ppermute | solution.py:436
  67.1 12.8 %collective-permute-start.7 = (bf16[160,1280]{1,0:T(8,128)(2,1)S(1)}, bf16[160,1280]{1,0:T(8,128)(2,1)S(1)}, u32[]{:S(2)}, u32[]{:S(2)}) collective-permute-start(bf16[160,1280]{1,0:T(8,128)(2,1)S(1)} %collective-permute-done.6.refs_1_), channel_id=1, source_target_pairs={{0,64},{1,17},{2,66},{3,19},{4,68},{5,21},{6,70},{7,23},{8,72},{9,... | collective-permute-start | bytes 1228808 | tf_op jit(solution)/shard_map/ppermute | solution.py:437
  79.8 8.7 %copy-start.8 = (bf16[2,320,1280]{2,1,0:T(8,128)(2,1)S(1)}, bf16[2,320,1280]{2,1,0:T(8,128)(2,1)}, u32[]{:S(2)}) copy-start(bf16[2,320,1280]{2,1,0:T(8,128)(2,1)} %refs_8_.3) | copy-start | bytes 4915204
  79.9 31.6 %collective-permute-start.17 = (bf16[1,336,1280]{2,1,0:T(8,128)(2,1)S(1)}, bf16[1,336,1280]{2,1,0:T(8,128)(2,1)S(1)}, u32[]{:S(2)}, u32[]{:S(2)}) collective-permute-start(bf16[1,336,1280]{2,1,0:T(8,128)(2,1)S(1)} %slice.22), channel_id=1, source_target_pairs={{0,48},{1,193},{2,50},{3,195},{4,52},{5,197},{6,54},{7,199},{8,56}... | collective-permute-start | bytes 2580488 | tf_op jit(solution)/shard_map/ppermute | solution.py:454
  85.6 25.9 %collective-permute-start.18 = (bf16[1,320,1280]{2,1,0:T(8,128)(2,1)S(1)}, bf16[1,320,1280]{2,1,0:T(8,128)(2,1)S(1)}, u32[]{:S(2)}, u32[]{:S(2)}) collective-permute-start(bf16[1,320,1280]{2,1,0:T(8,128)(2,1)S(1)} %slice.23), channel_id=1, source_target_pairs={{0,16},{1,65},{2,18},{3,67},{4,20},{5,69},{6,22},{7,71},{8,24},{9,... | collective-permute-start | bytes 2457608 | tf_op jit(solution)/shard_map/ppermute | solution.py:453
  85.7 13.1 %collective-permute-start.14 = (bf16[160,1280]{1,0:T(8,128)(2,1)S(1)}, bf16[160,1280]{1,0:T(8,128)(2,1)S(1)}, u32[]{:S(2)}, u32[]{:S(2)}) collective-permute-start(bf16[160,1280]{1,0:T(8,128)(2,1)S(1)} %get-tuple-element.52.refs_3_), channel_id=1, source_target_pairs={{0,128},{1,33},{2,130},{3,35},{4,132},{5,37},{6,134},{7,39},{8,136... | collective-permute-start | bytes 1228808 | tf_op jit(solution)/shard_map/ppermute | solution.py:437
  85.8 18.0 %collective-permute-start.15 = (bf16[160,1280]{1,0:T(8,128)(2,1)S(1)}, bf16[160,1280]{1,0:T(8,128)(2,1)S(1)}, u32[]{:S(2)}, u32[]{:S(2)}) collective-permute-start(bf16[160,1280]{1,0:T(8,128)(2,1)S(1)} %get-tuple-element.52.refs_3_), channel_id=1, source_target_pairs={{0,64},{1,17},{2,66},{3,19},{4,68},{5,21},{6,70},{7,23},{8,72},{9,... | collective-permute-start | bytes 1228808 | tf_op jit(solution)/shard_map/ppermute | solution.py:435
  86.2 19.5 %collective-permute-start.16 = (bf16[160,1280]{1,0:T(8,128)(2,1)S(1)}, bf16[160,1280]{1,0:T(8,128)(2,1)S(1)}, u32[]{:S(2)}, u32[]{:S(2)}) collective-permute-start(bf16[160,1280]{1,0:T(8,128)(2,1)S(1)} %get-tuple-element.52.refs_3_), channel_id=1, source_target_pairs={{0,192},{1,49},{2,194},{3,51},{4,196},{5,53},{6,198},{7,55},{8,200... | collective-permute-start | bytes 1228808 | tf_op jit(solution)/shard_map/ppermute | solution.py:436
  98.8 22.2 %collective-permute-start.11 = (bf16[160,1280]{1,0:T(8,128)(2,1)S(1)}, bf16[160,1280]{1,0:T(8,128)(2,1)S(1)}, u32[]{:S(2)}, u32[]{:S(2)}) collective-permute-start(bf16[160,1280]{1,0:T(8,128)(2,1)S(1)} %get-tuple-element.45), channel_id=1, source_target_pairs={{0,128},{1,33},{2,130},{3,35},{4,132},{5,37},{6,134},{7,39},{8,136... | collective-permute-start | bytes 1228808 | tf_op jit(solution)/shard_map/ppermute | solution.py:444
  103.7 18.0 %collective-permute-start.12 = (bf16[160,1280]{1,0:T(8,128)(2,1)S(1)}, bf16[160,1280]{1,0:T(8,128)(2,1)S(1)}, u32[]{:S(2)}, u32[]{:S(2)}) collective-permute-start(bf16[160,1280]{1,0:T(8,128)(2,1)S(1)} %get-tuple-element.46), channel_id=1, source_target_pairs={{0,192},{1,49},{2,194},{3,51},{4,196},{5,53},{6,198},{7,55},{8,200... | collective-permute-start | bytes 1228808 | tf_op jit(solution)/shard_map/ppermute | solution.py:445
  105.6 16.1 %copy-start.6 = (f32[2,1280]{1,0:T(2,128)S(1)}, f32[2,1280]{1,0:T(2,128)}, u32[]{:S(2)}) copy-start(f32[2,1280]{1,0:T(2,128)} %bias.3) | copy-start | bytes 30724
  105.6 16.1 %collective-permute-start.13 = (bf16[160,1280]{1,0:T(8,128)(2,1)S(1)}, bf16[160,1280]{1,0:T(8,128)(2,1)S(1)}, u32[]{:S(2)}, u32[]{:S(2)}) collective-permute-start(bf16[160,1280]{1,0:T(8,128)(2,1)S(1)} %get-tuple-element.47), channel_id=1, source_target_pairs={{0,64},{1,17},{2,66},{3,19},{4,68},{5,21},{6,70},{7,23},{8,72},{9,... | collective-permute-start | bytes 1228808 | tf_op jit(solution)/shard_map/ppermute | solution.py:446
  120.0 8.7 %collective-permute-start.19 = (bf16[160,1280]{1,0:T(8,128)(2,1)S(1)}, bf16[160,1280]{1,0:T(8,128)(2,1)S(1)}, u32[]{:S(2)}, u32[]{:S(2)}) collective-permute-start(bf16[160,1280]{1,0:T(8,128)(2,1)S(1)} %get-tuple-element.56), channel_id=1, source_target_pairs={{0,128},{1,33},{2,130},{3,35},{4,132},{5,37},{6,134},{7,39},{8,136... | collective-permute-start | bytes 1228808 | tf_op jit(solution)/shard_map/ppermute | solution.py:444
  120.1 10.2 %collective-permute-start.20 = (bf16[160,1280]{1,0:T(8,128)(2,1)S(1)}, bf16[160,1280]{1,0:T(8,128)(2,1)S(1)}, u32[]{:S(2)}, u32[]{:S(2)}) collective-permute-start(bf16[160,1280]{1,0:T(8,128)(2,1)S(1)} %get-tuple-element.57), channel_id=1, source_target_pairs={{0,192},{1,49},{2,194},{3,51},{4,196},{5,53},{6,198},{7,55},{8,200... | collective-permute-start | bytes 1228808 | tf_op jit(solution)/shard_map/ppermute | solution.py:445
  121.0 12.1 %collective-permute-start.21 = (bf16[160,1280]{1,0:T(8,128)(2,1)S(1)}, bf16[160,1280]{1,0:T(8,128)(2,1)S(1)}, u32[]{:S(2)}, u32[]{:S(2)}) collective-permute-start(bf16[160,1280]{1,0:T(8,128)(2,1)S(1)} %get-tuple-element.58), channel_id=1, source_target_pairs={{0,64},{1,17},{2,66},{3,19},{4,68},{5,21},{6,70},{7,23},{8,72},{9,... | collective-permute-start | bytes 1228808 | tf_op jit(solution)/shard_map/ppermute | solution.py:446
  121.7 11.4 %copy-start.3 = (bf16[2,640,320]{2,1,0:T(8,128)(2,1)S(1)}, bf16[2,640,320]{2,1,0:T(8,128)(2,1)}, u32[]{:S(2)}) copy-start(bf16[2,640,320]{2,1,0:T(8,128)(2,1)} %constant.5.clone.place) | copy-start | bytes 2457604
  135.3 6.0 %copy-start.13 = (f32[1,4,64]{2,1,0:T(4,128)S(1)}, f32[1,4,64]{2,1,0:T(4,128)}, u32[]{:S(2)}) copy-start(f32[1,4,64]{2,1,0:T(4,128)} %param.15) | copy-start | bytes 3076
  135.3 29.4 %copy-start.2 = (f32[256,1280]{1,0:T(8,128)S(1)}, f32[256,1280]{1,0:T(8,128)}, u32[]{:S(2)}) copy-start(f32[256,1280]{1,0:T(8,128)} %copy-done.1) | copy-start | bytes 3932164
  135.3 29.4 %all-to-all-start.1 = ((bf16[16,40,640]{2,1,0:T(8,128)(2,1)}), bf16[16,40,640]{2,1,0:T(8,128)(2,1)S(1)}, u32[]{:S(2)}, u32[]{:S(2)}) async-start(bf16[16,40,640]{2,1,0:T(8,128)(2,1)} %bitcast.7), calls=%async_computation.1 | async-start | bytes 1638400 | tf_op jit(solution)/shard_map/all_to_all | solution.py:432

commit v5 on v4

--- a/solution.py
+++ b/solution.py
@@ -225,23 +225,22 @@
     units = wos[0].shape[1]
     first, second = [], []
     for k in range(SIDE):
-        at = expert if k < SIDE - 1 else 0
         first.append(
             pltpu.make_async_copy(xs[k], x_v.at[pl.ds(k * rows, rows)], x_sem.at[k])
         )
         first.append(
             pltpu.make_async_copy(
-                wis[k].at[at, pl.ds(0, units)], wi_v.at[pl.ds(k * units, units)], w_sem.at[0, k]
+                wis[k].at[expert, pl.ds(0, units)], wi_v.at[pl.ds(k * units, units)], w_sem.at[0, k]
             )
         )
         first.append(
             pltpu.make_async_copy(
-                wis[k].at[at, pl.ds(units, EXTRA)], b_v.at[k], w_sem.at[2, k]
+                wis[k].at[expert, pl.ds(units, EXTRA)], b_v.at[k], w_sem.at[2, k]
             )
         )
         second.append(
             pltpu.make_async_copy(
-                wos[k].at[at], wo_v.at[pl.ds(k * units, units)], w_sem.at[1, k]
+                wos[k].at[expert], wo_v.at[pl.ds(k * units, units)], w_sem.at[1, k]
             )
         )
     for copy in first + second:
@@ -423,8 +422,8 @@
         conv_bias,
     )
     columns, wo_on, wi_on, *_ = together((columns, wo_prev, wi_next, wo_next, wi_prev))
-    wo_far_0 = lax.ppermute(wo_on[0:1], AXES, send_w(1))
-    wi_far_0 = lax.ppermute(wi_on[0:1], AXES, send_w(-1))
+    wo_far = lax.ppermute(wo_on, AXES, send_w(1))
+    wi_far = lax.ppermute(wi_on, AXES, send_w(-1))
 
     def exchange(msg):
         shape = msg.shape
@@ -448,16 +447,14 @@
 
     pick, place = tables(exp_size, slots)
     rows_0, rows_1 = unpack(exchange(msg), pick)
+    weights = ((wi, wi_prev, wi_next, wi_far), (wo, wo_prev, wo_next, wo_far))
     rows_0 = spread(rows_0, True)
-    rows_1, rows_0, wo_on, wi_on = together((rows_1, rows_0, wo_on, wi_on))
-    wo_far_1 = lax.ppermute(wo_on[1:2], AXES, send_w(1))
-    wi_far_1 = lax.ppermute(wi_on[1:2], AXES, send_w(-1))
-    weights_0 = ((wi, wi_prev, wi_next, wi_far_0), (wo, wo_prev, wo_next, wo_far_0))
-    weights_1 = ((wi, wi_prev, wi_next, wi_far_1), (wo, wo_prev, wo_next, wo_far_1))
+    rows_1, rows_0, wi_far, wo_far = together((rows_1, rows_0, wi_far, wo_far))
+    weights = ((wi, wi_prev, wi_next, wi_far), (wo, wo_prev, wo_next, wo_far))
     rows_1 = spread(rows_1, False)
-    parts_0 = ffn(0, rows_0, *weights_0)
+    parts_0 = ffn(0, rows_0, *weights)
     rows_1, _ = together((rows_1, parts_0[0]))
-    parts_1 = ffn(1, rows_1, *weights_1)
+    parts_1 = ffn(1, rows_1, *weights)
     early = add_parts(b_out, returned(parts_0))
     back = pack(place, b_out, early, returned(parts_1))
     back = exchange(back)

time: 167 us -> 162 us (0.970)
  blocking collectives: 32.2 us -> 0 us
  waiting for transfers between devices: 59 us -> 76.2 us
  starting transfers between devices: 38 us -> 51.9 us
  local copies, waits for them, and re-layouts: 9.43 us -> 6.01 us
    all_to_all x1 -> x0, blocking collectives: 32.2 us -> none  [exchange(): lax.all_to_all(msg, 'exp', split_axis=0, concat_axis=0, tiled=True)]
    all_to_all x1 -> x2, starting transfers between devices: 6.03 us -> 24.2 us  [exchange(): lax.all_to_all(msg, 'exp', split_axis=0, concat_axis=0, tiled=True)]
    ppermute x1, waiting for transfers between devices: 0.01 us -> 16.8 us  [body(): wi_prev = lax.ppermute(wi, AXES, send_w(1))]
    ppermute x2, waiting for transfers between devices: 9.35 us -> 0.01 us  [spread(): nxt = lax.ppermute(rows, AXES, send_t(-1))]
    ppermute x2, waiting for transfers between devices: 5.15 us -> 12.9 us  [spread(): lax.ppermute(prev if forward else rows, AXES, send_t(1 if forward else 2))]
    ppermute x4 -> x2, starting transfers between devices: 8.94 us -> 2.34 us  [the longest x1 2.34 us: body(): wi_far = lax.ppermute(wi_on, AXES, send_w(-1))]
    ppermute x4 -> x2, waiting for transfers between devices: 5.31 us -> 0.01 us  [the longest x1 0.01 us: body(): wo_far = lax.ppermute(wo_on, AXES, send_w(1))]
    ppermute x2, waiting for transfers between devices: 4.92 us -> 10.2 us  [spread(): prev = lax.ppermute(rows, AXES, send_t(1))]
  transfers between devices with their start and end apart: 23 -> 22, of which waited for: 9 -> 8; matrix products, arithmetic and copies ran while one was open for 2% -> 1% of each run, Pallas kernels for 14% -> 14%
where the time goes in v5:
time: 162 us; the launch traced here: 161 us
  waiting for transfers between devices  76.2 us (47%)
  starting transfers between devices  51.9 us (32%)
  Pallas kernels  26.3 us (16%)
  local copies, waits for them, and re-layouts  6.01 us (4%)
    all_to_all x2, waiting for transfers between devices, exchange(): lax.all_to_all(msg, 'exp', split_axis=0, concat_axis=0, tiled=True)  27.2 us
    all_to_all x2, starting transfers between devices, exchange(): lax.all_to_all(msg, 'exp', split_axis=0, concat_axis=0, tiled=True)  24.2 us
    pallas_call x2, Pallas kernels, ffn(): pl.pallas_call(functools.partial(ffn_kernel, expert), out_shape=[jax.Shap...  17.4 us
    ppermute x1, waiting for transfers between devices, body(): wi_prev = lax.ppermute(wi, AXES, send_w(1))  16.8 us
    ppermute x2, waiting for transfers between devices, spread(): lax.ppermute(prev if forward else rows, AXES, send_t(1 if forward else 2))  12.9 us
    ppermute x2, waiting for transfers between devices, spread(): prev = lax.ppermute(rows, AXES, send_t(1))  10.2 us
    ppermute x2, starting transfers between devices, returned(): lax.ppermute(prev, AXES, send_t(-1))  4.83 us
    ppermute x2, waiting for transfers between devices, returned(): lax.ppermute(far, AXES, send_t(2))  4.71 us
  transfers between devices with their start and end apart: 22, of which 8 were waited for; matrix products, arithmetic and copies ran while one was open for 1% of the time, Pallas kernels for 14%

profile of v5, /device:TPU:1, one launch (start us, length us, event | category | flops | bytes accessed | tf_op | source)
XLA Modules:
  0.0 161.3 jit_solution(14823146994754678258)
XLA Ops:
  0.0 1.0 slice_bitcast_fusion
  1.0 1.3 collective-permute-start.1
  2.3 4.6 %collective-permute-start = (bf16[1,64,1280]{2,1,0:T(8,128)(2,1)S(1)}, bf16[1,64,1280]{2,1,0:T(8,128)(2,1)S(1)}, u32[]{:S(2)}, u32[]{:S(2)}) collective-permute-start(bf16[1,64,1280]{2,1,0:T(8,128)(2,1)S(1)} %get-tuple-element.60), channel_id=1, source_target_pairs={{0,16},{16,32},{32,48},{48,64},{64,80},{80,96},{96,112},{112,128},... | collective-permute-start | bytes 491528 | tf_op jit(solution)/shard_map/ppermute | solution.py:406
  6.9 4.3 %collective-permute-start.4 = (bf16[2,320,1280]{2,1,0:T(8,128)(2,1)}, bf16[2,320,1280]{2,1,0:T(8,128)(2,1)}, u32[]{:S(2)}, u32[]{:S(2)}) collective-permute-start(bf16[2,320,1280]{2,1,0:T(8,128)(2,1)} %refs_8_.3), channel_id=1, source_target_pairs={{0,48},{1,193},{2,50},{3,195},{4,52},{5,197},{6,54},{7,199},{8,56}... | collective-permute-start | bytes 4915208 | tf_op jit(solution)/shard_map/ppermute | solution.py:409
  11.2 0.0 collective-permute-start.2
  11.2 1.4 copy-done
  12.6 0.7 copy-done.8
  13.3 0.0 copy-start.12
  13.3 0.0 copy-start.13
  13.3 0.4 append_rows.1.refs_4_
  13.7 0.1 collective-permute-start.5
  13.8 0.5 broadcast.3
  14.3 0.7 reduce.3
  15.0 0.1 reshape.24.ids_ref
  15.1 0.0 collective-permute-done.1.down_ref
  15.1 2.7 %collective-permute-start.3 = (bf16[2,336,1280]{2,1,0:T(8,128)(2,1)S(1)}, bf16[2,336,1280]{2,1,0:T(8,128)(2,1)}, u32[]{:S(2)}, u32[]{:S(2)}) collective-permute-start(bf16[2,336,1280]{2,1,0:T(8,128)(2,1)S(1)} %append_rows.1.refs_4_), channel_id=1, source_target_pairs={{0,48},{1,193},{2,50},{3,195},{4,52},{5,197},{6,54},{7,199},{8,56}... | collective-permute-start | bytes 5160968 | tf_op jit(solution)/shard_map/ppermute | solution.py:411
  17.7 0.0 collective-permute-done.up_ref
  17.8 3.5 %mix.1 = (f32[256,1280]{1,0:T(8,128)S(1)}, bf16[640,640]{1,0:T(8,128)(2,1)S(1)}, s32[1,256]{1,0:T(1,128)S(1)}) custom-call(bf16[4,64,1280]{2,1,0:T(8,128)(2,1)S(1)} %bitcast.17, bf16[1,64,1280]{2,1,0:T(8,128)(2,1)S(1)} %collective-permute-done.up_ref, bf16[1,64,1280]{2,1,0:T(8,128)(2,1)S(1)} %collective-permute-done.1.down_ref, ...), custom_call_target="tpu_custom_call" | custom-call | flops 19660800000 | bytes 1966080 | tf_op jit(solution)/shard_map/mix/pallas_call | solution.py:176
  21.3 1.1 copy-done.1
  22.4 0.9 copy-done.5
  23.3 11.3 %all-to-all-start = ((bf16[16,40,640]{2,1,0:T(8,128)(2,1)}), bf16[16,40,640]{2,1,0:T(8,128)(2,1)S(1)}, u32[]{:S(2)}, u32[]{:S(2)}) async-start(bf16[16,40,640]{2,1,0:T(8,128)(2,1)} %bitcast.16), calls=%async_computation | async-start | bytes 1638400 | tf_op jit(solution)/shard_map/all_to_all | solution.py:431
  34.6 0.0 collective-permute-done.4.refs_10_
  34.6 0.0 collective-permute-done.2.refs_9_
  34.7 16.8 %collective-permute-done.5.refs_5_ = bf16[2,336,1280]{2,1,0:T(8,128)(2,1)} collective-permute-done((bf16[2,336,1280]{2,1,0:T(8,128)(2,1)S(1)}, bf16[2,336,1280]{2,1,0:T(8,128)(2,1)}, u32[]{:S(2)}, u32[]{:S(2)}) %collective-permute-start.5) | collective-permute-done | bytes 1720352 | tf_op jit(solution)/shard_map/ppermute | solution.py:410
  51.4 0.0 collective-permute-done.3.refs_6_
  51.4 2.3 %collective-permute-start.9 = (bf16[2,336,1280]{2,1,0:T(8,128)(2,1)}, bf16[2,336,1280]{2,1,0:T(8,128)(2,1)}, u32[]{:S(2)}, u32[]{:S(2)}) collective-permute-start(bf16[2,336,1280]{2,1,0:T(8,128)(2,1)} %collective-permute-done.3.refs_6_), channel_id=1, source_target_pairs={{0,48},{1,193},{2,50},{3,195},{4,52},{5,197},{6,54},{7,199},{8,56}... | collective-permute-start | bytes 5160968 | tf_op jit(solution)/shard_map/ppermute | solution.py:426
  53.8 0.0 collective-permute-start.10
  53.8 4.2 %all-to-all-done = bf16[16,40,640]{2,1,0:T(8,128)(2,1)S(1)} async-done(((bf16[16,40,640]{2,1,0:T(8,128)(2,1)}), bf16[16,40,640]{2,1,0:T(8,128)(2,1)S(1)}, u32[]{:S(2)}, u32[]{:S(2)}) %all-to-all-start) | async-done | bytes 819232 | tf_op jit(solution)/shard_map/all_to_all | solution.py:431
  58.0 0.9 unpack.1
  58.9 0.1 collective-permute-start.6
  59.0 2.7 %collective-permute-start.8 = (bf16[160,1280]{1,0:T(8,128)(2,1)S(1)}, bf16[160,1280]{1,0:T(8,128)(2,1)S(1)}, u32[]{:S(2)}, u32[]{:S(2)}) collective-permute-start(bf16[160,1280]{1,0:T(8,128)(2,1)S(1)} %get-tuple-element.43.refs_3_), channel_id=1, source_target_pairs={{0,192},{1,49},{2,194},{3,51},{4,196},{5,53},{6,198},{7,55},{8,200... | collective-permute-start | bytes 1228808 | tf_op jit(solution)/shard_map/ppermute | solution.py:435
  61.6 10.2 %collective-permute-done.6.refs_1_ = bf16[160,1280]{1,0:T(8,128)(2,1)S(1)} collective-permute-done((bf16[160,1280]{1,0:T(8,128)(2,1)S(1)}, bf16[160,1280]{1,0:T(8,128)(2,1)S(1)}, u32[]{:S(2)}, u32[]{:S(2)}) %collective-permute-start.6) | collective-permute-done | bytes 409632 | tf_op jit(solution)/shard_map/ppermute | solution.py:434
  71.8 0.0 collective-permute-start.7
  71.8 0.0 collective-permute-done.8.refs_2_
  71.8 12.9 %collective-permute-done.7.refs_0_ = bf16[160,1280]{1,0:T(8,128)(2,1)S(1)} collective-permute-done((bf16[160,1280]{1,0:T(8,128)(2,1)S(1)}, bf16[160,1280]{1,0:T(8,128)(2,1)S(1)}, u32[]{:S(2)}, u32[]{:S(2)}) %collective-permute-start.7) | collective-permute-done | bytes 409632 | tf_op jit(solution)/shard_map/ppermute | solution.py:436
  84.7 0.0 collective-permute-done.10.refs_11_
  84.7 0.0 collective-permute-done.9.refs_7_
  84.7 0.0 collective-permute-start.16
  84.7 1.5 collective-permute-start.15
  86.2 0.0 collective-permute-start.14
  86.2 8.7 %ffn.2 = (bf16[160,1280]{1,0:T(8,128)(2,1)S(1)}, bf16[160,1280]{1,0:T(8,128)(2,1)S(1)}, bf16[160,1280]{1,0:T(8,128)(2,1)S(1)}, bf16[160,1280]{1,0:T(8,128)(2,1)S(1)}) custom-call(bf16[160,1280]{1,0:T(8,128)(2,1)S(1)} %collective-permute-done.7.refs_0_, bf16[160,1280]{1,0:T(8,128)(2,1)S(1)} %collective-permute-done.6.refs_1_, ...), custom_call_target="tpu_custom_call" | custom-call | flops 8388608000 | bytes 9830400 | tf_op jit(solution)/shard_map/ffn/pallas_call | solution.py:282
  94.9 2.5 %collective-permute-start.12 = (bf16[160,1280]{1,0:T(8,128)(2,1)S(1)}, bf16[160,1280]{1,0:T(8,128)(2,1)S(1)}, u32[]{:S(2)}, u32[]{:S(2)}) collective-permute-start(bf16[160,1280]{1,0:T(8,128)(2,1)S(1)} %get-tuple-element.48), channel_id=1, source_target_pairs={{0,192},{1,49},{2,194},{3,51},{4,196},{5,53},{6,198},{7,55},{8,200... | collective-permute-start | bytes 1228808 | tf_op jit(solution)/shard_map/ppermute | solution.py:444
  97.4 0.0 collective-permute-start.13
  97.4 0.0 collective-permute-done.16.refs_2_
  97.4 2.0 %collective-permute-start.11 = (bf16[160,1280]{1,0:T(8,128)(2,1)S(1)}, bf16[160,1280]{1,0:T(8,128)(2,1)S(1)}, u32[]{:S(2)}, u32[]{:S(2)}) collective-permute-start(bf16[160,1280]{1,0:T(8,128)(2,1)S(1)} %get-tuple-element.47), channel_id=1, source_target_pairs={{0,128},{1,33},{2,130},{3,35},{4,132},{5,37},{6,134},{7,39},{8,136... | collective-permute-start | bytes 1228808 | tf_op jit(solution)/shard_map/ppermute | solution.py:443
  99.4 0.0 collective-permute-done.15.refs_1_
  99.4 0.0 collective-permute-done.14.refs_0_
  99.4 8.7 %ffn.3 = (bf16[160,1280]{1,0:T(8,128)(2,1)S(1)}, bf16[160,1280]{1,0:T(8,128)(2,1)S(1)}, bf16[160,1280]{1,0:T(8,128)(2,1)S(1)}, bf16[160,1280]{1,0:T(8,128)(2,1)S(1)}) custom-call(bf16[160,1280]{1,0:T(8,128)(2,1)S(1)} %collective-permute-done.14.refs_0_, bf16[160,1280]{1,0:T(8,128)(2,1)S(1)} %collective-permute-done.15.refs_1_, ...), custom_call_target="tpu_custom_call" | custom-call | flops 8388608000 | bytes 9830400 | tf_op jit(solution)/shard_map/ffn/pallas_call | solution.py:282
  108.1 1.3 collective-permute-start.17
  109.5 2.4 %collective-permute-start.18 = (bf16[160,1280]{1,0:T(8,128)(2,1)S(1)}, bf16[160,1280]{1,0:T(8,128)(2,1)S(1)}, u32[]{:S(2)}, u32[]{:S(2)}) collective-permute-start(bf16[160,1280]{1,0:T(8,128)(2,1)S(1)} %get-tuple-element.57), channel_id=1, source_target_pairs={{0,192},{1,49},{2,194},{3,51},{4,196},{5,53},{6,198},{7,55},{8,200... | collective-permute-start | bytes 1228808 | tf_op jit(solution)/shard_map/ppermute | solution.py:444
  111.8 0.0 collective-permute-done.12.refs_2_
  111.8 0.0 collective-permute-start.19
  111.9 0.0 collective-permute-done.11.refs_1_
  111.9 0.0 copy-start.3
  111.9 0.2 add_parts.1.done_ref
  112.1 4.7 %collective-permute-done.17.refs_1_ = bf16[160,1280]{1,0:T(8,128)(2,1)S(1)} collective-permute-done((bf16[160,1280]{1,0:T(8,128)(2,1)S(1)}, bf16[160,1280]{1,0:T(8,128)(2,1)S(1)}, u32[]{:S(2)}, u32[]{:S(2)}) %collective-permute-start.17) | collective-permute-done | bytes 409632 | tf_op jit(solution)/shard_map/ppermute | solution.py:443
  116.8 3.3 %collective-permute-done.18.refs_2_ = bf16[160,1280]{1,0:T(8,128)(2,1)S(1)} collective-permute-done((bf16[160,1280]{1,0:T(8,128)(2,1)S(1)}, bf16[160,1280]{1,0:T(8,128)(2,1)S(1)}, u32[]{:S(2)}, u32[]{:S(2)}) %collective-permute-start.18) | collective-permute-done | bytes 409632 | tf_op jit(solution)/shard_map/ppermute | solution.py:444
  120.2 1.1 collective-permute-done.19.refs_3_
  121.2 2.2 %pack.1 = bf16[640,640]{1,0:T(8,128)(2,1)} custom-call(bf16[2,640,320]{2,1,0:T(8,128)(2,1)S(1)} %copy-done.3, f32[2,1280]{1,0:T(2,128)S(1)} %copy-done.7, bf16[160,1280]{1,0:T(8,128)(2,1)S(1)} %add_parts.1.done_ref, bf16[160,1280]{1,0:T(8,128)(2,1)S(1)} %get-tuple-element.55.refs_0_, bf16[160,1280]{1,0:T(8,128)(2,1)S(1)} %collective-permute-done.17.refs_1_, ...), custom_call_target="tpu_custom_call" | custom-call | tf_op jit(solution)/shard_map/pack/pallas_call | solution.py:341
  123.4 12.9 %all-to-all-start.1 = ((bf16[16,40,640]{2,1,0:T(8,128)(2,1)}), bf16[16,40,640]{2,1,0:T(8,128)(2,1)S(1)}, u32[]{:S(2)}, u32[]{:S(2)}) async-start(bf16[16,40,640]{2,1,0:T(8,128)(2,1)} %bitcast.7), calls=%async_computation.1 | async-start | bytes 1638400 | tf_op jit(solution)/shard_map/all_to_all | solution.py:431
  136.3 0.1 reshape.32.gate_ref
  136.4 0.1 copy.15.col_ref
  136.6 23.0 %all-to-all-done.1 = bf16[16,40,640]{2,1,0:T(8,128)(2,1)S(1)} async-done(((bf16[16,40,640]{2,1,0:T(8,128)(2,1)}), bf16[16,40,640]{2,1,0:T(8,128)(2,1)S(1)}, u32[]{:S(2)}, u32[]{:S(2)}) %all-to-all-start.1) | async-done | bytes 819232 | tf_op jit(solution)/shard_map/all_to_all | solution.py:431
  159.6 1.7 %combine.1 = bf16[256,1280]{1,0:T(8,128)(2,1)} custom-call(f32[256,1280]{1,0:T(8,128)S(1)} %copy-done.2, f32[256,1]{1,0:T(8,128)S(1)} %reshape.32.gate_ref, s32[256,1]{1,0:T(8,128)S(1)} %copy.15.col_ref, bf16[640,640]{1,0:T(8,128)(2,1)S(1)} %bitcast.14), custom_call_target="tpu_custom_call" | custom-call | tf_op jit(solution)/shard_map/combine/pallas_call | solution.py:370
  (26 shorter events, 0.0 us)
Async XLA Ops:
  1.0 14.0 %collective-permute-start.1 = (bf16[1,64,1280]{2,1,0:T(8,128)(2,1)S(1)}, bf16[1,64,1280]{2,1,0:T(8,128)(2,1)S(1)}, u32[]{:S(2)}, u32[]{:S(2)}) collective-permute-start(bf16[1,64,1280]{2,1,0:T(8,128)(2,1)S(1)} %get-tuple-element.59), channel_id=1, source_target_pairs={{16,0},{32,16},{48,32},{64,48},{80,64},{96,80},{112,96},{128,112},... | collective-permute-start | bytes 491528 | tf_op jit(solution)/shard_map/ppermute | solution.py:407
  2.3 15.4 %collective-permute-start = (bf16[1,64,1280]{2,1,0:T(8,128)(2,1)S(1)}, bf16[1,64,1280]{2,1,0:T(8,128)(2,1)S(1)}, u32[]{:S(2)}, u32[]{:S(2)}) collective-permute-start(bf16[1,64,1280]{2,1,0:T(8,128)(2,1)S(1)} %get-tuple-element.60), channel_id=1, source_target_pairs={{0,16},{16,32},{32,48},{48,64},{64,80},{80,96},{96,112},{112,128},... | collective-permute-start | bytes 491528 | tf_op jit(solution)/shard_map/ppermute | solution.py:406
  6.9 27.7 %collective-permute-start.4 = (bf16[2,320,1280]{2,1,0:T(8,128)(2,1)}, bf16[2,320,1280]{2,1,0:T(8,128)(2,1)}, u32[]{:S(2)}, u32[]{:S(2)}) collective-permute-start(bf16[2,320,1280]{2,1,0:T(8,128)(2,1)} %refs_8_.3), channel_id=1, source_target_pairs={{0,48},{1,193},{2,50},{3,195},{4,52},{5,197},{6,54},{7,199},{8,56}... | collective-permute-start | bytes 4915208 | tf_op jit(solution)/shard_map/ppermute | solution.py:409
  11.2 23.5 %collective-permute-start.2 = (bf16[2,320,1280]{2,1,0:T(8,128)(2,1)}, bf16[2,320,1280]{2,1,0:T(8,128)(2,1)}, u32[]{:S(2)}, u32[]{:S(2)}) collective-permute-start(bf16[2,320,1280]{2,1,0:T(8,128)(2,1)} %refs_8_.3), channel_id=1, source_target_pairs={{0,16},{1,65},{2,18},{3,67},{4,20},{5,69},{6,22},{7,71},{8,24},{9,... | collective-permute-start | bytes 4915208 | tf_op jit(solution)/shard_map/ppermute | solution.py:408
  11.2 1.4 copy-start
  12.6 0.7 copy-start.8
  13.3 1.0 copy-start.15
  13.3 4.5 %copy-start.6 = (bf16[1,4,64,1280]{3,2,1,0:T(8,128)(2,1)S(1)}, bf16[1,4,64,1280]{3,2,1,0:T(8,128)(2,1)}, u32[]{:S(2)}) copy-start(bf16[1,4,64,1280]{3,2,1,0:T(8,128)(2,1)} %param.13) | copy-start | bytes 1966084
  13.3 4.5 %copy-start.10 = (f32[3,3,1280]{2,1,0:T(4,128)S(1)}, f32[3,3,1280]{2,1,0:T(4,128)}, u32[]{:S(2)}) copy-start(f32[3,3,1280]{2,1,0:T(4,128)} %conv_weight.1) | copy-start | bytes 138244
  13.3 4.5 %copy-start.11 = (f32[1280]{0:T(1024)S(1)}, f32[1280]{0:T(1024)}, u32[]{:S(2)}) copy-start(f32[1280]{0:T(1024)} %mixer_gain.1) | copy-start | bytes 15364
  13.3 4.5 %copy-start.12 = (f32[1280]{0:T(1024)S(1)}, f32[1280]{0:T(1024)}, u32[]{:S(2)}) copy-start(f32[1280]{0:T(1024)} %expert_gain.1) | copy-start | bytes 15364
  13.3 4.5 %copy-start.13 = (f32[1280]{0:T(1024)S(1)}, f32[1280]{0:T(1024)}, u32[]{:S(2)}) copy-start(f32[1280]{0:T(1024)} %conv_bias.1) | copy-start | bytes 15364
  13.7 37.7 %collective-permute-start.5 = (bf16[2,336,1280]{2,1,0:T(8,128)(2,1)S(1)}, bf16[2,336,1280]{2,1,0:T(8,128)(2,1)}, u32[]{:S(2)}, u32[]{:S(2)}) collective-permute-start(bf16[2,336,1280]{2,1,0:T(8,128)(2,1)S(1)} %append_rows.1.refs_4_), channel_id=1, source_target_pairs={{0,16},{1,65},{2,18},{3,67},{4,20},{5,69},{6,22},{7,71},{8,24},{9,... | collective-permute-start | bytes 5160968 | tf_op jit(solution)/shard_map/ppermute | solution.py:410
  15.1 36.4 %collective-permute-start.3 = (bf16[2,336,1280]{2,1,0:T(8,128)(2,1)S(1)}, bf16[2,336,1280]{2,1,0:T(8,128)(2,1)}, u32[]{:S(2)}, u32[]{:S(2)}) collective-permute-start(bf16[2,336,1280]{2,1,0:T(8,128)(2,1)S(1)} %append_rows.1.refs_4_), channel_id=1, source_target_pairs={{0,48},{1,193},{2,50},{3,195},{4,52},{5,197},{6,54},{7,199},{8,56}... | collective-permute-start | bytes 5160968 | tf_op jit(solution)/shard_map/ppermute | solution.py:411
  21.3 1.1 copy-start.1
  22.4 0.9 copy-start.5
  23.3 34.7 %copy-start.4 = (bf16[2,320,640]{2,1,0:T(8,128)(2,1)S(1)}, bf16[2,320,640]{2,1,0:T(8,128)(2,1)}, u32[]{:S(2)}) copy-start(bf16[2,320,640]{2,1,0:T(8,128)(2,1)} %constant.4.clone.pick) | copy-start | bytes 2457604
  23.3 34.7 %all-to-all-start = ((bf16[16,40,640]{2,1,0:T(8,128)(2,1)}), bf16[16,40,640]{2,1,0:T(8,128)(2,1)S(1)}, u32[]{:S(2)}, u32[]{:S(2)}) async-start(bf16[16,40,640]{2,1,0:T(8,128)(2,1)} %bitcast.16), calls=%async_computation | async-start | bytes 1638400 | tf_op jit(solution)/shard_map/all_to_all | solution.py:431
  51.4 33.3 %collective-permute-start.9 = (bf16[2,336,1280]{2,1,0:T(8,128)(2,1)}, bf16[2,336,1280]{2,1,0:T(8,128)(2,1)}, u32[]{:S(2)}, u32[]{:S(2)}) collective-permute-start(bf16[2,336,1280]{2,1,0:T(8,128)(2,1)} %collective-permute-done.3.refs_6_), channel_id=1, source_target_pairs={{0,48},{1,193},{2,50},{3,195},{4,52},{5,197},{6,54},{7,199},{8,56}... | collective-permute-start | bytes 5160968 | tf_op jit(solution)/shard_map/ppermute | solution.py:426
  53.8 30.9 %collective-permute-start.10 = (bf16[2,320,1280]{2,1,0:T(8,128)(2,1)}, bf16[2,320,1280]{2,1,0:T(8,128)(2,1)}, u32[]{:S(2)}, u32[]{:S(2)}) collective-permute-start(bf16[2,320,1280]{2,1,0:T(8,128)(2,1)} %collective-permute-done.2.refs_9_), channel_id=1, source_target_pairs={{0,16},{1,65},{2,18},{3,67},{4,20},{5,69},{6,22},{7,71},{8,24},{9,... | collective-permute-start | bytes 4915208 | tf_op jit(solution)/shard_map/ppermute | solution.py:425
  58.0 28.2 %copy-start.9 = (bf16[2,320,1280]{2,1,0:T(8,128)(2,1)S(1)}, bf16[2,320,1280]{2,1,0:T(8,128)(2,1)}, u32[]{:S(2)}) copy-start(bf16[2,320,1280]{2,1,0:T(8,128)(2,1)} %refs_8_.3) | copy-start | bytes 4915204
  58.9 12.9 %collective-permute-start.6 = (bf16[160,1280]{1,0:T(8,128)(2,1)S(1)}, bf16[160,1280]{1,0:T(8,128)(2,1)S(1)}, u32[]{:S(2)}, u32[]{:S(2)}) collective-permute-start(bf16[160,1280]{1,0:T(8,128)(2,1)S(1)} %get-tuple-element.43.refs_3_), channel_id=1, source_target_pairs={{0,64},{1,17},{2,66},{3,19},{4,68},{5,21},{6,70},{7,23},{8,72},{9,... | collective-permute-start | bytes 1228808 | tf_op jit(solution)/shard_map/ppermute | solution.py:434
  59.0 12.9 %collective-permute-start.8 = (bf16[160,1280]{1,0:T(8,128)(2,1)S(1)}, bf16[160,1280]{1,0:T(8,128)(2,1)S(1)}, u32[]{:S(2)}, u32[]{:S(2)}) collective-permute-start(bf16[160,1280]{1,0:T(8,128)(2,1)S(1)} %get-tuple-element.43.refs_3_), channel_id=1, source_target_pairs={{0,192},{1,49},{2,194},{3,51},{4,196},{5,53},{6,198},{7,55},{8,200... | collective-permute-start | bytes 1228808 | tf_op jit(solution)/shard_map/ppermute | solution.py:435
  71.8 12.9 %collective-permute-start.7 = (bf16[160,1280]{1,0:T(8,128)(2,1)S(1)}, bf16[160,1280]{1,0:T(8,128)(2,1)S(1)}, u32[]{:S(2)}, u32[]{:S(2)}) collective-permute-start(bf16[160,1280]{1,0:T(8,128)(2,1)S(1)} %collective-permute-done.6.refs_1_), channel_id=1, source_target_pairs={{0,64},{1,17},{2,66},{3,19},{4,68},{5,21},{6,70},{7,23},{8,72},{9,... | collective-permute-start | bytes 1228808 | tf_op jit(solution)/shard_map/ppermute | solution.py:436
  84.7 12.7 %collective-permute-start.16 = (bf16[160,1280]{1,0:T(8,128)(2,1)S(1)}, bf16[160,1280]{1,0:T(8,128)(2,1)S(1)}, u32[]{:S(2)}, u32[]{:S(2)}) collective-permute-start(bf16[160,1280]{1,0:T(8,128)(2,1)S(1)} %get-tuple-element.54.refs_3_), channel_id=1, source_target_pairs={{0,192},{1,49},{2,194},{3,51},{4,196},{5,53},{6,198},{7,55},{8,200... | collective-permute-start | bytes 1228808 | tf_op jit(solution)/shard_map/ppermute | solution.py:435
  84.7 14.7 %collective-permute-start.15 = (bf16[160,1280]{1,0:T(8,128)(2,1)S(1)}, bf16[160,1280]{1,0:T(8,128)(2,1)S(1)}, u32[]{:S(2)}, u32[]{:S(2)}) collective-permute-start(bf16[160,1280]{1,0:T(8,128)(2,1)S(1)} %get-tuple-element.54.refs_3_), channel_id=1, source_target_pairs={{0,64},{1,17},{2,66},{3,19},{4,68},{5,21},{6,70},{7,23},{8,72},{9,... | collective-permute-start | bytes 1228808 | tf_op jit(solution)/shard_map/ppermute | solution.py:434
  86.2 13.3 %collective-permute-start.14 = (bf16[160,1280]{1,0:T(8,128)(2,1)S(1)}, bf16[160,1280]{1,0:T(8,128)(2,1)S(1)}, u32[]{:S(2)}, u32[]{:S(2)}) collective-permute-start(bf16[160,1280]{1,0:T(8,128)(2,1)S(1)} %get-tuple-element.54.refs_3_), channel_id=1, source_target_pairs={{0,128},{1,33},{2,130},{3,35},{4,132},{5,37},{6,134},{7,39},{8,136... | collective-permute-start | bytes 1228808 | tf_op jit(solution)/shard_map/ppermute | solution.py:436
  94.9 17.0 %collective-permute-start.12 = (bf16[160,1280]{1,0:T(8,128)(2,1)S(1)}, bf16[160,1280]{1,0:T(8,128)(2,1)S(1)}, u32[]{:S(2)}, u32[]{:S(2)}) collective-permute-start(bf16[160,1280]{1,0:T(8,128)(2,1)S(1)} %get-tuple-element.48), channel_id=1, source_target_pairs={{0,192},{1,49},{2,194},{3,51},{4,196},{5,53},{6,198},{7,55},{8,200... | collective-permute-start | bytes 1228808 | tf_op jit(solution)/shard_map/ppermute | solution.py:444
  97.4 14.5 %collective-permute-start.13 = (bf16[160,1280]{1,0:T(8,128)(2,1)S(1)}, bf16[160,1280]{1,0:T(8,128)(2,1)S(1)}, u32[]{:S(2)}, u32[]{:S(2)}) collective-permute-start(bf16[160,1280]{1,0:T(8,128)(2,1)S(1)} %get-tuple-element.49), channel_id=1, source_target_pairs={{0,64},{1,17},{2,66},{3,19},{4,68},{5,21},{6,70},{7,23},{8,72},{9,... | collective-permute-start | bytes 1228808 | tf_op jit(solution)/shard_map/ppermute | solution.py:445
  97.4 14.5 %copy-start.7 = (f32[2,1280]{1,0:T(2,128)S(1)}, f32[2,1280]{1,0:T(2,128)}, u32[]{:S(2)}) copy-start(f32[2,1280]{1,0:T(2,128)} %bias.3) | copy-start | bytes 30724
  97.4 14.5 %collective-permute-start.11 = (bf16[160,1280]{1,0:T(8,128)(2,1)S(1)}, bf16[160,1280]{1,0:T(8,128)(2,1)S(1)}, u32[]{:S(2)}, u32[]{:S(2)}) collective-permute-start(bf16[160,1280]{1,0:T(8,128)(2,1)S(1)} %get-tuple-element.47), channel_id=1, source_target_pairs={{0,128},{1,33},{2,130},{3,35},{4,132},{5,37},{6,134},{7,39},{8,136... | collective-permute-start | bytes 1228808 | tf_op jit(solution)/shard_map/ppermute | solution.py:443
  108.1 8.7 %collective-permute-start.17 = (bf16[160,1280]{1,0:T(8,128)(2,1)S(1)}, bf16[160,1280]{1,0:T(8,128)(2,1)S(1)}, u32[]{:S(2)}, u32[]{:S(2)}) collective-permute-start(bf16[160,1280]{1,0:T(8,128)(2,1)S(1)} %get-tuple-element.56), channel_id=1, source_target_pairs={{0,128},{1,33},{2,130},{3,35},{4,132},{5,37},{6,134},{7,39},{8,136... | collective-permute-start | bytes 1228808 | tf_op jit(solution)/shard_map/ppermute | solution.py:443
  109.5 10.7 %collective-permute-start.18 = (bf16[160,1280]{1,0:T(8,128)(2,1)S(1)}, bf16[160,1280]{1,0:T(8,128)(2,1)S(1)}, u32[]{:S(2)}, u32[]{:S(2)}) collective-permute-start(bf16[160,1280]{1,0:T(8,128)(2,1)S(1)} %get-tuple-element.57), channel_id=1, source_target_pairs={{0,192},{1,49},{2,194},{3,51},{4,196},{5,53},{6,198},{7,55},{8,200... | collective-permute-start | bytes 1228808 | tf_op jit(solution)/shard_map/ppermute | solution.py:444
  111.8 9.4 %collective-permute-start.19 = (bf16[160,1280]{1,0:T(8,128)(2,1)S(1)}, bf16[160,1280]{1,0:T(8,128)(2,1)S(1)}, u32[]{:S(2)}, u32[]{:S(2)}) collective-permute-start(bf16[160,1280]{1,0:T(8,128)(2,1)S(1)} %get-tuple-element.58), channel_id=1, source_target_pairs={{0,64},{1,17},{2,66},{3,19},{4,68},{5,21},{6,70},{7,23},{8,72},{9,... | collective-permute-start | bytes 1228808 | tf_op jit(solution)/shard_map/ppermute | solution.py:445
  111.9 9.4 %copy-start.3 = (bf16[2,640,320]{2,1,0:T(8,128)(2,1)S(1)}, bf16[2,640,320]{2,1,0:T(8,128)(2,1)}, u32[]{:S(2)}) copy-start(bf16[2,640,320]{2,1,0:T(8,128)(2,1)} %constant.5.clone.place) | copy-start | bytes 2457604
  123.4 12.9 %copy-start.14 = (f32[1,4,64]{2,1,0:T(4,128)S(1)}, f32[1,4,64]{2,1,0:T(4,128)}, u32[]{:S(2)}) copy-start(f32[1,4,64]{2,1,0:T(4,128)} %param.15) | copy-start | bytes 3076
  123.4 36.2 %copy-start.2 = (f32[256,1280]{1,0:T(8,128)S(1)}, f32[256,1280]{1,0:T(8,128)}, u32[]{:S(2)}) copy-start(f32[256,1280]{1,0:T(8,128)} %copy-done.1) | copy-start | bytes 3932164
  123.4 36.2 %all-to-all-start.1 = ((bf16[16,40,640]{2,1,0:T(8,128)(2,1)}), bf16[16,40,640]{2,1,0:T(8,128)(2,1)S(1)}, u32[]{:S(2)}, u32[]{:S(2)}) async-start(bf16[16,40,640]{2,1,0:T(8,128)(2,1)} %bitcast.7), calls=%async_computation.1 | async-start | bytes 1638400 | tf_op jit(solution)/shard_map/all_to_all | solution.py:431
